TPU v7x, 512 devices: a whole 4x4x16 slice. The times are simulated.
512 devices in a mesh: img: 16 (over y, z_hi, core), ref: 32 (over z_lo, x).
Axes of the slice: x: 4, y: 4, z: 16 (z_hi: 2, z_lo: 8; z = z_hi * 8 + z_lo), core: 2. Of those that a mesh axis runs over, the one named last changes fastest.
Arguments:
- images: float32 [2, 256, 32768], P(None, 'img', 'ref'), may hold values from -6 to 6
- references: float32 [2, 256, 32768], P(None, 'ref', 'img'), may hold values from -2 to 2
- precision: float32 [256], P('img'), may hold values from 0.00390625 to 0.0390625
- shifts: int32 [12, 2], replicated, may hold values from -6 to 6, as said below
- labels: int32 [256], P('ref'), may hold values from 0 to 3
- log_prior: float32 [4], replicated, may hold values from -4 to 4
Outputs:
- new_refs: float32 [2, 256, 32768], P(None, 'ref', 'img')
- class_post: float32 [256, 4], P('img')
Inputs may be any that keep to these rules, and one draw needn't show every extreme that they name: `shifts`: both ends of the range occur in every draw.
All inputs are finite; a program needn't handle non-finite values.
Results may differ from a plain program's by a relative error of at most 0.0056.
Values may be sent and summed in bfloat16 or wider, within the bound.
No kernel may reach another device: no remote copies, remote signals or barrier semaphores. Data moves between devices by JAX's collectives and lax.ppermute only.
A program may use at most 64 MiB of HBM per device.

v0:
```python
import math

import jax
import jax.numpy as jnp
from jax import lax
from jax.sharding import PartitionSpec as P

ROWS = 256
COLS = 128
SHIFTS = 12
CLASSES = 4


def phases(shifts):
    index = jnp.arange(ROWS * COLS, dtype=jnp.int32)
    freq_y = (index // COLS - ROWS // 2).astype(jnp.float32)
    freq_x = (index % COLS).astype(jnp.float32)
    shift_x = shifts[:, 0].astype(jnp.float32)[:, None]
    shift_y = shifts[:, 1].astype(jnp.float32)[:, None]
    angles = 2.0 * math.pi / ROWS * (freq_x[None, :] * shift_x + freq_y[None, :] * shift_y)
    return (jnp.cos(angles), jnp.sin(angles))


def inner_rows(left, right):
    return lax.dot_general(
        left, right, (((1,), (1,)), ((), ())), preferred_element_type=jnp.float32
    )


def inner_cols(left, right):
    return lax.dot_general(
        left, right, (((0,), (0,)), ((), ())), preferred_element_type=jnp.float32
    )


def local(images, references, precision, shifts, labels, log_prior):
    img_low = lax.all_gather(images.astype(jnp.bfloat16), "ref", axis=2, tiled=True)
    ref_low = lax.all_gather(references.astype(jnp.bfloat16), "img", axis=2, tiled=True)
    pixels = img_low.shape[2]
    img_dev = img_low.shape[1]
    ref_dev = ref_low.shape[1]
    blocks = SHIFTS // 4
    cosine, sine_part = phases(shifts)
    cos_blocks = cosine.reshape(blocks, 4, pixels)
    sin_blocks = sine_part.reshape(blocks, 4, pixels)
    ref_wide = ref_low.astype(jnp.float32)
    energy = jnp.sum(ref_wide * ref_wide, axis=(0, 2))
    onehot = (labels[:, None] == jnp.arange(CLASSES, dtype=jnp.int32)[None, :]).astype(jnp.float32)
    prior_term = jnp.sum(onehot * log_prior[None, :], axis=1)

    def cross_block(operands):
        cos_rows, sin_rows = operands
        shifted_re = (
            ref_wide[0][None] * cos_rows[:, None, :] + ref_wide[1][None] * sin_rows[:, None, :]
        ).astype(jnp.bfloat16)
        shifted_im = (
            ref_wide[1][None] * cos_rows[:, None, :] - ref_wide[0][None] * sin_rows[:, None, :]
        ).astype(jnp.bfloat16)
        return inner_rows(img_low[0], shifted_re.reshape(4 * ref_dev, pixels)) + inner_rows(
            img_low[1], shifted_im.reshape(4 * ref_dev, pixels)
        )

    cross_terms = lax.map(cross_block, (cos_blocks, sin_blocks))
    cross_terms = jnp.transpose(cross_terms, (1, 0, 2)).reshape(img_dev, SHIFTS, ref_dev)
    scores = (
        precision[:, None, None] * (cross_terms - 0.5 * energy[None, None, :])
        + prior_term[None, None, :]
    )
    local_top = jnp.max(scores, axis=(1, 2))
    top_score = lax.pmax(local_top, "ref")
    exponent = jnp.exp(scores - top_score[:, None, None])
    local_class = jnp.einsum(
        "ik,kc->ic", jnp.sum(exponent, axis=1), onehot, precision=lax.Precision.HIGHEST
    )
    row_total, class_sum = lax.psum((jnp.sum(exponent, axis=(1, 2)), local_class), "ref")
    posterior = exponent / row_total[:, None, None]
    class_post = class_sum / row_total[:, None]
    local_mass = jnp.sum(posterior, axis=(0, 1))
    post_low = posterior.astype(jnp.bfloat16).reshape(img_dev, blocks, 4 * ref_dev)
    post_low = jnp.transpose(post_low, (1, 0, 2))

    def back_block(running, operands):
        weights_blk, cos_rows, sin_rows = operands
        back_re = inner_cols(weights_blk, img_low[0]).reshape(4, ref_dev, pixels)
        back_im = inner_cols(weights_blk, img_low[1]).reshape(4, ref_dev, pixels)
        part_re = jnp.sum(back_re * cos_rows[:, None, :] - back_im * sin_rows[:, None, :], axis=0)
        part_im = jnp.sum(back_im * cos_rows[:, None, :] + back_re * sin_rows[:, None, :], axis=0)
        return (running + jnp.stack([part_re, part_im]), None)

    start_sum = jnp.zeros((2, ref_dev, pixels), jnp.float32)
    summed, unused = lax.scan(back_block, start_sum, (post_low, cos_blocks, sin_blocks))
    summed_all, ref_mass = lax.psum((summed, local_mass), "img")
    pix_block = pixels // lax.axis_size("img")
    summed_part = lax.dynamic_slice_in_dim(
        summed_all, lax.axis_index("img") * pix_block, pix_block, 2
    )
    new_refs = summed_part / (ref_mass + 1.0)[None, :, None]
    return (new_refs, class_post)


def solution(mesh):
    return jax.shard_map(
        local,
        mesh=mesh,
        in_specs=(P(None, "img", "ref"), P(None, "ref", "img"), P("img"), P(), P("ref"), P()),
        out_specs=(P(None, "ref", "img"), P("img", None)),
        check_vma=False,
    )
```

profile of v0, /device:TPU:102, one launch (start us, length us, event | category | flops | bytes accessed | tf_op | source)
XLA Modules:
  0.0 916.9 jit_solution(10611607265250826830)
XLA Ops:
  7.2 1.5 convert_element_type.63
  8.8 1.5 convert_element_type.69
  10.5 0.8 convert_reduce_fusion.1
  11.4 0.8 select_reduce_fusion
  12.3 12.6 %fusion.39 = (f32[3,4,32768]{2,1,0:T(4,128)}, f32[3,4,32768]{2,1,0:T(4,128)}) fusion(f32[3,4]{1,0:T(4,128)S(1)} %mul.207, f32[32768]{0:T(1024)S(1)} %get-tuple-element.128, f32[3,4]{1,0:T(4,128)S(1)} %mul.203, f32[32768]{0:T(1024)S(1)} %get-tuple-element.127), kind=kLoop, calls=%fused_computation.44 | loop fusion | flops 1572864 | bytes 3407968 | tf_op jit(solution)/shard_map/sin | solution.py:21
  24.9 59.6 %all-gather.3.cloned.1.call-done = bf16[2,8,32768]{2,1,0:T(8,128)(2,1)} async-done(((bf16[2,8,2048]{2,1,0:T(8,128)(2,1)}), bf16[2,8,32768]{2,1,0:T(8,128)(2,1)}) %all-gather.3.cloned.1.call-update) | async-done | bytes 1048592 | tf_op jit(solution)/shard_map/all_gather | solution.py:38
  84.5 1.9 multiply_reduce_fusion
  86.5 2.7 convert_element_type.64
  89.2 173.8 %all-gather.5.cloned.1.call-done = bf16[2,16,32768]{2,1,0:T(8,128)(2,1)} async-done(((bf16[2,16,1024]{2,1,0:T(8,128)(2,1)}), bf16[2,16,32768]{2,1,0:T(8,128)(2,1)}) %all-gather.5.cloned.1.call-update) | async-done | bytes 2097168 | tf_op jit(solution)/shard_map/all_gather | solution.py:37
  263.0 14.6 %while.21 = (s32[]{:T(128)}, f32[3,16,32]{2,1,0:T(8,128)S(1)}, f32[2,8,32768]{2,1,0:T(8,128)}, f32[3,4,32768]{2,1,0:T(4,128)}, f32[3,4,32768]{2,1,0:T(4,128)}, /*index=5*/bf16[2,16,32768]{2,1,0:T(8,128)(2,1)}, s32[]{:T(128)}) while((s32[]{:T(128)}, f32[3,16,32]{2,1,0:T(8,128)S(1)}, f32[2,8,32768]{2,1,0:T(8,128)}, f32[3,4,32768]{2,1,0:T(4,128)}, ...), condition=%wide.region_1.2_spmd, body=%wide.region_0.1_spmd.sunk | while | flops 75497984 | bytes 31475852 | solution.py:63
  263.0 1.4 dynamic-slice_bitcast_fusion.6
  264.4 0.5 copy-done.1
  265.0 1.4 copy-done.2
  266.5 0.7 fusion.69
  267.1 0.7 fusion.70
  267.9 1.4 dynamic-slice_bitcast_fusion.6
  269.3 0.5 copy-done.1
  269.9 1.4 copy-done.2
  271.4 0.7 fusion.69
  272.0 0.7 fusion.70
  272.7 1.4 dynamic-slice_bitcast_fusion.6
  274.2 0.5 copy-done.1
  274.8 1.4 copy-done.2
  276.2 0.7 fusion.69
  276.9 0.7 fusion.70
  277.8 100.4 %pmax.7 = f32[16]{0:T(128)S(1)} all-reduce(f32[16]{0:T(128)S(1)} %fusion.52), channel_id=1, replica_groups=mesh['img'=16,'ref'=32] {'ref'}, use_global_device_ids=true, to_apply=%region_5.6 | all-reduce | flops 16 | bytes 128 | tf_op jit(solution)/shard_map/pmax | solution.py:70
  378.5 122.7 %all-reduce = (f32[16]{0:T(128)S(1)}, f32[16,4]{0,1:T(4,128)S(1)}) all-reduce(f32[16]{0:T(128)S(1)} %fusion.51, f32[16,4]{0,1:T(4,128)S(1)} %fusion.53), channel_id=1, replica_groups=mesh['img'=16,'ref'=32] {'ref'}, use_global_device_ids=true, to_apply=%region_7.8 | all-reduce | flops 80 | bytes 640 | tf_op jit(solution)/shard_map/psum | solution.py:75
  501.3 25.5 %while.22 = (s32[]{:T(128)}, f32[2,8,32768]{2,1,0:T(8,128)S(1)}, bf16[3,16,32]{1,2,0:T(8,128)(2,1)S(1)}, bf16[2,16,32768]{2,1,0:T(8,128)(2,1)}, f32[3,4,32768]{2...) while((s32[]{:T(128)}, f32[2,8,32768]{2,1,0:T(8,128)S(1)}, ...), condition=%wide.region_11.12_spmd.clone, body=%wide.region_8.11_spmd.clone.sunk | while | flops 76546048 | bytes 30425728 | solution.py:91
  501.3 1.9 fusion.73
  503.2 1.4 dynamic-slice_bitcast_fusion.7
  504.6 0.5 copy-done.3
  505.1 2.8 subtract_reduce_fusion.2
  507.9 1.8 maximum_add_fusion.2
  509.8 1.9 fusion.73
  511.7 1.4 dynamic-slice_bitcast_fusion.7
  513.1 0.5 copy-done.3
  513.6 2.8 subtract_reduce_fusion.2
  516.4 1.8 maximum_add_fusion.2
  518.2 1.9 fusion.73
  520.2 1.4 dynamic-slice_bitcast_fusion.7
  521.6 0.5 copy-done.3
  522.1 2.8 subtract_reduce_fusion.2
  524.9 1.8 maximum_add_fusion.2
  526.7 1.3 copy-done
  528.3 62.1 %psum.30 = f32[8]{0:T(128)S(1)} all-reduce(f32[8]{0:T(128)S(1)} %reduce_sum.75), channel_id=1, replica_groups=mesh['img'=16,'ref'=32] {'img'}, use_global_device_ids=true, to_apply=%region_15.16 | all-reduce | flops 8 | bytes 64 | tf_op jit(solution)/shard_map/psum | solution.py:92
  590.4 0.6 broadcast_divide_fusion
  591.0 317.7 %all-reduce.3.cloned.1.call-done = f32[2,8,32768]{2,1,0:T(8,128)} async-done(((f32[2,8,32768]{2,1,0:T(8,128)}), f32[2,8,32768]{2,1,0:T(8,128)}) %all-reduce.3.cloned.1.call-update) | async-done | bytes 2097168 | tf_op jit(solution)/shard_map/psum | solution.py:92
  908.7 1.6 dynamic-slice_divide_fusion
  (43 shorter events, 1.9 us)
Async XLA Ops:
  7.2 77.4 %all-gather.3.cloned.1.call-start = ((), (), s32[]{:S(2)}) async-start(), calls=%async_computation | async-start | bytes 1114112 | tf_op jit(solution)/shard_map/all_gather | solution.py:38
  8.8 254.2 %all-gather.5.cloned.1.call-start = ((), (), s32[]{:S(2)}) async-start(), calls=%async_computation.1 | async-start | bytes 2162688 | tf_op jit(solution)/shard_map/all_gather | solution.py:37
  10.4 898.3 %all-reduce.3.cloned.1.call-start = ((), (), s32[]{:S(2)}) async-start(), calls=%async_computation.2 | async-start | bytes 4194304 | tf_op jit(solution)/shard_map/psum | solution.py:92
  262.9 14.7 %copy-start.4 = (f32[16]{0:T(128)S(1)}, f32[16]{0:T(128)}, u32[]{:S(2)}) copy-start(f32[16]{0:T(128)} %param.12) | copy-start | bytes 196
  262.9 115.4 %copy-start.5 = (s32[8]{0:T(128)S(1)}, s32[8]{0:T(128)}, u32[]{:S(2)}) copy-start(s32[8]{0:T(128)} %param.14) | copy-start | bytes 100
  263.0 1.9 copy-start.1
  264.9 1.6 copy-start.2
  267.9 1.9 copy-start.1
  269.8 1.6 copy-start.2
  272.7 1.9 copy-start.1
  274.6 1.6 copy-start.2
  503.2 1.9 copy-start.3
  511.7 1.9 copy-start.3
  520.2 1.9 copy-start.3
  526.7 1.3 copy-start
Sparse Core Ops, SparseCore 0:
  11.9 72.5 all-gather.2
  86.6 176.2 all-gather.4
  528.2 380.4 all-reduce.2
where the time goes:
time: 918 us; the launch traced here: 917 us
  waiting for transfers between devices  551 us (60%)
  blocking collectives  285 us (31%)
  other arithmetic  30.1 us (3%)
  matrix products  18.4 us (2%)
  local copies, waits for them, and re-layouts  18 us (2%)
  between operations  13.8 us (2%)
    psum x1, waiting for transfers between devices, local(): summed_all, ref_mass = lax.psum((summed, local_mass), 'img')  318 us
    all_gather x1, waiting for transfers between devices, local(): lax.all_gather(images.astype(jnp.bfloat16), 'ref', axis=2, tiled=True)  174 us
    psum x1, blocking collectives, local(): lax.psum((jnp.sum(exponent, axis=(1, 2)), local_class), 'ref')  123 us
    pmax x1, blocking collectives, local(): top_score = lax.pmax(local_top, 'ref')  100 us
    psum x1, blocking collectives, local(): summed_all, ref_mass = lax.psum((summed, local_mass), 'img')  62.1 us
    all_gather x1, waiting for transfers between devices, local(): lax.all_gather(references.astype(jnp.bfloat16), 'img', axis=2, tiled=True)  59.6 us
  transfers between devices with their start and end apart: 3, of which 3 were waited for; matrix products, arithmetic and copies ran while one was open for 2% of the time, Pallas kernels for 0%

commit v1 on v0

v1 whole, which is shorter than its diff:
```python
import math

import jax
import jax.numpy as jnp
from jax import lax
from jax.experimental import pallas as pl
from jax.experimental.pallas import tpu as pltpu
from jax.sharding import Mesh
from jax.sharding import PartitionSpec as P

ROWS = 256
COLS = 128
SHIFTS = 12
CLASSES = 4
LANES = 128
USED = SHIFTS * 8
SIZES = {"y": 4, "zh": 2, "c": 2, "zl": 8, "x": 4}
ALL = ("y", "zh", "c", "zl", "x")
SPACE = ("y", "c", "x")
IMG = ("y", "zh", "c")
REF = ("zl", "x")


def place(y, zh, c, zl, x):
    return (((y * 2 + zh) * 2 + c) * 8 + zl) * 4 + x


def every():
    return [
        (y, zh, c, zl, x)
        for y in range(4)
        for zh in range(2)
        for c in range(2)
        for zl in range(8)
        for x in range(4)
    ]


REF_ROUTE = [
    (place(y, zh, c, zl, x), place(zl // 2, zh, zl % 2, y * 2 + c, x)) for y, zh, c, zl, x in every()
]
IMG_ROUTE = [
    (place(y, zh, c, zl, x), place(y, zl & 1, c, (zl >> 1) * 2 + (x >> 1), zh * 2 + (x & 1)))
    for y, zh, c, zl, x in every()
]


def phases(shifts, block):
    index = block * 2048 + jnp.arange(2048, dtype=jnp.int32)
    freq_y = (index // COLS - ROWS // 2).astype(jnp.float32)
    freq_x = (index % COLS).astype(jnp.float32)
    shift_x = shifts[:, 0].astype(jnp.float32)[:, None]
    shift_y = shifts[:, 1].astype(jnp.float32)[:, None]
    angles = 2.0 * math.pi / ROWS * (freq_x[None, :] * shift_x + freq_y[None, :] * shift_y)
    return jnp.cos(angles), jnp.sin(angles)


def own_lanes():
    lane = lax.broadcasted_iota(jnp.int32, (8, LANES), 1)
    row = lax.broadcasted_iota(jnp.int32, (8, LANES), 0)
    return (lane % 8 == row) & (lane < USED)


def cross_kernel(img_ref, ref_ref, cos_ref, sin_ref, label_ref, out_ref, shifted):
    re = ref_ref[0].astype(jnp.float32)
    im = ref_ref[1].astype(jnp.float32)
    energy = jnp.sum(re * re + im * im, axis=1, keepdims=True)
    half = jnp.sum(jnp.where(own_lanes(), 0.5 * energy, 0.0), axis=0, keepdims=True)
    for pair in range(SHIFTS // 2):
        rot_re, rot_im = [], []
        for t in (2 * pair, 2 * pair + 1):
            cos, sin = cos_ref[t : t + 1, :], sin_ref[t : t + 1, :]
            rot_re.append(re * cos + im * sin)
            rot_im.append(im * cos - re * sin)
        rows = slice(16 * pair, 16 * pair + 16)
        shifted[0, rows, :] = jnp.concatenate(rot_re, axis=0).astype(jnp.bfloat16)
        shifted[1, rows, :] = jnp.concatenate(rot_im, axis=0).astype(jnp.bfloat16)
    shifted[:, USED:, :] = jnp.zeros((2, LANES - USED, 2048), jnp.bfloat16)
    total = jnp.zeros((256, LANES), jnp.float32)
    for h in range(2):
        for part in range(2):
            total += lax.dot_general(
                img_ref[:, :, :, h, part].reshape(256, 1024),
                shifted[part, :, h * 1024 : (h + 1) * 1024],
                (((1,), (1,)), ((), ())),
                preferred_element_type=jnp.float32,
            )
    total = (total - half + label_ref[...]).reshape(4, 2, 2, 16, LANES)
    for y in range(4):
        for c in range(2):
            for zh in range(2):
                for copy in range(2):
                    out_ref[(y * 2 + zh) * 2 + c, copy] = total[y, c, zh]


def softmax_kernel(got_ref, prior_ref, precision_ref, out_ref):
    both = got_ref[:, 0] + got_ref[:, 1]
    tile = both[:, :, 0:8] + both[:, :, 8:16] + both[:, :, 16:24] + both[:, :, 24:32]
    row = lax.broadcasted_iota(jnp.int32, (8, LANES), 0)
    lane = lax.broadcasted_iota(jnp.int32, (8, LANES), 1)
    low = row < 4
    scores, labels = [], []
    for y in range(4):
        label = jnp.where(lane < USED, 0.0, got_ref[0, 0, 0, 8 * y : 8 * y + 8, :])
        label = label + pltpu.roll(label, 32, 1)
        label = label + pltpu.roll(label, 64, 1)
        labels.append(label)
        prior = jnp.zeros((8, LANES), jnp.float32)
        for k in range(CLASSES):
            prior = jnp.where(label == k, prior_ref[k], prior)
        first = tile[y, 0] + pltpu.roll(tile[y, 0], 4, 0)
        second = tile[y, 1] + pltpu.roll(tile[y, 1], 4, 0)
        cross = jnp.where(low, first, second)
        score = precision_ref[0] * cross + prior
        scores.append(jnp.where(lane < USED, score, -jnp.inf))
    top = jnp.max(jnp.maximum(jnp.maximum(scores[0], scores[1]), jnp.maximum(scores[2], scores[3])))
    weights = [jnp.exp(score - top) for score in scores]
    total = jnp.sum(weights[0] + weights[1] + weights[2] + weights[3])
    posts = [weight / total for weight in weights]
    classes = jnp.zeros((8, LANES), jnp.float32)
    for k in range(CLASSES):
        mass = sum(jnp.where(labels[y] == k, posts[y], 0.0) for y in range(4))
        classes = jnp.where(lane == USED + k, jnp.sum(mass), classes)
    for y in range(4):
        post = jnp.where(lane < USED, posts[y], classes)
        turned = pltpu.roll(post, 4, 0)
        for c in range(2):
            message = jnp.where(low, post, turned) if c == 0 else jnp.where(low, turned, post)
            for zh in range(2):
                for pair in range(4):
                    out_ref[y, zh, c, 8 * pair : 8 * pair + 8, :] = message


def back_kernel(got_ref, img_ref, cos_ref, sin_ref, out_ref):
    lane = lax.broadcasted_iota(jnp.int32, (256, LANES), 1)
    post = jnp.concatenate(
        [got_ref[(y * 2 + zh) * 2 + c, 0] for y in range(4) for c in range(2) for zh in range(2)], axis=0
    )
    post = jnp.where(lane < USED, post, 0.0)
    mass_row = jnp.sum(post, axis=0, keepdims=True)
    mass = jnp.sum(jnp.where(own_lanes(), mass_row, 0.0), axis=1, keepdims=True)
    weights = jnp.transpose(post).astype(jnp.bfloat16)
    for h in range(2):
        cols = slice(h * 1024, (h + 1) * 1024)
        back = [
            jnp.dot(
                weights,
                img_ref[:, :, :, h, part].reshape(256, 1024),
                preferred_element_type=jnp.float32,
            )
            for part in range(2)
        ]
        sum_re = jnp.zeros((8, 1024), jnp.float32)
        sum_im = jnp.zeros((8, 1024), jnp.float32)
        for t in range(SHIFTS):
            cos, sin = cos_ref[t : t + 1, cols], sin_ref[t : t + 1, cols]
            back_re, back_im = back[0][8 * t : 8 * t + 8], back[1][8 * t : 8 * t + 8]
            sum_re += back_re * cos - back_im * sin
            sum_im += back_im * cos + back_re * sin
        out_ref[0, :, cols] = sum_re / (mass + 1.0)
        out_ref[1, :, cols] = sum_im / (mass + 1.0)


def vmem(count):
    return [pl.BlockSpec(memory_space=pltpu.VMEM)] * count


def call(kernel, shape, dtype, args, scratch=(), specs=None):
    return pl.pallas_call(
        kernel,
        out_shape=jax.ShapeDtypeStruct(shape, dtype),
        in_specs=specs or vmem(len(args)),
        out_specs=pl.BlockSpec(memory_space=pltpu.VMEM),
        scratch_shapes=list(scratch),
        compiler_params=pltpu.CompilerParams(vmem_limit_bytes=32 << 20),
    )(*args)


def local(images, references, precision, shifts, labels, log_prior):
    y, zh, c, zl, x = (lax.axis_index(name) for name in ALL)
    img_low = lax.ppermute(images.astype(jnp.bfloat16), ALL, IMG_ROUTE)
    ref_low = lax.ppermute(references.astype(jnp.bfloat16), ALL, REF_ROUTE)
    label_lanes = jnp.concatenate([jnp.zeros((USED,), jnp.float32), jnp.tile(labels.astype(jnp.float32), 4)])
    units = lax.all_to_all(
        jnp.broadcast_to(img_low[None], (32,) + img_low.shape), SPACE, 0, 0, tiled=True
    )
    units = units.reshape(4, 2, 2, 2, 2, 16, 1024)
    cosine, sine = phases(shifts, (zl // 2) * 4 + zh * 2 + zl % 2)
    cross = call(
        cross_kernel,
        (16, 2, 16, LANES),
        jnp.float32,
        (units, ref_low, cosine, sine, label_lanes[None]),
        [pltpu.VMEM((2, LANES, 2048), jnp.bfloat16)],
    )
    got = lax.all_to_all(cross.reshape(512, 1, LANES), ALL, 0, 0, tiled=True)
    own = lax.dynamic_slice_in_dim(precision, (zl % 4) * 4 + x, 1)
    post = call(
        softmax_kernel,
        (4, 2, 2, 32, LANES),
        jnp.float32,
        (got.reshape(4, 2, 2, 32, LANES), log_prior, own),
        specs=vmem(1) + [pl.BlockSpec(memory_space=pltpu.SMEM)] * 2,
    )
    back = lax.all_to_all(post.reshape(512, 1, LANES), ALL, 0, 0, tiled=True).reshape(16, 2, 16, LANES)
    summed = call(back_kernel, (2, 8, 2048), jnp.float32, (back, units, cosine, sine))
    new_refs = lax.ppermute(summed, ALL, REF_ROUTE)
    mine = lax.dynamic_slice_in_dim(back, (y * 2 + zh) * 2 + c, 1, 0)
    class_post = mine[0, 0, :, USED : USED + CLASSES]
    return new_refs, class_post


def solution(mesh):
    whole = Mesh(mesh.devices.reshape(tuple(SIZES.values())), tuple(SIZES))
    return jax.shard_map(
        local,
        mesh=whole,
        in_specs=(P(None, IMG, REF), P(None, REF, IMG), P(IMG), P(), P(REF), P()),
        out_specs=(P(None, REF, IMG), P(IMG, None)),
        check_vma=False,
    )
```

time: 918 us -> 166 us (0.18)
  the two profiles are of different devices: /device:TPU:102 before, /device:TPU:8 now
where the time goes in v1:
time: 166 us; the launch traced here: 165 us
  waiting for transfers between devices  62.6 us (38%)
  starting transfers between devices  59.3 us (36%)
  blocking collectives  33.4 us (20%)
  Pallas kernels  3.91 us (2%)
  local copies, waits for them, and re-layouts  3.76 us (2%)
    all_to_all x1, blocking collectives, local(): lax.all_to_all(post.reshape(512, 1, LANES), ALL, 0, 0, tiled=True)  33.4 us
    all_to_all x1, starting transfers between devices, local(): lax.all_to_all(jnp.broadcast_to(img_low[None], (32,) + img_low.shape), SP...  25.7 us
    all_to_all x1, starting transfers between devices, local(): got = lax.all_to_all(cross.reshape(512, 1, LANES), ALL, 0, 0, tiled=True)  23.6 us
    all_to_all x1, waiting for transfers between devices, local(): got = lax.all_to_all(cross.reshape(512, 1, LANES), ALL, 0, 0, tiled=True)  22.8 us
    all_to_all x1, waiting for transfers between devices, local(): lax.all_to_all(jnp.broadcast_to(img_low[None], (32,) + img_low.shape), SP...  18.3 us
    ppermute x1, waiting for transfers between devices, local(): new_refs = lax.ppermute(summed, ALL, REF_ROUTE)  18 us
    ppermute x1, starting transfers between devices, local(): new_refs = lax.ppermute(summed, ALL, REF_ROUTE)  4.79 us
    ppermute x1, starting transfers between devices, local(): ref_low = lax.ppermute(references.astype(jnp.bfloat16), ALL, REF_ROUTE)  4.58 us
  transfers between devices with their start and end apart: 5, of which 4 were waited for; matrix products, arithmetic and copies ran while one was open for 1% of the time, Pallas kernels for 0%

profile of v1, /device:TPU:8, one launch (start us, length us, event | category | flops | bytes accessed | tf_op | source)
XLA Modules:
  0.0 165.3 jit_solution(1639702486377493857)
XLA Ops:
  0.6 0.9 convert_element_type.31
  1.5 0.7 collective-permute-start
  2.2 0.0 collective-permute-done
  2.2 1.6 broadcast_in_dim.4
  3.8 0.0 copy-start.1
  3.8 0.0 copy-start.3
  3.8 0.0 copy-start.2
  3.8 25.7 %all-to-all-start = ((bf16[32,2,16,1024]{3,2,1,0:T(8,128)(2,1)}), bf16[32,2,16,1024]{3,2,1,0:T(8,128)(2,1)S(1)}, u32[]{:S(2)}, u32[]{:S(2)}) async-start(bf16[32,2,16,1024]{3,2,1,0:T(8,128)(2,1)} %broadcast_in_dim.4), calls=%async_computation | async-start | bytes 4194304 | tf_op jit(solution)/shard_map/all_to_all | solution.py:184
  29.5 0.0 copy-done.1
  29.5 0.0 copy-start.4
  29.6 0.0 copy-start
  29.6 4.6 %collective-permute-start.1 = (bf16[2,8,2048]{2,1,0:T(8,128)(2,1)S(1)}, bf16[2,8,2048]{2,1,0:T(8,128)(2,1)S(1)}, u32[]{:S(2)}, u32[]{:S(2)}) collective-permute-start(bf16[2,8,2048]{2,1,0:T(8,128)(2,1)S(1)} %convert_element_type.32), channel_id=1, source_target_pairs={{0,0},{1,1},{2,2},{3,3},{4,32},{5,33},{6,34},{7,35},{8,128},{9,129... | collective-permute-start | bytes 196616 | tf_op jit(solution)/shard_map/ppermute | solution.py:182
  34.2 0.0 copy-done.3
  34.2 0.1 tile.10
  34.3 0.0 copy-done.2
  34.4 0.6 fusion
  34.9 0.1 pad_bitcast_fusion.label_ref
  35.0 3.5 %collective-permute-done.1.ref_ref = bf16[2,8,2048]{2,1,0:T(8,128)(2,1)S(1)} collective-permute-done((bf16[2,8,2048]{2,1,0:T(8,128)(2,1)S(1)}, bf16[2,8,2048]{2,1,0:T(8,128)(2,1)S(1)}, u32[]{:S(2)}, u32[]{:S(2)}) %collective-permute-start.1) | collective-permute-done | bytes 65568 | tf_op jit(solution)/shard_map/ppermute | solution.py:182
  38.4 18.3 %all-to-all-done = bf16[32,2,16,1024]{3,2,1,0:T(8,128)(2,1)S(1)} async-done(((bf16[32,2,16,1024]{3,2,1,0:T(8,128)(2,1)}), bf16[32,2,16,1024]{3,2,1,0:T(8,128)(2,1)S(1)}, u32[]{:S(2)}, u32[]{:S(2)}) %all-to-all-start) | async-done | bytes 2097184 | tf_op jit(solution)/shard_map/all_to_all | solution.py:184
  56.8 1.5 shard_map.77
  58.3 23.6 %all-to-all-start.1 = ((f32[512,1,128]{2,1,0:T(1,128)}), f32[512,1,128]{2,1,0:T(1,128)S(1)}, u32[]{:S(2)}, u32[]{:S(2)}) async-start(f32[512,1,128]{2,1,0:T(1,128)} %bitcast.5), calls=%async_computation.1 | async-start | bytes 524288 | tf_op jit(solution)/shard_map/all_to_all | solution.py:196
  81.9 0.0 copy-done.4
  81.9 0.6 dynamic_slice.6.precision_ref
  82.5 22.8 %all-to-all-done.1 = f32[512,1,128]{2,1,0:T(1,128)S(1)} async-done(((f32[512,1,128]{2,1,0:T(1,128)}), f32[512,1,128]{2,1,0:T(1,128)S(1)}, u32[]{:S(2)}, u32[]{:S(2)}) %all-to-all-start.1) | async-done | bytes 262176 | tf_op jit(solution)/shard_map/all_to_all | solution.py:196
  105.3 0.0 copy-done
  105.3 1.7 %shard_map.78 = f32[4,2,2,32,128]{4,3,2,1,0:T(8,128)S(1)} custom-call(f32[4,2,2,32,128]{4,3,2,1,0:T(8,128)S(1)} %bitcast.20, f32[4]{0:T(128)S(1)} %copy-done, f32[1]{0:T(128)} %dynamic_slice.6.precision_ref), custom_call_target="tpu_custom_call" | custom-call | tf_op jit(solution)/shard_map/pallas_call | solution.py:169
  107.0 33.4 %all_to_all.15 = f32[512,1,128]{2,1,0:T(1,128)S(1)} all-to-all(f32[512,1,128]{2,1,0:T(1,128)S(1)} %bitcast.21), channel_id=1, replica_groups=mesh['y'=4,'zh'=2,'c'=2,'zl'=8,'x'=4] {'y','zh','c','zl','x'}, dimensions={0} | all-to-all | bytes 524288 | tf_op jit(solution)/shard_map/all_to_all | solution.py:205
  140.4 0.7 shard_map.79
  141.1 4.8 %collective-permute-start.2 = (f32[2,8,2048]{2,1,0:T(8,128)S(1)}, f32[2,8,2048]{2,1,0:T(8,128)S(1)}, u32[]{:S(2)}, u32[]{:S(2)}) collective-permute-start(f32[2,8,2048]{2,1,0:T(8,128)S(1)} %shard_map.79), channel_id=1, source_target_pairs={{0,0},{1,1},{2,2},{3,3},{4,32},{5,33},{6,34},{7,35},{8,128},{9,129... | collective-permute-start | bytes 393224 | tf_op jit(solution)/shard_map/ppermute | solution.py:207
  145.9 0.1 constant_dynamic-slice_fusion
  145.9 0.7 copy.11
  146.6 18.0 %collective-permute-done.2 = f32[2,8,2048]{2,1,0:T(8,128)S(1)} collective-permute-done((f32[2,8,2048]{2,1,0:T(8,128)S(1)}, f32[2,8,2048]{2,1,0:T(8,128)S(1)}, u32[]{:S(2)}, u32[]{:S(2)}) %collective-permute-start.2) | collective-permute-done | bytes 131104 | tf_op jit(solution)/shard_map/ppermute | solution.py:207
  164.6 0.7 copy.13
  (5 shorter events, 0.0 us)
Async XLA Ops:
  1.5 0.7 collective-permute-start
  3.8 25.7 %copy-start.1 = (f32[2,8,2048]{2,1,0:T(8,128)S(1)}, f32[2,8,2048]{2,1,0:T(8,128)}, u32[]{:S(2)}) copy-start(f32[2,8,2048]{2,1,0:T(8,128)} %param.7) | copy-start | bytes 393220
  3.8 30.4 %copy-start.3 = (s32[8]{0:T(128)S(1)}, s32[8]{0:T(128)}, u32[]{:S(2)}) copy-start(s32[8]{0:T(128)} %param.10) | copy-start | bytes 100
  3.8 30.5 %copy-start.2 = (s32[12,2]{0,1:T(2,128)S(1)}, s32[12,2]{0,1:T(2,128)}, u32[]{:S(2)}) copy-start(s32[12,2]{0,1:T(2,128)} %param.9) | copy-start | bytes 292
  3.8 52.9 %all-to-all-start = ((bf16[32,2,16,1024]{3,2,1,0:T(8,128)(2,1)}), bf16[32,2,16,1024]{3,2,1,0:T(8,128)(2,1)S(1)}, u32[]{:S(2)}, u32[]{:S(2)}) async-start(bf16[32,2,16,1024]{3,2,1,0:T(8,128)(2,1)} %broadcast_in_dim.4), calls=%async_computation | async-start | bytes 4194304 | tf_op jit(solution)/shard_map/all_to_all | solution.py:184
  29.5 52.4 %copy-start.4 = (f32[16]{0:T(128)S(1)}, f32[16]{0:T(128)}, u32[]{:S(2)}) copy-start(f32[16]{0:T(128)} %param.8) | copy-start | bytes 196
  29.6 75.7 %copy-start = (f32[4]{0:T(128)S(1)}, f32[4]{0:T(128)}, u32[]{:S(2)}) copy-start(f32[4]{0:T(128)} %prior_ref.1) | copy-start | bytes 52
  29.6 8.8 %collective-permute-start.1 = (bf16[2,8,2048]{2,1,0:T(8,128)(2,1)S(1)}, bf16[2,8,2048]{2,1,0:T(8,128)(2,1)S(1)}, u32[]{:S(2)}, u32[]{:S(2)}) collective-permute-start(bf16[2,8,2048]{2,1,0:T(8,128)(2,1)S(1)} %convert_element_type.32), channel_id=1, source_target_pairs={{0,0},{1,1},{2,2},{3,3},{4,32},{5,33},{6,34},{7,35},{8,128},{9,129... | collective-permute-start | bytes 196616 | tf_op jit(solution)/shard_map/ppermute | solution.py:182
  58.3 47.0 %all-to-all-start.1 = ((f32[512,1,128]{2,1,0:T(1,128)}), f32[512,1,128]{2,1,0:T(1,128)S(1)}, u32[]{:S(2)}, u32[]{:S(2)}) async-start(f32[512,1,128]{2,1,0:T(1,128)} %bitcast.5), calls=%async_computation.1 | async-start | bytes 524288 | tf_op jit(solution)/shard_map/all_to_all | solution.py:196
  141.1 23.6 %collective-permute-start.2 = (f32[2,8,2048]{2,1,0:T(8,128)S(1)}, f32[2,8,2048]{2,1,0:T(8,128)S(1)}, u32[]{:S(2)}, u32[]{:S(2)}) collective-permute-start(f32[2,8,2048]{2,1,0:T(8,128)S(1)} %shard_map.79), channel_id=1, source_target_pairs={{0,0},{1,1},{2,2},{3,3},{4,32},{5,33},{6,34},{7,35},{8,128},{9,129... | collective-permute-start | bytes 393224 | tf_op jit(solution)/shard_map/ppermute | solution.py:207

commit v2 on v0

v2 whole, which is shorter than its diff:
```python
import itertools
import math

import jax
import jax.numpy as jnp
from jax import lax
from jax.experimental import pallas as pl
from jax.experimental.pallas import tpu as pltpu
from jax.sharding import Mesh
from jax.sharding import PartitionSpec as P

ROWS = 256
COLS = 128
SHIFTS = 12
CLASSES = 4
LANES = 128
USED = SHIFTS * 8
PIXELS = 2048
HALF = 1024
SIZES = {"y": 4, "zh": 2, "c": 2, "zl": 8, "xh": 2, "xl": 2}
ALL = tuple(SIZES)
IMG = ("y", "zh", "c")
REF = ("zl", "xh", "xl")
SPACE = ("y", "c", "xl")
BLOCK = ("zl", "xh")


def place(*coords):
    number = 0
    for size, coord in zip(SIZES.values(), coords, strict=True):
        number = number * size + coord
    return number


def routes(inward):
    made = []
    for r in range(2):
        pairs = []
        for y, zh, c, zl, xh, xl in itertools.product(*(range(size) for size in SIZES.values())):
            work = place(y, zh, c, zl, xh, xl)
            home = place(zl // 2, zl % 2, xh, 2 * y + c, r ^ zh, xl)
            pairs.append((home, work) if inward else (work, home))
        made.append(pairs)
    return made


def phases(shifts, block):
    index = block * PIXELS + jnp.arange(PIXELS, dtype=jnp.int32)
    freq_y = (index // COLS - ROWS // 2).astype(jnp.float32)
    freq_x = (index % COLS).astype(jnp.float32)
    shift_x = shifts[:, 0].astype(jnp.float32)[:, None]
    shift_y = shifts[:, 1].astype(jnp.float32)[:, None]
    angles = 2.0 * math.pi / ROWS * (freq_x[None, :] * shift_x + freq_y[None, :] * shift_y)
    return jnp.cos(angles), jnp.sin(angles)


def iota(shape, axis):
    return lax.broadcasted_iota(jnp.int32, shape, axis)


def own_lanes():
    lane = iota((8, LANES), 1)
    return (lane % 8 == iota((8, LANES), 0)) & (lane < USED)


def as_row(column):
    return jnp.sum(jnp.where(own_lanes(), column, 0.0), axis=0, keepdims=True)


def image_kernel(img_ref, precision_ref, out_ref):
    low = img_ref[...].astype(jnp.bfloat16)
    precision = jnp.sum(
        jnp.where(iota((16, 16), 0) == iota((16, 16), 1), precision_ref[...], 0.0), axis=1, keepdims=True
    )
    first = precision.astype(jnp.bfloat16).astype(jnp.float32)
    second = (precision - first).astype(jnp.bfloat16).astype(jnp.float32)
    third = precision - first - second
    lane = iota((16, LANES), 1)
    pieces = jnp.where(lane == 0, first, jnp.where(lane == 1, second, jnp.where(lane == 2, third, 0.0)))
    pieces = pieces.astype(jnp.bfloat16)
    for copy in range(16):
        out_ref[copy, :, :, :HALF] = low
        out_ref[copy, 0, :, HALF:] = pieces
        out_ref[copy, 1, :, HALF:] = pieces


def ref_kernel(ref_ref, label_ref, out_ref):
    out_ref[:, :, :PIXELS] = ref_ref[...].astype(jnp.bfloat16)
    label = label_ref[...].astype(jnp.float32)
    label = jnp.sum(jnp.where(iota((8, 8), 0) == iota((8, 8), 1), label, 0.0), axis=1, keepdims=True)
    label = jnp.broadcast_to(label, (8, LANES)).astype(jnp.bfloat16)
    out_ref[0, :, PIXELS:] = label
    out_ref[1, :, PIXELS:] = label


def cross_kernel(img_ref, ref0_ref, ref1_ref, cos_ref, sin_ref, zh_ref, out_ref, shifted):
    straight = zh_ref[0] == 0
    ref0 = ref0_ref[:, :, :PIXELS].astype(jnp.float32)
    ref1 = ref1_ref[:, :, :PIXELS].astype(jnp.float32)
    halves = []
    for e in range(2):
        ref = jnp.where(straight, ref0, ref1) if e == 0 else jnp.where(straight, ref1, ref0)
        re, im = ref[0], ref[1]
        halves.append(as_row(0.5 * jnp.sum(re * re + im * im, axis=1, keepdims=True)))
        for pair in range(SHIFTS // 2):
            rot_re, rot_im = [], []
            for t in (2 * pair, 2 * pair + 1):
                cos, sin = cos_ref[t : t + 1, :], sin_ref[t : t + 1, :]
                rot_re.append(re * cos + im * sin)
                rot_im.append(im * cos - re * sin)
            rows = slice(e * LANES + 16 * pair, e * LANES + 16 * pair + 16)
            shifted[0, rows, :] = jnp.concatenate(rot_re, axis=0).astype(jnp.bfloat16)
            shifted[1, rows, :] = jnp.concatenate(rot_im, axis=0).astype(jnp.bfloat16)
        spare = slice(e * LANES + USED, (e + 1) * LANES)
        shifted[:, spare, :] = jnp.zeros((2, LANES - USED, PIXELS), jnp.bfloat16)
    total = jnp.zeros((128, 2 * LANES), jnp.float32)
    for h in range(2):
        for part in range(2):
            total += lax.dot_general(
                img_ref[:, h, part, :, :HALF].reshape(128, HALF),
                shifted[part, :, h * HALF : (h + 1) * HALF],
                (((1,), (1,)), ((), ())),
                preferred_element_type=jnp.float32,
            )
    pieces = img_ref[:, 0, 0, :, HALF:].reshape(128, LANES).astype(jnp.float32)
    precision = jnp.sum(pieces, axis=1, keepdims=True)
    scaled = precision * (total - jnp.concatenate(halves, axis=1))
    out_ref[...] = scaled.reshape(16, 8, 2 * LANES)


def label_rows(ref0_ref, ref1_ref, straight):
    first = ref0_ref[0].astype(jnp.float32)
    second = ref1_ref[0].astype(jnp.float32)
    low, high = jnp.where(straight, first, second), jnp.where(straight, second, first)
    return jnp.concatenate([as_row(low), as_row(high)], axis=1)


def score_kernel(got_ref, ref0_ref, ref1_ref, prior_ref, zh_ref, score_ref, out_ref):
    labels = label_rows(ref0_ref, ref1_ref, zh_ref[0] == 0)
    prior = jnp.zeros((1, 2 * LANES), jnp.float32)
    for k in range(CLASSES):
        prior = jnp.where(labels == k, prior_ref[k], prior)
    scores = jnp.sum(got_ref[...], axis=0) + prior
    scores = jnp.where(iota((8, 2 * LANES), 1) % LANES < USED, scores, -jnp.inf)
    score_ref[...] = scores
    top = jnp.max(scores, axis=1, keepdims=True)
    weights = jnp.exp(scores - top)
    lane = iota((8, LANES), 1)
    stats = jnp.where(lane == 0, top, 0.0)
    for k in range(CLASSES):
        mass = jnp.sum(jnp.where(labels == k, weights, 0.0), axis=1, keepdims=True)
        stats = jnp.where(lane == k + 1, mass, stats)
    out_ref[...] = jnp.broadcast_to(stats[None], (16, 8, LANES))


def post_kernel(got_ref, score_ref, out_ref):
    got = got_ref[...]
    tops = got[:, :, 0:1]
    top = jnp.max(tops, axis=0)
    lane = iota((8, LANES), 1)
    sums = jnp.sum(got * jnp.exp(tops - top[None]), axis=0)
    sums = jnp.where((lane > 0) & (lane <= CLASSES), sums, 0.0)
    total = jnp.sum(sums, axis=1, keepdims=True)
    classes = pltpu.roll(sums / total, USED - 1, 1)
    post = jnp.exp(score_ref[...] - top) / total
    post = jnp.concatenate([jnp.where(lane < USED, post[:, :LANES], classes), post[:, LANES:]], axis=1)
    out_ref[...] = jnp.broadcast_to(post[None], (16, 8, 2 * LANES))


def back_kernel(got_ref, img_ref, cos_ref, sin_ref, zh_ref, out0_ref, out1_ref):
    straight = zh_ref[0] == 0
    post = got_ref[...].reshape(128, 2 * LANES)
    post = jnp.where(iota((128, 2 * LANES), 1) % LANES < USED, post, 0.0)
    mass_row = jnp.sum(post, axis=0, keepdims=True)
    weights = jnp.transpose(post).astype(jnp.bfloat16)
    for h in range(2):
        cols = slice(h * HALF, (h + 1) * HALF)
        back = [
            jnp.dot(
                weights,
                img_ref[:, h, part, :, :HALF].reshape(128, HALF),
                preferred_element_type=jnp.float32,
            )
            for part in range(2)
        ]
        sums = [jnp.zeros((8, HALF), jnp.float32) for both in range(4)]
        for t in range(SHIFTS):
            cos, sin = cos_ref[t : t + 1, cols], sin_ref[t : t + 1, cols]
            for e in range(2):
                rows = slice(e * LANES + 8 * t, e * LANES + 8 * t + 8)
                back_re, back_im = back[0][rows], back[1][rows]
                sums[2 * e] += back_re * cos - back_im * sin
                sums[2 * e + 1] += back_im * cos + back_re * sin
        for part in range(2):
            out0_ref[part, :, cols] = jnp.where(straight, sums[part], sums[2 + part])
            out1_ref[part, :, cols] = jnp.where(straight, sums[2 + part], sums[part])
    masses = []
    for e in range(2):
        row = mass_row[:, e * LANES : (e + 1) * LANES]
        mass = jnp.sum(jnp.where(own_lanes(), row, 0.0), axis=1, keepdims=True)
        masses.append(jnp.broadcast_to(mass, (8, LANES)))
    for part in range(2):
        out0_ref[part, :, PIXELS:] = jnp.where(straight, masses[0], masses[1])
        out1_ref[part, :, PIXELS:] = jnp.where(straight, masses[1], masses[0])


def call(kernel, shapes, args, scratch=(), scalars=0):
    in_vmem = [pl.BlockSpec(memory_space=pltpu.VMEM)] * (len(args) - scalars)
    in_smem = [pl.BlockSpec(memory_space=pltpu.SMEM)] * scalars
    out = [jax.ShapeDtypeStruct(shape, dtype) for shape, dtype in shapes]
    return pl.pallas_call(
        kernel,
        out_shape=out,
        in_specs=in_vmem + in_smem,
        out_specs=[pl.BlockSpec(memory_space=pltpu.VMEM)] * len(out),
        scratch_shapes=list(scratch),
        compiler_params=pltpu.CompilerParams(vmem_limit_bytes=32 << 20),
    )(*args)


def swap(operand, axes):
    return lax.all_to_all(operand, axes, 0, 0, tiled=True)


def local(images, references, precision, shifts, labels, log_prior):
    y, zh, c, zl, xh, xl = (lax.axis_index(name) for name in ALL)
    half = zh.astype(jnp.int32)[None]
    (sent,) = call(image_kernel, [((16, 2, 16, HALF + LANES), jnp.bfloat16)], (images, precision[None]))
    units = swap(sent, SPACE).reshape(8, 2, 2, 16, HALF + LANES)
    (low,) = call(ref_kernel, [((2, 8, PIXELS + LANES), jnp.bfloat16)], (references, labels[None]))
    refs = [lax.ppermute(low, ALL, route) for route in routes(True)]
    tags = [ref[:1, :, PIXELS:] for ref in refs]
    cosine, sine = phases(shifts, zl * 2 + xh)
    (cross,) = call(
        cross_kernel,
        [((16, 8, 2 * LANES), jnp.float32)],
        (units, *refs, cosine, sine, half),
        [pltpu.VMEM((2, 2 * LANES, PIXELS), jnp.bfloat16)],
        scalars=1,
    )
    scores, stats = call(
        score_kernel,
        [((8, 2 * LANES), jnp.float32), ((16, 8, LANES), jnp.float32)],
        (swap(cross, BLOCK), *tags, log_prior, half),
        scalars=2,
    )
    (post,) = call(post_kernel, [((16, 8, 2 * LANES), jnp.float32)], (swap(stats, SPACE), scores))
    posts = swap(post, BLOCK)
    partial = call(
        back_kernel,
        [((2, 8, PIXELS + LANES), jnp.float32)] * 2,
        (posts, units, cosine, sine, half),
        scalars=1,
    )
    first, second = [lax.ppermute(part, ALL, route) for part, route in zip(partial, routes(False), strict=True)]
    both = first + second
    new_refs = both[:, :, :PIXELS] / (both[:, :, PIXELS : PIXELS + 1] + 1.0)
    mine = lax.dynamic_slice_in_dim(posts, (y * 2 + c) * 2, 2, 0)
    class_post = mine.reshape(16, 2 * LANES)[:, USED : USED + CLASSES]
    return new_refs, class_post


def solution(mesh):
    whole = Mesh(mesh.devices.reshape(tuple(SIZES.values())), ALL)
    return jax.shard_map(
        local,
        mesh=whole,
        in_specs=(P(None, IMG, REF), P(None, REF, IMG), P(IMG), P(), P(REF), P()),
        out_specs=(P(None, REF, IMG), P(IMG, None)),
        check_vma=False,
    )
```

time: 918 us -> 125 us (0.14)
  the two profiles are of different devices: /device:TPU:102 before, /device:TPU:24 now
where the time goes in v2:
time: 125 us; the launch traced here: 124 us
  waiting for transfers between devices  44.9 us (36%)
  starting transfers between devices  41.6 us (33%)
  blocking collectives  28.7 us (23%)
  Pallas kernels  4.74 us (4%)
  local copies, waits for them, and re-layouts  2.31 us (2%)
  other arithmetic  1.42 us (1%)
    all_to_all x2, blocking collectives, swap(): return lax.all_to_all(operand, axes, 0, 0, tiled=True)  28.7 us
    all_to_all x2, starting transfers between devices, swap(): return lax.all_to_all(operand, axes, 0, 0, tiled=True)  18.5 us
    ppermute x2, waiting for transfers between devices, local(): lax.ppermute(part, ALL, route)  16.1 us
    ppermute x2, waiting for transfers between devices, local(): refs = [lax.ppermute(low, ALL, route) for route in routes(True)]  15.1 us
    all_to_all x2, waiting for transfers between devices, swap(): return lax.all_to_all(operand, axes, 0, 0, tiled=True)  13.8 us
    ppermute x2, starting transfers between devices, local(): lax.ppermute(part, ALL, route)  13.2 us
    ppermute x2, starting transfers between devices, local(): refs = [lax.ppermute(low, ALL, route) for route in routes(True)]  9.9 us
    pallas_call x6, Pallas kernels, call(): pl.pallas_call(kernel, out_shape=out, in_specs=in_vmem + in_smem, out_spe...  4.74 us
  transfers between devices with their start and end apart: 6, of which 5 were waited for; matrix products, arithmetic and copies ran while one was open for 1% of the time, Pallas kernels for 0%

profile of v2, /device:TPU:24, one launch (start us, length us, event | category | flops | bytes accessed | tf_op | source)
XLA Modules:
  0.0 124.4 jit_solution(50589269148794151)
XLA Ops:
  0.6 0.0 copy-start
  0.6 0.9 copy-done
  1.5 0.0 copy-start.2
  1.5 0.7 copy-done.2
  2.2 1.1 shard_map.77
  3.3 0.0 copy-start.1
  3.3 0.0 copy-start.3
  3.3 0.0 copy-start.5
  3.3 9.3 %all-to-all-start = ((bf16[16,2,16,1152]{3,2,1,0:T(8,128)(2,1)}), bf16[16,2,16,1152]{3,2,1,0:T(8,128)(2,1)S(1)}, u32[]{:S(2)}, u32[]{:S(2)}) async-start(bf16[16,2,16,1152]{3,2,1,0:T(8,128)(2,1)} %shard_map.77), calls=%async_computation | async-start | bytes 2359296 | tf_op jit(solution)/shard_map/all_to_all | solution.py:222
  12.6 0.0 copy-done.1
  12.6 0.0 copy-done.3
  12.6 0.1 shard_map.78
  12.7 0.0 copy-start.4
  12.7 7.9 %collective-permute-start = (bf16[2,8,2176]{2,1,0:T(8,128)(2,1)S(1)}, bf16[2,8,2176]{2,1,0:T(8,128)(2,1)S(1)}, u32[]{:S(2)}, u32[]{:S(2)}) collective-permute-start(bf16[2,8,2176]{2,1,0:T(8,128)(2,1)S(1)} %shard_map.78), channel_id=1, source_target_pairs={{0,0},{1,1},{32,2},{33,3},{64,4},{65,5},{96,6},{97,7},{128,8},{129... | collective-permute-start | bytes 208904 | tf_op jit(solution)/shard_map/ppermute | solution.py:231
  20.7 2.0 %collective-permute-start.1 = (bf16[2,8,2176]{2,1,0:T(8,128)(2,1)S(1)}, bf16[2,8,2176]{2,1,0:T(8,128)(2,1)S(1)}, u32[]{:S(2)}, u32[]{:S(2)}) collective-permute-start(bf16[2,8,2176]{2,1,0:T(8,128)(2,1)S(1)} %shard_map.78), channel_id=1, source_target_pairs={{2,0},{3,1},{34,2},{35,3},{66,4},{67,5},{98,6},{99,7},{130,8},{131... | collective-permute-start | bytes 208904 | tf_op jit(solution)/shard_map/ppermute | solution.py:231
  22.7 0.0 copy-done.5
  22.7 0.6 fusion
  23.3 8.1 %collective-permute-done.ref0_ref = bf16[2,8,2176]{2,1,0:T(8,128)(2,1)S(1)} collective-permute-done((bf16[2,8,2176]{2,1,0:T(8,128)(2,1)S(1)}, bf16[2,8,2176]{2,1,0:T(8,128)(2,1)S(1)}, u32[]{:S(2)}, u32[]{:S(2)}) %collective-permute-start) | collective-permute-done | bytes 69664 | tf_op jit(solution)/shard_map/ppermute | solution.py:231
  31.3 7.0 %collective-permute-done.1.ref1_ref = bf16[2,8,2176]{2,1,0:T(8,128)(2,1)S(1)} collective-permute-done((bf16[2,8,2176]{2,1,0:T(8,128)(2,1)S(1)}, bf16[2,8,2176]{2,1,0:T(8,128)(2,1)S(1)}, u32[]{:S(2)}, u32[]{:S(2)}) %collective-permute-start.1) | collective-permute-done | bytes 69664 | tf_op jit(solution)/shard_map/ppermute | solution.py:231
  38.3 0.0 all-to-all-done
  38.3 1.5 %shard_map.79 = f32[16,8,256]{2,1,0:T(8,128)} custom-call(bf16[8,2,2,16,1152]{4,3,2,1,0:T(8,128)(2,1)S(1)} %bitcast.10, bf16[2,8,2176]{2,1,0:T(8,128)(2,1)S(1)} %collective-permute-done.ref0_ref, bf16[2,8,2176]{2,1,0:T(8,128)(2,1)S(1)} %collective-permute-done.1.ref1_ref, f32[12,2048]{1,0:T(8,128)S(1)} %get-tuple-element.13.cos_ref, ...), custom_call_target="tpu_custom_call" | custom-call | tf_op jit(solution)/shard_map/pallas_call | solution.py:211
  39.9 9.2 %all-to-all-start.1 = ((f32[16,8,256]{2,1,0:T(8,128)}), f32[16,8,256]{2,1,0:T(8,128)S(1)}, u32[]{:S(2)}, u32[]{:S(2)}) async-start(f32[16,8,256]{2,1,0:T(8,128)} %shard_map.79), calls=%async_computation.1 | async-start | bytes 262144 | tf_op jit(solution)/shard_map/all_to_all | solution.py:222
  49.1 13.8 %all-to-all-done.1.got_ref = f32[16,8,256]{2,1,0:T(8,128)S(1)} async-done(((f32[16,8,256]{2,1,0:T(8,128)}), f32[16,8,256]{2,1,0:T(8,128)S(1)}, u32[]{:S(2)}, u32[]{:S(2)}) %all-to-all-start.1) | async-done | bytes 131104 | tf_op jit(solution)/shard_map/all_to_all | solution.py:222
  62.8 0.0 copy-done.4
  62.8 0.7 shard_map.80
  63.6 9.8 %all_to_all.20.got_ref = f32[16,8,128]{2,1,0:T(8,128)S(1)} all-to-all(f32[16,8,128]{2,1,0:T(8,128)S(1)} %get-tuple-element.6), channel_id=1, replica_groups=mesh['y'=4,'zh'=2,'c'=2,'zl'=8,'xh'=2,'xl'=2] {'y','c','xl'}, dimensions={0} | all-to-all | bytes 131072 | tf_op jit(solution)/shard_map/all_to_all | solution.py:222
  73.4 0.2 shard_map.81
  73.6 18.9 %all_to_all.21.got_ref = f32[16,8,256]{2,1,0:T(8,128)S(1)} all-to-all(f32[16,8,256]{2,1,0:T(8,128)S(1)} %shard_map.81), channel_id=1, replica_groups=mesh['y'=4,'zh'=2,'c'=2,'zl'=8,'xh'=2,'xl'=2] {'zl','xh'}, dimensions={0} | all-to-all | bytes 262144 | tf_op jit(solution)/shard_map/all_to_all | solution.py:222
  92.5 1.0 shard_map.82
  93.5 5.6 %collective-permute-start.2 = (f32[2,8,2176]{2,1,0:T(8,128)S(1)}, f32[2,8,2176]{2,1,0:T(8,128)S(1)}, u32[]{:S(2)}, u32[]{:S(2)}) collective-permute-start(f32[2,8,2176]{2,1,0:T(8,128)S(1)} %get-tuple-element.8), channel_id=1, source_target_pairs={{0,0},{1,1},{2,32},{3,33},{4,64},{5,65},{6,96},{7,97},{8,128},{9,1... | collective-permute-start | bytes 417800 | tf_op jit(solution)/shard_map/ppermute | solution.py:255
  99.2 7.6 %collective-permute-start.3 = (f32[2,8,2176]{2,1,0:T(8,128)S(1)}, f32[2,8,2176]{2,1,0:T(8,128)S(1)}, u32[]{:S(2)}, u32[]{:S(2)}) collective-permute-start(f32[2,8,2176]{2,1,0:T(8,128)S(1)} %get-tuple-element.9), channel_id=1, source_target_pairs={{0,2},{1,3},{2,34},{3,35},{4,66},{5,67},{6,98},{7,99},{8,130},{9,1... | collective-permute-start | bytes 417800 | tf_op jit(solution)/shard_map/ppermute | solution.py:255
  106.8 0.1 slice.32
  106.9 0.7 copy.8
  107.5 3.1 %collective-permute-done.2 = f32[2,8,2176]{2,1,0:T(8,128)S(1)} collective-permute-done((f32[2,8,2176]{2,1,0:T(8,128)S(1)}, f32[2,8,2176]{2,1,0:T(8,128)S(1)}, u32[]{:S(2)}, u32[]{:S(2)}) %collective-permute-start.2) | collective-permute-done | bytes 139296 | tf_op jit(solution)/shard_map/ppermute | solution.py:255
  110.6 13.0 %collective-permute-done.3 = f32[2,8,2176]{2,1,0:T(8,128)S(1)} collective-permute-done((f32[2,8,2176]{2,1,0:T(8,128)S(1)}, f32[2,8,2176]{2,1,0:T(8,128)S(1)}, u32[]{:S(2)}, u32[]{:S(2)}) %collective-permute-start.3) | collective-permute-done | bytes 139296 | tf_op jit(solution)/shard_map/ppermute | solution.py:255
  123.6 0.1 fusion.5
  123.7 0.7 slice_divide_fusion
  (6 shorter events, 0.1 us)
Async XLA Ops:
  0.6 0.9 copy-start
  1.5 0.7 copy-start.2
  3.3 9.3 %copy-start.1 = (f32[2,8,2048]{2,1,0:T(8,128)S(1)}, f32[2,8,2048]{2,1,0:T(8,128)}, u32[]{:S(2)}) copy-start(f32[2,8,2048]{2,1,0:T(8,128)} %ref_ref.1) | copy-start | bytes 393220
  3.3 9.3 %copy-start.3 = (s32[8]{0:T(128)S(1)}, s32[8]{0:T(128)}, u32[]{:S(2)}) copy-start(s32[8]{0:T(128)} %param.10) | copy-start | bytes 100
  3.3 19.3 %copy-start.5 = (s32[12,2]{0,1:T(2,128)S(1)}, s32[12,2]{0,1:T(2,128)}, u32[]{:S(2)}) copy-start(s32[12,2]{0,1:T(2,128)} %param.9) | copy-start | bytes 292
  3.3 35.0 %all-to-all-start = ((bf16[16,2,16,1152]{3,2,1,0:T(8,128)(2,1)}), bf16[16,2,16,1152]{3,2,1,0:T(8,128)(2,1)S(1)}, u32[]{:S(2)}, u32[]{:S(2)}) async-start(bf16[16,2,16,1152]{3,2,1,0:T(8,128)(2,1)} %shard_map.77), calls=%async_computation | async-start | bytes 2359296 | tf_op jit(solution)/shard_map/all_to_all | solution.py:222
  12.7 50.1 %copy-start.4 = (f32[4]{0:T(128)S(1)}, f32[4]{0:T(128)}, u32[]{:S(2)}) copy-start(f32[4]{0:T(128)} %prior_ref.1) | copy-start | bytes 52
  12.7 18.6 %collective-permute-start = (bf16[2,8,2176]{2,1,0:T(8,128)(2,1)S(1)}, bf16[2,8,2176]{2,1,0:T(8,128)(2,1)S(1)}, u32[]{:S(2)}, u32[]{:S(2)}) collective-permute-start(bf16[2,8,2176]{2,1,0:T(8,128)(2,1)S(1)} %shard_map.78), channel_id=1, source_target_pairs={{0,0},{1,1},{32,2},{33,3},{64,4},{65,5},{96,6},{97,7},{128,8},{129... | collective-permute-start | bytes 208904 | tf_op jit(solution)/shard_map/ppermute | solution.py:231
  20.7 17.6 %collective-permute-start.1 = (bf16[2,8,2176]{2,1,0:T(8,128)(2,1)S(1)}, bf16[2,8,2176]{2,1,0:T(8,128)(2,1)S(1)}, u32[]{:S(2)}, u32[]{:S(2)}) collective-permute-start(bf16[2,8,2176]{2,1,0:T(8,128)(2,1)S(1)} %shard_map.78), channel_id=1, source_target_pairs={{2,0},{3,1},{34,2},{35,3},{66,4},{67,5},{98,6},{99,7},{130,8},{131... | collective-permute-start | bytes 208904 | tf_op jit(solution)/shard_map/ppermute | solution.py:231
  39.9 23.0 %all-to-all-start.1 = ((f32[16,8,256]{2,1,0:T(8,128)}), f32[16,8,256]{2,1,0:T(8,128)S(1)}, u32[]{:S(2)}, u32[]{:S(2)}) async-start(f32[16,8,256]{2,1,0:T(8,128)} %shard_map.79), calls=%async_computation.1 | async-start | bytes 262144 | tf_op jit(solution)/shard_map/all_to_all | solution.py:222
  93.5 17.1 %collective-permute-start.2 = (f32[2,8,2176]{2,1,0:T(8,128)S(1)}, f32[2,8,2176]{2,1,0:T(8,128)S(1)}, u32[]{:S(2)}, u32[]{:S(2)}) collective-permute-start(f32[2,8,2176]{2,1,0:T(8,128)S(1)} %get-tuple-element.8), channel_id=1, source_target_pairs={{0,0},{1,1},{2,32},{3,33},{4,64},{5,65},{6,96},{7,97},{8,128},{9,1... | collective-permute-start | bytes 417800 | tf_op jit(solution)/shard_map/ppermute | solution.py:255
  99.2 24.4 %collective-permute-start.3 = (f32[2,8,2176]{2,1,0:T(8,128)S(1)}, f32[2,8,2176]{2,1,0:T(8,128)S(1)}, u32[]{:S(2)}, u32[]{:S(2)}) collective-permute-start(f32[2,8,2176]{2,1,0:T(8,128)S(1)} %get-tuple-element.9), channel_id=1, source_target_pairs={{0,2},{1,3},{2,34},{3,35},{4,66},{5,67},{6,98},{7,99},{8,130},{9,1... | collective-permute-start | bytes 417800 | tf_op jit(solution)/shard_map/ppermute | solution.py:255

commit v3 on v2

--- a/solution.py
+++ b/solution.py
@@ -15,6 +15,8 @@
 CLASSES = 4
 LANES = 128
 USED = SHIFTS * 8
+MASS = USED
+CLASS = USED + 4
 PIXELS = 2048
 HALF = 1024
 SIZES = {"y": 4, "zh": 2, "c": 2, "zl": 8, "xh": 2, "xl": 2}
@@ -67,14 +69,18 @@
     return jnp.sum(jnp.where(own_lanes(), column, 0.0), axis=0, keepdims=True)
 
 
+def pieces_of(value):
+    first = value.astype(jnp.bfloat16).astype(jnp.float32)
+    second = (value - first).astype(jnp.bfloat16).astype(jnp.float32)
+    return first, second, value - first - second
+
+
 def image_kernel(img_ref, precision_ref, out_ref):
     low = img_ref[...].astype(jnp.bfloat16)
     precision = jnp.sum(
         jnp.where(iota((16, 16), 0) == iota((16, 16), 1), precision_ref[...], 0.0), axis=1, keepdims=True
     )
-    first = precision.astype(jnp.bfloat16).astype(jnp.float32)
-    second = (precision - first).astype(jnp.bfloat16).astype(jnp.float32)
-    third = precision - first - second
+    first, second, third = pieces_of(precision)
     lane = iota((16, LANES), 1)
     pieces = jnp.where(lane == 0, first, jnp.where(lane == 1, second, jnp.where(lane == 2, third, 0.0)))
     pieces = pieces.astype(jnp.bfloat16)
@@ -161,17 +167,27 @@
     sums = jnp.sum(got * jnp.exp(tops - top[None]), axis=0)
     sums = jnp.where((lane > 0) & (lane <= CLASSES), sums, 0.0)
     total = jnp.sum(sums, axis=1, keepdims=True)
-    classes = pltpu.roll(sums / total, USED - 1, 1)
+    classes = pieces_of(sums / total)
     post = jnp.exp(score_ref[...] - top) / total
-    post = jnp.concatenate([jnp.where(lane < USED, post[:, :LANES], classes), post[:, LANES:]], axis=1)
-    out_ref[...] = jnp.broadcast_to(post[None], (16, 8, 2 * LANES))
+    mass_row = jnp.sum(post, axis=0, keepdims=True)
+    for e in range(2):
+        half = slice(e * LANES, (e + 1) * LANES)
+        mass = jnp.sum(jnp.where(own_lanes(), mass_row[:, half], 0.0), axis=1, keepdims=True)
+        message = jnp.where(lane < USED, post[:, half], 0.0)
+        for number, piece in enumerate(pieces_of(mass)):
+            message = jnp.where(lane == MASS + number, piece, message)
+        if e == 0:
+            for number, piece in enumerate(classes):
+                message += pltpu.roll(piece, CLASS + CLASSES * number - 1, 1)
+        out_ref[:, :, half] = jnp.broadcast_to(message.astype(jnp.bfloat16)[None], (16, 8, LANES))
 
 
 def back_kernel(got_ref, img_ref, cos_ref, sin_ref, zh_ref, out0_ref, out1_ref):
     straight = zh_ref[0] == 0
-    post = got_ref[...].reshape(128, 2 * LANES)
+    got = got_ref[...].astype(jnp.float32)
+    extra = jnp.sum(got, axis=0)
+    post = got.reshape(128, 2 * LANES)
     post = jnp.where(iota((128, 2 * LANES), 1) % LANES < USED, post, 0.0)
-    mass_row = jnp.sum(post, axis=0, keepdims=True)
     weights = jnp.transpose(post).astype(jnp.bfloat16)
     for h in range(2):
         cols = slice(h * HALF, (h + 1) * HALF)
@@ -192,16 +208,29 @@
                 sums[2 * e] += back_re * cos - back_im * sin
                 sums[2 * e + 1] += back_im * cos + back_re * sin
         for part in range(2):
-            out0_ref[part, :, cols] = jnp.where(straight, sums[part], sums[2 + part])
-            out1_ref[part, :, cols] = jnp.where(straight, sums[2 + part], sums[part])
+            low, high = sums[part].astype(jnp.bfloat16), sums[2 + part].astype(jnp.bfloat16)
+            out0_ref[part, :, cols] = jnp.where(straight, low, high)
+            out1_ref[part, :, cols] = jnp.where(straight, high, low)
+    lane = iota((8, LANES), 1)
     masses = []
     for e in range(2):
-        row = mass_row[:, e * LANES : (e + 1) * LANES]
-        mass = jnp.sum(jnp.where(own_lanes(), row, 0.0), axis=1, keepdims=True)
-        masses.append(jnp.broadcast_to(mass, (8, LANES)))
+        mine = (lane >= MASS) & (lane < MASS + 3)
+        mass = jnp.sum(jnp.where(mine, extra[:, e * LANES : (e + 1) * LANES], 0.0), axis=1, keepdims=True)
+        row = jnp.zeros((8, LANES), jnp.float32)
+        for number, piece in enumerate(pieces_of(mass)):
+            row = jnp.where(lane == number, piece, row)
+        masses.append(row.astype(jnp.bfloat16))
     for part in range(2):
         out0_ref[part, :, PIXELS:] = jnp.where(straight, masses[0], masses[1])
         out1_ref[part, :, PIXELS:] = jnp.where(straight, masses[1], masses[0])
+
+
+def final_kernel(first_ref, second_ref, out_ref):
+    extra = first_ref[0, :, PIXELS:].astype(jnp.float32) + second_ref[0, :, PIXELS:].astype(jnp.float32)
+    mass = jnp.sum(extra, axis=1, keepdims=True)
+    for part in range(2):
+        both = first_ref[part, :, :PIXELS].astype(jnp.float32) + second_ref[part, :, :PIXELS].astype(jnp.float32)
+        out_ref[part] = both / (mass + 1.0)
 
 
 def call(kernel, shapes, args, scratch=(), scalars=0):
@@ -244,19 +273,19 @@
         (swap(cross, BLOCK), *tags, log_prior, half),
         scalars=2,
     )
-    (post,) = call(post_kernel, [((16, 8, 2 * LANES), jnp.float32)], (swap(stats, SPACE), scores))
+    (post,) = call(post_kernel, [((16, 8, 2 * LANES), jnp.bfloat16)], (swap(stats, SPACE), scores))
     posts = swap(post, BLOCK)
     partial = call(
         back_kernel,
-        [((2, 8, PIXELS + LANES), jnp.float32)] * 2,
+        [((2, 8, PIXELS + LANES), jnp.bfloat16)] * 2,
         (posts, units, cosine, sine, half),
         scalars=1,
     )
     first, second = [lax.ppermute(part, ALL, route) for part, route in zip(partial, routes(False), strict=True)]
-    both = first + second
-    new_refs = both[:, :, :PIXELS] / (both[:, :, PIXELS : PIXELS + 1] + 1.0)
-    mine = lax.dynamic_slice_in_dim(posts, (y * 2 + c) * 2, 2, 0)
-    class_post = mine.reshape(16, 2 * LANES)[:, USED : USED + CLASSES]
+    (new_refs,) = call(final_kernel, [((2, 8, PIXELS), jnp.float32)], (first, second))
+    mine = lax.dynamic_slice_in_dim(posts, (y * 2 + c) * 2, 2, 0).reshape(16, 2 * LANES)
+    shares = mine[:, CLASS : CLASS + 3 * CLASSES].astype(jnp.float32).reshape(16, 3, CLASSES)
+    class_post = jnp.sum(shares, axis=1)
     return new_refs, class_post
 
 

time: 125 us -> 120 us (0.960)
  the two profiles are of different devices: /device:TPU:24 before, /device:TPU:33 now
where the time goes in v3:
time: 120 us
  starting transfers between devices  61.7 us (51%)
  waiting for transfers between devices  36.5 us (30%)
  blocking collectives  11.6 us (10%)
  Pallas kernels  6.19 us (5%)
  local copies, waits for them, and re-layouts  1.68 us (1%)
  other arithmetic  1.24 us (1%)
    all_to_all x3, starting transfers between devices, swap(): return lax.all_to_all(operand, axes, 0, 0, tiled=True)  29.4 us
    all_to_all x3, waiting for transfers between devices, swap(): return lax.all_to_all(operand, axes, 0, 0, tiled=True)  22.2 us
    ppermute x2, starting transfers between devices, local(): refs = [lax.ppermute(low, ALL, route) for route in routes(True)]  19 us
    ppermute x2, starting transfers between devices, local(): lax.ppermute(part, ALL, route)  13.3 us
    ppermute x2, waiting for transfers between devices, local(): lax.ppermute(part, ALL, route)  12.3 us
    all_to_all x1, blocking collectives, swap(): return lax.all_to_all(operand, axes, 0, 0, tiled=True)  11.6 us
    pallas_call x7, Pallas kernels, call(): pl.pallas_call(kernel, out_shape=out, in_specs=in_vmem + in_smem, out_spe...  6.19 us
  transfers between devices with their start and end apart: 7, of which 4 were waited for; matrix products, arithmetic and copies ran while one was open for 1% of the time, Pallas kernels for 0%

profile of v3, /device:TPU:33, one launch (start us, length us, event | category | flops | bytes accessed | tf_op | source)
XLA Modules:
  0.0 119.6 jit_solution(4162786086954806483)
XLA Ops:
  0.6 0.0 copy-start
  0.6 0.9 copy-done
  1.5 0.0 copy-start.2
  1.5 0.7 copy-done.2
  2.2 1.2 shard_map.77
  3.4 0.0 copy-start.1
  3.4 0.0 copy-start.3
  3.4 0.0 copy-start.5
  3.4 6.2 %all-to-all-start = ((bf16[16,2,16,1152]{3,2,1,0:T(8,128)(2,1)}), bf16[16,2,16,1152]{3,2,1,0:T(8,128)(2,1)S(1)}, u32[]{:S(2)}, u32[]{:S(2)}) async-start(bf16[16,2,16,1152]{3,2,1,0:T(8,128)(2,1)} %shard_map.77), calls=%async_computation | async-start | bytes 2359296 | tf_op jit(solution)/shard_map/all_to_all | solution.py:251
  9.6 0.0 copy-done.1
  9.6 0.0 copy-done.3
  9.6 0.1 shard_map.78
  9.7 0.0 copy-start.4
  9.7 4.0 %collective-permute-start = (bf16[2,8,2176]{2,1,0:T(8,128)(2,1)S(1)}, bf16[2,8,2176]{2,1,0:T(8,128)(2,1)S(1)}, u32[]{:S(2)}, u32[]{:S(2)}) collective-permute-start(bf16[2,8,2176]{2,1,0:T(8,128)(2,1)S(1)} %shard_map.78), channel_id=1, source_target_pairs={{0,0},{1,1},{32,2},{33,3},{64,4},{65,5},{96,6},{97,7},{128,8},{129... | collective-permute-start | bytes 208904 | tf_op jit(solution)/shard_map/ppermute | solution.py:260
  13.7 15.0 %collective-permute-start.1 = (bf16[2,8,2176]{2,1,0:T(8,128)(2,1)S(1)}, bf16[2,8,2176]{2,1,0:T(8,128)(2,1)S(1)}, u32[]{:S(2)}, u32[]{:S(2)}) collective-permute-start(bf16[2,8,2176]{2,1,0:T(8,128)(2,1)S(1)} %shard_map.78), channel_id=1, source_target_pairs={{2,0},{3,1},{34,2},{35,3},{66,4},{67,5},{98,6},{99,7},{130,8},{131... | collective-permute-start | bytes 208904 | tf_op jit(solution)/shard_map/ppermute | solution.py:260
  28.7 0.0 copy-done.5
  28.8 0.6 fusion
  29.3 0.0 collective-permute-done.ref0_ref
  29.3 2.0 %collective-permute-done.1.ref1_ref = bf16[2,8,2176]{2,1,0:T(8,128)(2,1)S(1)} collective-permute-done((bf16[2,8,2176]{2,1,0:T(8,128)(2,1)S(1)}, bf16[2,8,2176]{2,1,0:T(8,128)(2,1)S(1)}, u32[]{:S(2)}, u32[]{:S(2)}) %collective-permute-start.1) | collective-permute-done | bytes 69664 | tf_op jit(solution)/shard_map/ppermute | solution.py:260
  31.3 0.0 all-to-all-done
  31.3 1.5 %shard_map.79 = f32[16,8,256]{2,1,0:T(8,128)} custom-call(bf16[8,2,2,16,1152]{4,3,2,1,0:T(8,128)(2,1)S(1)} %bitcast.12, bf16[2,8,2176]{2,1,0:T(8,128)(2,1)S(1)} %collective-permute-done.ref0_ref, bf16[2,8,2176]{2,1,0:T(8,128)(2,1)S(1)} %collective-permute-done.1.ref1_ref, f32[12,2048]{1,0:T(8,128)S(1)} %get-tuple-element.11.cos_ref, ...), custom_call_target="tpu_custom_call" | custom-call | tf_op jit(solution)/shard_map/pallas_call | solution.py:240
  32.9 17.8 %all-to-all-start.1 = ((f32[16,8,256]{2,1,0:T(8,128)}), f32[16,8,256]{2,1,0:T(8,128)S(1)}, u32[]{:S(2)}, u32[]{:S(2)}) async-start(f32[16,8,256]{2,1,0:T(8,128)} %shard_map.79), calls=%async_computation.1 | async-start | bytes 262144 | tf_op jit(solution)/shard_map/all_to_all | solution.py:251
  50.7 11.3 %all-to-all-done.1.got_ref = f32[16,8,256]{2,1,0:T(8,128)S(1)} async-done(((f32[16,8,256]{2,1,0:T(8,128)}), f32[16,8,256]{2,1,0:T(8,128)S(1)}, u32[]{:S(2)}, u32[]{:S(2)}) %all-to-all-start.1) | async-done | bytes 131104 | tf_op jit(solution)/shard_map/all_to_all | solution.py:251
  62.0 0.0 copy-done.4
  62.0 0.7 shard_map.80
  62.7 11.6 %all_to_all.20.got_ref = f32[16,8,128]{2,1,0:T(8,128)S(1)} all-to-all(f32[16,8,128]{2,1,0:T(8,128)S(1)} %get-tuple-element.6), channel_id=1, replica_groups=mesh['y'=4,'zh'=2,'c'=2,'zl'=8,'xh'=2,'xl'=2] {'y','c','xl'}, dimensions={0} | all-to-all | bytes 131072 | tf_op jit(solution)/shard_map/all_to_all | solution.py:251
  74.3 0.9 shard_map.81
  75.2 5.4 %all-to-all-start.3 = ((bf16[16,8,256]{2,1,0:T(8,128)(2,1)}), bf16[16,8,256]{2,1,0:T(8,128)(2,1)S(1)}, u32[]{:S(2)}, u32[]{:S(2)}) async-start(bf16[16,8,256]{2,1,0:T(8,128)(2,1)} %shard_map.81), calls=%async_computation.3 | async-start | bytes 131072 | tf_op jit(solution)/shard_map/all_to_all | solution.py:251
  80.6 10.9 %all-to-all-done.3.got_ref = bf16[16,8,256]{2,1,0:T(8,128)(2,1)S(1)} async-done(((bf16[16,8,256]{2,1,0:T(8,128)(2,1)}), bf16[16,8,256]{2,1,0:T(8,128)(2,1)S(1)}, u32[]{:S(2)}, u32[]{:S(2)}) %all-to-all-start.3) | async-done | bytes 65568 | tf_op jit(solution)/shard_map/all_to_all | solution.py:251
  91.5 1.0 shard_map.82
  92.5 11.1 %collective-permute-start.2 = (bf16[2,8,2176]{2,1,0:T(8,128)(2,1)S(1)}, bf16[2,8,2176]{2,1,0:T(8,128)(2,1)S(1)}, u32[]{:S(2)}, u32[]{:S(2)}) collective-permute-start(bf16[2,8,2176]{2,1,0:T(8,128)(2,1)S(1)} %get-tuple-element.8), channel_id=1, source_target_pairs={{0,0},{1,1},{2,32},{3,33},{4,64},{5,65},{6,96},{7,97},{8,128},{9,1... | collective-permute-start | bytes 208904 | tf_op jit(solution)/shard_map/ppermute | solution.py:284
  103.6 2.2 %collective-permute-start.3 = (bf16[2,8,2176]{2,1,0:T(8,128)(2,1)S(1)}, bf16[2,8,2176]{2,1,0:T(8,128)(2,1)S(1)}, u32[]{:S(2)}, u32[]{:S(2)}) collective-permute-start(bf16[2,8,2176]{2,1,0:T(8,128)(2,1)S(1)} %get-tuple-element.9), channel_id=1, source_target_pairs={{0,2},{1,3},{2,34},{3,35},{4,66},{5,67},{6,98},{7,99},{8,130},{9,1... | collective-permute-start | bytes 208904 | tf_op jit(solution)/shard_map/ppermute | solution.py:284
  105.8 0.1 slice_convert_fusion
  105.9 0.1 copy.8
  106.0 0.6 reduce_sum.9
  106.6 0.0 collective-permute-done.2.first_ref
  106.6 12.3 %collective-permute-done.3.second_ref = bf16[2,8,2176]{2,1,0:T(8,128)(2,1)S(1)} collective-permute-done((bf16[2,8,2176]{2,1,0:T(8,128)(2,1)S(1)}, bf16[2,8,2176]{2,1,0:T(8,128)(2,1)S(1)}, u32[]{:S(2)}, u32[]{:S(2)}) %collective-permute-start.3) | collective-permute-done | bytes 69664 | tf_op jit(solution)/shard_map/ppermute | solution.py:284
  118.8 0.8 shard_map.83
  (6 shorter events, 0.0 us)
Async XLA Ops:
  0.6 0.9 copy-start
  1.5 0.7 copy-start.2
  3.4 6.2 %copy-start.1 = (f32[2,8,2048]{2,1,0:T(8,128)S(1)}, f32[2,8,2048]{2,1,0:T(8,128)}, u32[]{:S(2)}) copy-start(f32[2,8,2048]{2,1,0:T(8,128)} %ref_ref.1) | copy-start | bytes 393220
  3.4 6.2 %copy-start.3 = (s32[8]{0:T(128)S(1)}, s32[8]{0:T(128)}, u32[]{:S(2)}) copy-start(s32[8]{0:T(128)} %param.10) | copy-start | bytes 100
  3.4 25.4 %copy-start.5 = (s32[12,2]{0,1:T(2,128)S(1)}, s32[12,2]{0,1:T(2,128)}, u32[]{:S(2)}) copy-start(s32[12,2]{0,1:T(2,128)} %param.9) | copy-start | bytes 292
  3.4 28.0 %all-to-all-start = ((bf16[16,2,16,1152]{3,2,1,0:T(8,128)(2,1)}), bf16[16,2,16,1152]{3,2,1,0:T(8,128)(2,1)S(1)}, u32[]{:S(2)}, u32[]{:S(2)}) async-start(bf16[16,2,16,1152]{3,2,1,0:T(8,128)(2,1)} %shard_map.77), calls=%async_computation | async-start | bytes 2359296 | tf_op jit(solution)/shard_map/all_to_all | solution.py:251
  9.7 52.3 %copy-start.4 = (f32[4]{0:T(128)S(1)}, f32[4]{0:T(128)}, u32[]{:S(2)}) copy-start(f32[4]{0:T(128)} %prior_ref.1) | copy-start | bytes 52
  9.7 19.6 %collective-permute-start = (bf16[2,8,2176]{2,1,0:T(8,128)(2,1)S(1)}, bf16[2,8,2176]{2,1,0:T(8,128)(2,1)S(1)}, u32[]{:S(2)}, u32[]{:S(2)}) collective-permute-start(bf16[2,8,2176]{2,1,0:T(8,128)(2,1)S(1)} %shard_map.78), channel_id=1, source_target_pairs={{0,0},{1,1},{32,2},{33,3},{64,4},{65,5},{96,6},{97,7},{128,8},{129... | collective-permute-start | bytes 208904 | tf_op jit(solution)/shard_map/ppermute | solution.py:260
  13.7 17.6 %collective-permute-start.1 = (bf16[2,8,2176]{2,1,0:T(8,128)(2,1)S(1)}, bf16[2,8,2176]{2,1,0:T(8,128)(2,1)S(1)}, u32[]{:S(2)}, u32[]{:S(2)}) collective-permute-start(bf16[2,8,2176]{2,1,0:T(8,128)(2,1)S(1)} %shard_map.78), channel_id=1, source_target_pairs={{2,0},{3,1},{34,2},{35,3},{66,4},{67,5},{98,6},{99,7},{130,8},{131... | collective-permute-start | bytes 208904 | tf_op jit(solution)/shard_map/ppermute | solution.py:260
  32.9 29.1 %all-to-all-start.1 = ((f32[16,8,256]{2,1,0:T(8,128)}), f32[16,8,256]{2,1,0:T(8,128)S(1)}, u32[]{:S(2)}, u32[]{:S(2)}) async-start(f32[16,8,256]{2,1,0:T(8,128)} %shard_map.79), calls=%async_computation.1 | async-start | bytes 262144 | tf_op jit(solution)/shard_map/all_to_all | solution.py:251
  75.2 16.3 %all-to-all-start.3 = ((bf16[16,8,256]{2,1,0:T(8,128)(2,1)}), bf16[16,8,256]{2,1,0:T(8,128)(2,1)S(1)}, u32[]{:S(2)}, u32[]{:S(2)}) async-start(bf16[16,8,256]{2,1,0:T(8,128)(2,1)} %shard_map.81), calls=%async_computation.3 | async-start | bytes 131072 | tf_op jit(solution)/shard_map/all_to_all | solution.py:251
  92.5 14.1 %collective-permute-start.2 = (bf16[2,8,2176]{2,1,0:T(8,128)(2,1)S(1)}, bf16[2,8,2176]{2,1,0:T(8,128)(2,1)S(1)}, u32[]{:S(2)}, u32[]{:S(2)}) collective-permute-start(bf16[2,8,2176]{2,1,0:T(8,128)(2,1)S(1)} %get-tuple-element.8), channel_id=1, source_target_pairs={{0,0},{1,1},{2,32},{3,33},{4,64},{5,65},{6,96},{7,97},{8,128},{9,1... | collective-permute-start | bytes 208904 | tf_op jit(solution)/shard_map/ppermute | solution.py:284
  103.6 15.3 %collective-permute-start.3 = (bf16[2,8,2176]{2,1,0:T(8,128)(2,1)S(1)}, bf16[2,8,2176]{2,1,0:T(8,128)(2,1)S(1)}, u32[]{:S(2)}, u32[]{:S(2)}) collective-permute-start(bf16[2,8,2176]{2,1,0:T(8,128)(2,1)S(1)} %get-tuple-element.9), channel_id=1, source_target_pairs={{0,2},{1,3},{2,34},{3,35},{4,66},{5,67},{6,98},{7,99},{8,130},{9,1... | collective-permute-start | bytes 208904 | tf_op jit(solution)/shard_map/ppermute | solution.py:284

commit v4 on v3

--- a/solution.py
+++ b/solution.py
@@ -99,15 +99,16 @@
     out_ref[1, :, PIXELS:] = label
 
 
-def cross_kernel(img_ref, ref0_ref, ref1_ref, cos_ref, sin_ref, zh_ref, out_ref, shifted):
+def rotate_kernel(ref0_ref, ref1_ref, cos_ref, sin_ref, zh_ref, shifted, half_ref, label_ref):
     straight = zh_ref[0] == 0
-    ref0 = ref0_ref[:, :, :PIXELS].astype(jnp.float32)
-    ref1 = ref1_ref[:, :, :PIXELS].astype(jnp.float32)
-    halves = []
+    ref0 = ref0_ref[...].astype(jnp.float32)
+    ref1 = ref1_ref[...].astype(jnp.float32)
     for e in range(2):
         ref = jnp.where(straight, ref0, ref1) if e == 0 else jnp.where(straight, ref1, ref0)
-        re, im = ref[0], ref[1]
-        halves.append(as_row(0.5 * jnp.sum(re * re + im * im, axis=1, keepdims=True)))
+        re, im = ref[0, :, :PIXELS], ref[1, :, :PIXELS]
+        label_ref[:, e * LANES : (e + 1) * LANES] = as_row(ref[0, :, PIXELS:])
+        energy = jnp.sum(re * re + im * im, axis=1, keepdims=True)
+        half_ref[:, e * LANES : (e + 1) * LANES] = as_row(0.5 * energy)
         for pair in range(SHIFTS // 2):
             rot_re, rot_im = [], []
             for t in (2 * pair, 2 * pair + 1):
@@ -119,6 +120,9 @@
             shifted[1, rows, :] = jnp.concatenate(rot_im, axis=0).astype(jnp.bfloat16)
         spare = slice(e * LANES + USED, (e + 1) * LANES)
         shifted[:, spare, :] = jnp.zeros((2, LANES - USED, PIXELS), jnp.bfloat16)
+
+
+def cross_kernel(img_ref, shifted, half_ref, out_ref):
     total = jnp.zeros((128, 2 * LANES), jnp.float32)
     for h in range(2):
         for part in range(2):
@@ -130,19 +134,11 @@
             )
     pieces = img_ref[:, 0, 0, :, HALF:].reshape(128, LANES).astype(jnp.float32)
     precision = jnp.sum(pieces, axis=1, keepdims=True)
-    scaled = precision * (total - jnp.concatenate(halves, axis=1))
-    out_ref[...] = scaled.reshape(16, 8, 2 * LANES)
-
-
-def label_rows(ref0_ref, ref1_ref, straight):
-    first = ref0_ref[0].astype(jnp.float32)
-    second = ref1_ref[0].astype(jnp.float32)
-    low, high = jnp.where(straight, first, second), jnp.where(straight, second, first)
-    return jnp.concatenate([as_row(low), as_row(high)], axis=1)
-
-
-def score_kernel(got_ref, ref0_ref, ref1_ref, prior_ref, zh_ref, score_ref, out_ref):
-    labels = label_rows(ref0_ref, ref1_ref, zh_ref[0] == 0)
+    out_ref[...] = (precision * (total - half_ref[...])).reshape(16, 8, 2 * LANES)
+
+
+def score_kernel(got_ref, label_ref, prior_ref, score_ref, out_ref):
+    labels = label_ref[...]
     prior = jnp.zeros((1, 2 * LANES), jnp.float32)
     for k in range(CLASSES):
         prior = jnp.where(labels == k, prior_ref[k], prior)
@@ -233,7 +229,7 @@
         out_ref[part] = both / (mass + 1.0)
 
 
-def call(kernel, shapes, args, scratch=(), scalars=0):
+def call(kernel, shapes, args, scratch=(), scalars=0, cost=None):
     in_vmem = [pl.BlockSpec(memory_space=pltpu.VMEM)] * (len(args) - scalars)
     in_smem = [pl.BlockSpec(memory_space=pltpu.SMEM)] * scalars
     out = [jax.ShapeDtypeStruct(shape, dtype) for shape, dtype in shapes]
@@ -243,7 +239,8 @@
         in_specs=in_vmem + in_smem,
         out_specs=[pl.BlockSpec(memory_space=pltpu.VMEM)] * len(out),
         scratch_shapes=list(scratch),
-        compiler_params=pltpu.CompilerParams(vmem_limit_bytes=32 << 20),
+        compiler_params=pltpu.CompilerParams(vmem_limit_bytes=8 << 20),
+        cost_estimate=cost,
     )(*args)
 
 
@@ -254,24 +251,24 @@
 def local(images, references, precision, shifts, labels, log_prior):
     y, zh, c, zl, xh, xl = (lax.axis_index(name) for name in ALL)
     half = zh.astype(jnp.int32)[None]
+    (low,) = call(ref_kernel, [((2, 8, PIXELS + LANES), jnp.bfloat16)], (references, labels[None]))
+    refs = [lax.ppermute(low, ALL, route) for route in routes(True)]
     (sent,) = call(image_kernel, [((16, 2, 16, HALF + LANES), jnp.bfloat16)], (images, precision[None]))
     units = swap(sent, SPACE).reshape(8, 2, 2, 16, HALF + LANES)
-    (low,) = call(ref_kernel, [((2, 8, PIXELS + LANES), jnp.bfloat16)], (references, labels[None]))
-    refs = [lax.ppermute(low, ALL, route) for route in routes(True)]
-    tags = [ref[:1, :, PIXELS:] for ref in refs]
     cosine, sine = phases(shifts, zl * 2 + xh)
-    (cross,) = call(
-        cross_kernel,
-        [((16, 8, 2 * LANES), jnp.float32)],
-        (units, *refs, cosine, sine, half),
-        [pltpu.VMEM((2, 2 * LANES, PIXELS), jnp.bfloat16)],
+    shifted, energies, tags = call(
+        rotate_kernel,
+        [((2, 2 * LANES, PIXELS), jnp.bfloat16), ((1, 2 * LANES), jnp.float32), ((1, 2 * LANES), jnp.float32)],
+        (*refs, cosine, sine, half),
         scalars=1,
-    )
+        cost=pl.CostEstimate(flops=60_000_000_000, transcendentals=0, bytes_accessed=8 << 20),
+    )
+    (cross,) = call(cross_kernel, [((16, 8, 2 * LANES), jnp.float32)], (units, shifted, energies))
     scores, stats = call(
         score_kernel,
         [((8, 2 * LANES), jnp.float32), ((16, 8, LANES), jnp.float32)],
-        (swap(cross, BLOCK), *tags, log_prior, half),
-        scalars=2,
+        (swap(cross, BLOCK), tags, log_prior),
+        scalars=1,
     )
     (post,) = call(post_kernel, [((16, 8, 2 * LANES), jnp.bfloat16)], (swap(stats, SPACE), scores))
     posts = swap(post, BLOCK)

time: 120 us -> 125 us (1.042)
  blocking collectives: 11.6 us -> 30.5 us
  starting transfers between devices: 61.7 us -> 44.2 us
  local copies, waits for them, and re-layouts: 1.68 us -> 6.23 us
    all_to_all x1 -> x2, blocking collectives: 11.6 us -> 30.5 us  [swap(): return lax.all_to_all(operand, axes, 0, 0, tiled=True)]
    all_to_all x3 -> x2, starting transfers between devices: 29.4 us -> 13.9 us  [swap(): return lax.all_to_all(operand, axes, 0, 0, tiled=True)]
    unnamed x12 -> x20, local copies, waits for them, and re-layouts: 1.57 us -> 6.12 us
    ppermute x2, waiting for transfers between devices: 2 us -> 0.19 us  [local(): refs = [lax.ppermute(low, ALL, route) for route in routes(True)]]
    ppermute x2, starting transfers between devices: 13.3 us -> 11.8 us  [local(): lax.ppermute(part, ALL, route)]
    all_to_all x3 -> x2, waiting for transfers between devices: 22.2 us -> 23 us  [swap(): return lax.all_to_all(operand, axes, 0, 0, tiled=True)]
    pallas_call x7 -> x8, Pallas kernels: 6.19 us -> 6.19 us  [call(): pl.pallas_call(kernel, out_shape=out, in_specs=in_vmem + in_smem, out_spe...]
  transfers between devices with their start and end apart: 7 -> 6, of which waited for: 4 -> 4; matrix products, arithmetic and copies ran while one was open for 1% -> 1% of each run, Pallas kernels for 0% -> 2%
where the time goes in v4:
time: 125 us
  starting transfers between devices  44.2 us (35%)
  waiting for transfers between devices  35.5 us (28%)
  blocking collectives  30.5 us (24%)
  local copies, waits for them, and re-layouts  6.23 us (5%)
  Pallas kernels  6.19 us (5%)
    all_to_all x2, blocking collectives, swap(): return lax.all_to_all(operand, axes, 0, 0, tiled=True)  30.5 us
    all_to_all x2, waiting for transfers between devices, swap(): return lax.all_to_all(operand, axes, 0, 0, tiled=True)  23 us
    ppermute x2, starting transfers between devices, local(): refs = [lax.ppermute(low, ALL, route) for route in routes(True)]  18.5 us
    all_to_all x2, starting transfers between devices, swap(): return lax.all_to_all(operand, axes, 0, 0, tiled=True)  13.9 us
    ppermute x2, waiting for transfers between devices, local(): lax.ppermute(part, ALL, route)  12.3 us
    ppermute x2, starting transfers between devices, local(): lax.ppermute(part, ALL, route)  11.8 us
    pallas_call x8, Pallas kernels, call(): pl.pallas_call(kernel, out_shape=out, in_specs=in_vmem + in_smem, out_spe...  6.19 us
    unnamed x20, local copies, waits for them, and re-layouts  6.12 us
  transfers between devices with their start and end apart: 6, of which 4 were waited for; matrix products, arithmetic and copies ran while one was open for 1% of the time, Pallas kernels for 2%

profile of v4, /device:TPU:33, one launch (start us, length us, event | category | flops | bytes accessed | tf_op | source)
XLA Modules:
  0.0 124.6 jit_solution(1959428211045215124)
XLA Ops:
  0.6 0.0 copy-start.1
  0.6 0.9 copy-done.1
  1.5 0.0 copy-start.2
  1.5 0.7 copy-done.2
  2.2 0.1 shard_map.78
  2.3 16.5 %collective-permute-start.1 = (bf16[2,8,2176]{2,1,0:T(8,128)(2,1)S(1)}, bf16[2,8,2176]{2,1,0:T(8,128)(2,1)S(1)}, u32[]{:S(2)}, u32[]{:S(2)}) collective-permute-start(bf16[2,8,2176]{2,1,0:T(8,128)(2,1)S(1)} %shard_map.78), channel_id=1, source_target_pairs={{2,0},{3,1},{34,2},{35,3},{66,4},{67,5},{98,6},{99,7},{130,8},{131... | collective-permute-start | bytes 208904 | tf_op jit(solution)/shard_map/ppermute | solution.py:255
  18.8 1.9 %collective-permute-start = (bf16[2,8,2176]{2,1,0:T(8,128)(2,1)S(1)}, bf16[2,8,2176]{2,1,0:T(8,128)(2,1)S(1)}, u32[]{:S(2)}, u32[]{:S(2)}) collective-permute-start(bf16[2,8,2176]{2,1,0:T(8,128)(2,1)S(1)} %shard_map.78), channel_id=1, source_target_pairs={{0,0},{1,1},{32,2},{33,3},{64,4},{65,5},{96,6},{97,7},{128,8},{129... | collective-permute-start | bytes 208904 | tf_op jit(solution)/shard_map/ppermute | solution.py:255
  20.7 0.0 copy-start
  20.8 0.9 copy-done
  21.7 0.0 copy-start.3
  21.7 0.7 copy-done.3
  22.3 1.1 shard_map.77
  23.5 0.0 copy-start.9
  23.5 8.3 %all-to-all-start = ((bf16[16,2,16,1152]{3,2,1,0:T(8,128)(2,1)}), bf16[16,2,16,1152]{3,2,1,0:T(8,128)(2,1)S(1)}, u32[]{:S(2)}, u32[]{:S(2)}) async-start(bf16[16,2,16,1152]{3,2,1,0:T(8,128)(2,1)} %shard_map.77), calls=%async_computation | async-start | bytes 2359296 | tf_op jit(solution)/shard_map/all_to_all | solution.py:248
  31.7 0.0 copy-done.9
  31.8 0.6 fusion
  32.3 0.0 collective-permute-done.1.ref1_ref
  32.3 0.0 copy-start.5
  32.4 0.6 copy-done.5
  33.0 0.2 collective-permute-done.ref0_ref
  33.2 0.0 copy-start.7
  33.2 0.6 copy-done.7
  33.8 0.0 copy-start.6
  33.8 0.9 copy-done.6
  34.7 0.0 copy-start.8
  34.7 0.9 copy-done.8
  35.6 0.7 shard_map.79
  36.3 12.1 %all-to-all-done = bf16[16,2,16,1152]{3,2,1,0:T(8,128)(2,1)S(1)} async-done(((bf16[16,2,16,1152]{3,2,1,0:T(8,128)(2,1)}), bf16[16,2,16,1152]{3,2,1,0:T(8,128)(2,1)S(1)}, u32[]{:S(2)}, u32[]{:S(2)}) %all-to-all-start) | async-done | bytes 1179680 | tf_op jit(solution)/shard_map/all_to_all | solution.py:248
  48.4 0.0 copy-start.4
  48.4 0.8 shard_map.80
  49.3 19.7 %all_to_all.20.got_ref = f32[16,8,256]{2,1,0:T(8,128)S(1)} all-to-all(f32[16,8,256]{2,1,0:T(8,128)S(1)} %shard_map.80), channel_id=1, replica_groups=mesh['y'=4,'zh'=2,'c'=2,'zl'=8,'xh'=2,'xl'=2] {'zl','xh'}, dimensions={0} | all-to-all | bytes 262144 | tf_op jit(solution)/shard_map/all_to_all | solution.py:248
  68.9 0.0 copy-done.4
  68.9 0.7 shard_map.81
  69.7 10.8 %all_to_all.21.got_ref = f32[16,8,128]{2,1,0:T(8,128)S(1)} all-to-all(f32[16,8,128]{2,1,0:T(8,128)S(1)} %get-tuple-element.12), channel_id=1, replica_groups=mesh['y'=4,'zh'=2,'c'=2,'zl'=8,'xh'=2,'xl'=2] {'y','c','xl'}, dimensions={0} | all-to-all | bytes 131072 | tf_op jit(solution)/shard_map/all_to_all | solution.py:248
  80.5 0.9 shard_map.82
  81.4 5.6 %all-to-all-start.3 = ((bf16[16,8,256]{2,1,0:T(8,128)(2,1)}), bf16[16,8,256]{2,1,0:T(8,128)(2,1)S(1)}, u32[]{:S(2)}, u32[]{:S(2)}) async-start(bf16[16,8,256]{2,1,0:T(8,128)(2,1)} %shard_map.82), calls=%async_computation.3 | async-start | bytes 131072 | tf_op jit(solution)/shard_map/all_to_all | solution.py:248
  87.0 10.9 %all-to-all-done.3.got_ref = bf16[16,8,256]{2,1,0:T(8,128)(2,1)S(1)} async-done(((bf16[16,8,256]{2,1,0:T(8,128)(2,1)}), bf16[16,8,256]{2,1,0:T(8,128)(2,1)S(1)}, u32[]{:S(2)}, u32[]{:S(2)}) %all-to-all-start.3) | async-done | bytes 65568 | tf_op jit(solution)/shard_map/all_to_all | solution.py:248
  97.9 1.0 shard_map.83
  98.9 9.6 %collective-permute-start.2 = (bf16[2,8,2176]{2,1,0:T(8,128)(2,1)S(1)}, bf16[2,8,2176]{2,1,0:T(8,128)(2,1)S(1)}, u32[]{:S(2)}, u32[]{:S(2)}) collective-permute-start(bf16[2,8,2176]{2,1,0:T(8,128)(2,1)S(1)} %get-tuple-element.14), channel_id=1, source_target_pairs={{0,0},{1,1},{2,32},{3,33},{4,64},{5,65},{6,96},{7,97},{8,128},{9,1... | collective-permute-start | bytes 208904 | tf_op jit(solution)/shard_map/ppermute | solution.py:281
  108.6 2.2 %collective-permute-start.3 = (bf16[2,8,2176]{2,1,0:T(8,128)(2,1)S(1)}, bf16[2,8,2176]{2,1,0:T(8,128)(2,1)S(1)}, u32[]{:S(2)}, u32[]{:S(2)}) collective-permute-start(bf16[2,8,2176]{2,1,0:T(8,128)(2,1)S(1)} %get-tuple-element.15), channel_id=1, source_target_pairs={{0,2},{1,3},{2,34},{3,35},{4,66},{5,67},{6,98},{7,99},{8,130},{9,1... | collective-permute-start | bytes 208904 | tf_op jit(solution)/shard_map/ppermute | solution.py:281
  110.8 0.1 slice_convert_fusion
  110.9 0.1 copy.8
  111.0 0.6 reduce_sum.9
  111.6 0.0 collective-permute-done.2.first_ref
  111.6 12.3 %collective-permute-done.3.second_ref = bf16[2,8,2176]{2,1,0:T(8,128)(2,1)S(1)} collective-permute-done((bf16[2,8,2176]{2,1,0:T(8,128)(2,1)S(1)}, bf16[2,8,2176]{2,1,0:T(8,128)(2,1)S(1)}, u32[]{:S(2)}, u32[]{:S(2)}) %collective-permute-start.3) | collective-permute-done | bytes 69664 | tf_op jit(solution)/shard_map/ppermute | solution.py:281
  123.8 0.8 shard_map.84
  (4 shorter events, 0.0 us)
Async XLA Ops:
  0.6 0.9 copy-start.1
  1.5 0.7 copy-start.2
  2.3 30.1 %collective-permute-start.1 = (bf16[2,8,2176]{2,1,0:T(8,128)(2,1)S(1)}, bf16[2,8,2176]{2,1,0:T(8,128)(2,1)S(1)}, u32[]{:S(2)}, u32[]{:S(2)}) collective-permute-start(bf16[2,8,2176]{2,1,0:T(8,128)(2,1)S(1)} %shard_map.78), channel_id=1, source_target_pairs={{2,0},{3,1},{34,2},{35,3},{66,4},{67,5},{98,6},{99,7},{130,8},{131... | collective-permute-start | bytes 208904 | tf_op jit(solution)/shard_map/ppermute | solution.py:255
  18.8 14.3 %collective-permute-start = (bf16[2,8,2176]{2,1,0:T(8,128)(2,1)S(1)}, bf16[2,8,2176]{2,1,0:T(8,128)(2,1)S(1)}, u32[]{:S(2)}, u32[]{:S(2)}) collective-permute-start(bf16[2,8,2176]{2,1,0:T(8,128)(2,1)S(1)} %shard_map.78), channel_id=1, source_target_pairs={{0,0},{1,1},{32,2},{33,3},{64,4},{65,5},{96,6},{97,7},{128,8},{129... | collective-permute-start | bytes 208904 | tf_op jit(solution)/shard_map/ppermute | solution.py:255
  20.7 0.9 copy-start
  21.7 0.7 copy-start.3
  23.5 8.3 %copy-start.9 = (s32[12,2]{0,1:T(2,128)S(1)}, s32[12,2]{0,1:T(2,128)}, u32[]{:S(2)}) copy-start(s32[12,2]{0,1:T(2,128)} %param.9) | copy-start | bytes 292
  23.5 25.0 %all-to-all-start = ((bf16[16,2,16,1152]{3,2,1,0:T(8,128)(2,1)}), bf16[16,2,16,1152]{3,2,1,0:T(8,128)(2,1)S(1)}, u32[]{:S(2)}, u32[]{:S(2)}) async-start(bf16[16,2,16,1152]{3,2,1,0:T(8,128)(2,1)} %shard_map.77), calls=%async_computation | async-start | bytes 2359296 | tf_op jit(solution)/shard_map/all_to_all | solution.py:248
  32.3 0.6 copy-start.5
  33.2 0.6 copy-start.7
  33.8 0.9 copy-start.6
  34.7 0.9 copy-start.8
  48.4 20.5 %copy-start.4 = (f32[4]{0:T(128)S(1)}, f32[4]{0:T(128)}, u32[]{:S(2)}) copy-start(f32[4]{0:T(128)} %prior_ref.1) | copy-start | bytes 52
  81.4 16.5 %all-to-all-start.3 = ((bf16[16,8,256]{2,1,0:T(8,128)(2,1)}), bf16[16,8,256]{2,1,0:T(8,128)(2,1)S(1)}, u32[]{:S(2)}, u32[]{:S(2)}) async-start(bf16[16,8,256]{2,1,0:T(8,128)(2,1)} %shard_map.82), calls=%async_computation.3 | async-start | bytes 131072 | tf_op jit(solution)/shard_map/all_to_all | solution.py:248
  98.9 12.6 %collective-permute-start.2 = (bf16[2,8,2176]{2,1,0:T(8,128)(2,1)S(1)}, bf16[2,8,2176]{2,1,0:T(8,128)(2,1)S(1)}, u32[]{:S(2)}, u32[]{:S(2)}) collective-permute-start(bf16[2,8,2176]{2,1,0:T(8,128)(2,1)S(1)} %get-tuple-element.14), channel_id=1, source_target_pairs={{0,0},{1,1},{2,32},{3,33},{4,64},{5,65},{6,96},{7,97},{8,128},{9,1... | collective-permute-start | bytes 208904 | tf_op jit(solution)/shard_map/ppermute | solution.py:281
  108.6 15.3 %collective-permute-start.3 = (bf16[2,8,2176]{2,1,0:T(8,128)(2,1)S(1)}, bf16[2,8,2176]{2,1,0:T(8,128)(2,1)S(1)}, u32[]{:S(2)}, u32[]{:S(2)}) collective-permute-start(bf16[2,8,2176]{2,1,0:T(8,128)(2,1)S(1)} %get-tuple-element.15), channel_id=1, source_target_pairs={{0,2},{1,3},{2,34},{3,35},{4,66},{5,67},{6,98},{7,99},{8,130},{9,1... | collective-permute-start | bytes 208904 | tf_op jit(solution)/shard_map/ppermute | solution.py:281

commit v5 on v3

--- a/solution.py
+++ b/solution.py
@@ -99,10 +99,10 @@
     out_ref[1, :, PIXELS:] = label
 
 
-def cross_kernel(img_ref, ref0_ref, ref1_ref, cos_ref, sin_ref, zh_ref, out_ref, shifted):
+def cross_kernel(img_ref, ref_ref, cos_ref, sin_ref, zh_ref, out_ref, shifted):
     straight = zh_ref[0] == 0
-    ref0 = ref0_ref[:, :, :PIXELS].astype(jnp.float32)
-    ref1 = ref1_ref[:, :, :PIXELS].astype(jnp.float32)
+    ref0 = ref_ref[0, :, :, :PIXELS].astype(jnp.float32)
+    ref1 = ref_ref[1, :, :, :PIXELS].astype(jnp.float32)
     halves = []
     for e in range(2):
         ref = jnp.where(straight, ref0, ref1) if e == 0 else jnp.where(straight, ref1, ref0)
@@ -134,15 +134,15 @@
     out_ref[...] = scaled.reshape(16, 8, 2 * LANES)
 
 
-def label_rows(ref0_ref, ref1_ref, straight):
-    first = ref0_ref[0].astype(jnp.float32)
-    second = ref1_ref[0].astype(jnp.float32)
+def label_rows(tag_ref, straight):
+    first = tag_ref[0, 0].astype(jnp.float32)
+    second = tag_ref[1, 0].astype(jnp.float32)
     low, high = jnp.where(straight, first, second), jnp.where(straight, second, first)
     return jnp.concatenate([as_row(low), as_row(high)], axis=1)
 
 
-def score_kernel(got_ref, ref0_ref, ref1_ref, prior_ref, zh_ref, score_ref, out_ref):
-    labels = label_rows(ref0_ref, ref1_ref, zh_ref[0] == 0)
+def score_kernel(got_ref, tag_ref, prior_ref, zh_ref, score_ref, out_ref):
+    labels = label_rows(tag_ref, zh_ref[0] == 0)
     prior = jnp.zeros((1, 2 * LANES), jnp.float32)
     for k in range(CLASSES):
         prior = jnp.where(labels == k, prior_ref[k], prior)
@@ -257,20 +257,21 @@
     (sent,) = call(image_kernel, [((16, 2, 16, HALF + LANES), jnp.bfloat16)], (images, precision[None]))
     units = swap(sent, SPACE).reshape(8, 2, 2, 16, HALF + LANES)
     (low,) = call(ref_kernel, [((2, 8, PIXELS + LANES), jnp.bfloat16)], (references, labels[None]))
-    refs = [lax.ppermute(low, ALL, route) for route in routes(True)]
-    tags = [ref[:1, :, PIXELS:] for ref in refs]
+    other = lax.ppermute(low, "xh", [(0, 1), (1, 0)])
+    refs = lax.ppermute(jnp.stack([low, other]), ALL, routes(True)[0])
+    tags = refs[:, :1, :, PIXELS:]
     cosine, sine = phases(shifts, zl * 2 + xh)
     (cross,) = call(
         cross_kernel,
         [((16, 8, 2 * LANES), jnp.float32)],
-        (units, *refs, cosine, sine, half),
+        (units, refs, cosine, sine, half),
         [pltpu.VMEM((2, 2 * LANES, PIXELS), jnp.bfloat16)],
         scalars=1,
     )
     scores, stats = call(
         score_kernel,
         [((8, 2 * LANES), jnp.float32), ((16, 8, LANES), jnp.float32)],
-        (swap(cross, BLOCK), *tags, log_prior, half),
+        (swap(cross, BLOCK), tags, log_prior, half),
         scalars=2,
     )
     (post,) = call(post_kernel, [((16, 8, 2 * LANES), jnp.bfloat16)], (swap(stats, SPACE), scores))

time: 120 us -> 142 us (1.18)
  waiting for transfers between devices: 36.5 us -> 61.5 us
  starting transfers between devices: 61.7 us -> 57 us
    ppermute x2, waiting for transfers between devices: 2 us -> 27.1 us  [the longest x1 13.7 us: local(): other = lax.ppermute(low, 'xh', [(0, 1), (1, 0)])]
    ppermute x2, starting transfers between devices: 19 us -> 9.56 us  [the longest x1 5.19 us: local(): refs = lax.ppermute(jnp.stack([low, other]), ALL, routes(True)[0])]
    all_to_all x3, starting transfers between devices: 29.4 us -> 35.9 us  [swap(): return lax.all_to_all(operand, axes, 0, 0, tiled=True)]
    ppermute x2, starting transfers between devices: 13.3 us -> 11.6 us  [local(): lax.ppermute(part, ALL, route)]
    all_to_all x1, blocking collectives: 11.6 us -> 13 us  [swap(): return lax.all_to_all(operand, axes, 0, 0, tiled=True)]
  transfers between devices with their start and end apart: 7 -> 7, of which waited for: 4 -> 5; matrix products, arithmetic and copies ran while one was open for 1% -> 1% of each run, Pallas kernels for 0% -> 0%
where the time goes in v5:
time: 142 us; the launch traced here: 141 us
  waiting for transfers between devices  61.5 us (43%)
  starting transfers between devices  57 us (40%)
  blocking collectives  13 us (9%)
  Pallas kernels  6.19 us (4%)
  local copies, waits for them, and re-layouts  1.68 us (1%)
    all_to_all x3, starting transfers between devices, swap(): return lax.all_to_all(operand, axes, 0, 0, tiled=True)  35.9 us
    all_to_all x3, waiting for transfers between devices, swap(): return lax.all_to_all(operand, axes, 0, 0, tiled=True)  22.1 us
    ppermute x1, waiting for transfers between devices, local(): other = lax.ppermute(low, 'xh', [(0, 1), (1, 0)])  13.7 us
    ppermute x1, waiting for transfers between devices, local(): refs = lax.ppermute(jnp.stack([low, other]), ALL, routes(True)[0])  13.4 us
    all_to_all x1, blocking collectives, swap(): return lax.all_to_all(operand, axes, 0, 0, tiled=True)  13 us
    ppermute x2, waiting for transfers between devices, local(): lax.ppermute(part, ALL, route)  12.3 us
    ppermute x2, starting transfers between devices, local(): lax.ppermute(part, ALL, route)  11.6 us
    pallas_call x7, Pallas kernels, call(): pl.pallas_call(kernel, out_shape=out, in_specs=in_vmem + in_smem, out_spe...  6.19 us
  transfers between devices with their start and end apart: 7, of which 5 were waited for; matrix products, arithmetic and copies ran while one was open for 1% of the time, Pallas kernels for 0%

profile of v5, /device:TPU:33, one launch (start us, length us, event | category | flops | bytes accessed | tf_op | source)
XLA Modules:
  0.0 141.4 jit_solution(4086137327197865196)
XLA Ops:
  0.6 0.0 copy-start
  0.6 0.9 copy-done
  1.5 0.0 copy-start.2
  1.5 0.7 copy-done.2
  2.2 1.2 shard_map.77
  3.4 0.0 copy-start.1
  3.4 0.0 copy-start.3
  3.4 0.0 copy-start.5
  3.4 6.2 %all-to-all-start = ((bf16[16,2,16,1152]{3,2,1,0:T(8,128)(2,1)}), bf16[16,2,16,1152]{3,2,1,0:T(8,128)(2,1)S(1)}, u32[]{:S(2)}, u32[]{:S(2)}) async-start(bf16[16,2,16,1152]{3,2,1,0:T(8,128)(2,1)} %shard_map.77), calls=%async_computation | async-start | bytes 2359296 | tf_op jit(solution)/shard_map/all_to_all | solution.py:251
  9.6 0.0 copy-done.1
  9.6 0.0 copy-done.3
  9.6 0.1 shard_map.78
  9.7 4.4 %collective-permute-start = (bf16[2,8,2176]{2,1,0:T(8,128)(2,1)S(1)}, bf16[2,8,2176]{2,1,0:T(8,128)(2,1)S(1)}, u32[]{:S(2)}, u32[]{:S(2)}) collective-permute-start(bf16[2,8,2176]{2,1,0:T(8,128)(2,1)S(1)} %shard_map.78), channel_id=1, source_target_pairs={{0,2},{2,0},{1,3},{3,1},{4,6},{6,4},{5,7},{7,5},{8,10},{10,8},{9,1... | collective-permute-start | bytes 208904 | tf_op jit(solution)/shard_map/ppermute | solution.py:260
  14.1 0.0 copy-done.5
  14.1 13.7 %collective-permute-done = bf16[2,8,2176]{2,1,0:T(8,128)(2,1)S(1)} collective-permute-done((bf16[2,8,2176]{2,1,0:T(8,128)(2,1)S(1)}, bf16[2,8,2176]{2,1,0:T(8,128)(2,1)S(1)}, u32[]{:S(2)}, u32[]{:S(2)}) %collective-permute-start) | collective-permute-done | bytes 69664 | tf_op jit(solution)/shard_map/ppermute | solution.py:260
  27.8 0.0 copy-start.4
  27.8 5.2 %collective-permute-start.1 = (bf16[2,2,8,2176]{3,2,1,0:T(8,128)(2,1)S(1)}, bf16[2,2,8,2176]{3,2,1,0:T(8,128)(2,1)S(1)}, u32[]{:S(2)}, u32[]{:S(2)}) collective-permute-start(bf16[2,2,8,2176]{3,2,1,0:T(8,128)(2,1)S(1)} %pad_maximum_fusion), channel_id=1, source_target_pairs={{0,0},{1,1},{32,2},{33,3},{64,4},{65,5},{96,6},{97,7},{128,8},{129... | collective-permute-start | bytes 417800 | tf_op jit(solution)/shard_map/ppermute | solution.py:261
  33.0 0.6 fusion
  33.6 13.4 %collective-permute-done.1.ref_ref = bf16[2,2,8,2176]{3,2,1,0:T(8,128)(2,1)S(1)} collective-permute-done((bf16[2,2,8,2176]{3,2,1,0:T(8,128)(2,1)S(1)}, bf16[2,2,8,2176]{3,2,1,0:T(8,128)(2,1)S(1)}, u32[]{:S(2)}, u32[]{:S(2)}) %collective-permute-start.1) | collective-permute-done | bytes 139296 | tf_op jit(solution)/shard_map/ppermute | solution.py:261
  47.0 0.0 all-to-all-done
  47.0 1.5 %shard_map.79 = f32[16,8,256]{2,1,0:T(8,128)} custom-call(bf16[8,2,2,16,1152]{4,3,2,1,0:T(8,128)(2,1)S(1)} %bitcast.14, bf16[2,2,8,2176]{3,2,1,0:T(8,128)(2,1)S(1)} %collective-permute-done.1.ref_ref, f32[12,2048]{1,0:T(8,128)S(1)} %get-tuple-element.11.cos_ref, f32[12,2048]{1,0:T(8,128)S(1)} %get-tuple-element.10.sin_ref, s32[1]{0:T(128)} %bitcast.7.zh_ref), custom_call_target="tpu_custom_call" | custom-call | tf_op jit(solution)/shard_map/pallas_call | solution.py:240
  48.6 24.7 %all-to-all-start.1 = ((f32[16,8,256]{2,1,0:T(8,128)}), f32[16,8,256]{2,1,0:T(8,128)S(1)}, u32[]{:S(2)}, u32[]{:S(2)}) async-start(f32[16,8,256]{2,1,0:T(8,128)} %shard_map.79), calls=%async_computation.1 | async-start | bytes 262144 | tf_op jit(solution)/shard_map/all_to_all | solution.py:251
  73.3 11.2 %all-to-all-done.1.got_ref = f32[16,8,256]{2,1,0:T(8,128)S(1)} async-done(((f32[16,8,256]{2,1,0:T(8,128)}), f32[16,8,256]{2,1,0:T(8,128)S(1)}, u32[]{:S(2)}, u32[]{:S(2)}) %all-to-all-start.1) | async-done | bytes 131104 | tf_op jit(solution)/shard_map/all_to_all | solution.py:251
  84.5 0.0 copy-done.4
  84.5 0.7 shard_map.80
  85.2 13.0 %all_to_all.20.got_ref = f32[16,8,128]{2,1,0:T(8,128)S(1)} all-to-all(f32[16,8,128]{2,1,0:T(8,128)S(1)} %get-tuple-element.6), channel_id=1, replica_groups=mesh['y'=4,'zh'=2,'c'=2,'zl'=8,'xh'=2,'xl'=2] {'y','c','xl'}, dimensions={0} | all-to-all | bytes 131072 | tf_op jit(solution)/shard_map/all_to_all | solution.py:251
  98.2 0.9 shard_map.81
  99.1 5.0 %all-to-all-start.3 = ((bf16[16,8,256]{2,1,0:T(8,128)(2,1)}), bf16[16,8,256]{2,1,0:T(8,128)(2,1)S(1)}, u32[]{:S(2)}, u32[]{:S(2)}) async-start(bf16[16,8,256]{2,1,0:T(8,128)(2,1)} %shard_map.81), calls=%async_computation.3 | async-start | bytes 131072 | tf_op jit(solution)/shard_map/all_to_all | solution.py:251
  104.1 10.9 %all-to-all-done.3.got_ref = bf16[16,8,256]{2,1,0:T(8,128)(2,1)S(1)} async-done(((bf16[16,8,256]{2,1,0:T(8,128)(2,1)}), bf16[16,8,256]{2,1,0:T(8,128)(2,1)S(1)}, u32[]{:S(2)}, u32[]{:S(2)}) %all-to-all-start.3) | async-done | bytes 65568 | tf_op jit(solution)/shard_map/all_to_all | solution.py:251
  115.0 1.0 shard_map.82
  116.0 9.3 %collective-permute-start.2 = (bf16[2,8,2176]{2,1,0:T(8,128)(2,1)S(1)}, bf16[2,8,2176]{2,1,0:T(8,128)(2,1)S(1)}, u32[]{:S(2)}, u32[]{:S(2)}) collective-permute-start(bf16[2,8,2176]{2,1,0:T(8,128)(2,1)S(1)} %get-tuple-element.8), channel_id=1, source_target_pairs={{0,0},{1,1},{2,32},{3,33},{4,64},{5,65},{6,96},{7,97},{8,128},{9,1... | collective-permute-start | bytes 208904 | tf_op jit(solution)/shard_map/ppermute | solution.py:285
  125.3 2.2 %collective-permute-start.3 = (bf16[2,8,2176]{2,1,0:T(8,128)(2,1)S(1)}, bf16[2,8,2176]{2,1,0:T(8,128)(2,1)S(1)}, u32[]{:S(2)}, u32[]{:S(2)}) collective-permute-start(bf16[2,8,2176]{2,1,0:T(8,128)(2,1)S(1)} %get-tuple-element.9), channel_id=1, source_target_pairs={{0,2},{1,3},{2,34},{3,35},{4,66},{5,67},{6,98},{7,99},{8,130},{9,1... | collective-permute-start | bytes 208904 | tf_op jit(solution)/shard_map/ppermute | solution.py:285
  127.6 0.1 slice_convert_fusion
  127.6 0.1 copy.8
  127.7 0.6 reduce_sum.9
  128.3 0.0 collective-permute-done.2.first_ref
  128.3 12.3 %collective-permute-done.3.second_ref = bf16[2,8,2176]{2,1,0:T(8,128)(2,1)S(1)} collective-permute-done((bf16[2,8,2176]{2,1,0:T(8,128)(2,1)S(1)}, bf16[2,8,2176]{2,1,0:T(8,128)(2,1)S(1)}, u32[]{:S(2)}, u32[]{:S(2)}) %collective-permute-start.3) | collective-permute-done | bytes 69664 | tf_op jit(solution)/shard_map/ppermute | solution.py:285
  140.6 0.8 shard_map.83
  (6 shorter events, 0.1 us)
Async XLA Ops:
  0.6 0.9 copy-start
  1.5 0.7 copy-start.2
  3.4 6.2 %copy-start.1 = (f32[2,8,2048]{2,1,0:T(8,128)S(1)}, f32[2,8,2048]{2,1,0:T(8,128)}, u32[]{:S(2)}) copy-start(f32[2,8,2048]{2,1,0:T(8,128)} %ref_ref.1) | copy-start | bytes 393220
  3.4 6.2 %copy-start.3 = (s32[8]{0:T(128)S(1)}, s32[8]{0:T(128)}, u32[]{:S(2)}) copy-start(s32[8]{0:T(128)} %param.10) | copy-start | bytes 100
  3.4 10.7 %copy-start.5 = (s32[12,2]{0,1:T(2,128)S(1)}, s32[12,2]{0,1:T(2,128)}, u32[]{:S(2)}) copy-start(s32[12,2]{0,1:T(2,128)} %param.9) | copy-start | bytes 292
  3.4 43.7 %all-to-all-start = ((bf16[16,2,16,1152]{3,2,1,0:T(8,128)(2,1)}), bf16[16,2,16,1152]{3,2,1,0:T(8,128)(2,1)S(1)}, u32[]{:S(2)}, u32[]{:S(2)}) async-start(bf16[16,2,16,1152]{3,2,1,0:T(8,128)(2,1)} %shard_map.77), calls=%async_computation | async-start | bytes 2359296 | tf_op jit(solution)/shard_map/all_to_all | solution.py:251
  9.7 18.1 %collective-permute-start = (bf16[2,8,2176]{2,1,0:T(8,128)(2,1)S(1)}, bf16[2,8,2176]{2,1,0:T(8,128)(2,1)S(1)}, u32[]{:S(2)}, u32[]{:S(2)}) collective-permute-start(bf16[2,8,2176]{2,1,0:T(8,128)(2,1)S(1)} %shard_map.78), channel_id=1, source_target_pairs={{0,2},{2,0},{1,3},{3,1},{4,6},{6,4},{5,7},{7,5},{8,10},{10,8},{9,1... | collective-permute-start | bytes 208904 | tf_op jit(solution)/shard_map/ppermute | solution.py:260
  27.8 56.6 %copy-start.4 = (f32[4]{0:T(128)S(1)}, f32[4]{0:T(128)}, u32[]{:S(2)}) copy-start(f32[4]{0:T(128)} %prior_ref.1) | copy-start | bytes 52
  27.8 19.2 %collective-permute-start.1 = (bf16[2,2,8,2176]{3,2,1,0:T(8,128)(2,1)S(1)}, bf16[2,2,8,2176]{3,2,1,0:T(8,128)(2,1)S(1)}, u32[]{:S(2)}, u32[]{:S(2)}) collective-permute-start(bf16[2,2,8,2176]{3,2,1,0:T(8,128)(2,1)S(1)} %pad_maximum_fusion), channel_id=1, source_target_pairs={{0,0},{1,1},{32,2},{33,3},{64,4},{65,5},{96,6},{97,7},{128,8},{129... | collective-permute-start | bytes 417800 | tf_op jit(solution)/shard_map/ppermute | solution.py:261
  48.6 35.9 %all-to-all-start.1 = ((f32[16,8,256]{2,1,0:T(8,128)}), f32[16,8,256]{2,1,0:T(8,128)S(1)}, u32[]{:S(2)}, u32[]{:S(2)}) async-start(f32[16,8,256]{2,1,0:T(8,128)} %shard_map.79), calls=%async_computation.1 | async-start | bytes 262144 | tf_op jit(solution)/shard_map/all_to_all | solution.py:251
  99.1 15.9 %all-to-all-start.3 = ((bf16[16,8,256]{2,1,0:T(8,128)(2,1)}), bf16[16,8,256]{2,1,0:T(8,128)(2,1)S(1)}, u32[]{:S(2)}, u32[]{:S(2)}) async-start(bf16[16,8,256]{2,1,0:T(8,128)(2,1)} %shard_map.81), calls=%async_computation.3 | async-start | bytes 131072 | tf_op jit(solution)/shard_map/all_to_all | solution.py:251
  116.0 12.4 %collective-permute-start.2 = (bf16[2,8,2176]{2,1,0:T(8,128)(2,1)S(1)}, bf16[2,8,2176]{2,1,0:T(8,128)(2,1)S(1)}, u32[]{:S(2)}, u32[]{:S(2)}) collective-permute-start(bf16[2,8,2176]{2,1,0:T(8,128)(2,1)S(1)} %get-tuple-element.8), channel_id=1, source_target_pairs={{0,0},{1,1},{2,32},{3,33},{4,64},{5,65},{6,96},{7,97},{8,128},{9,1... | collective-permute-start | bytes 208904 | tf_op jit(solution)/shard_map/ppermute | solution.py:285
  125.3 15.3 %collective-permute-start.3 = (bf16[2,8,2176]{2,1,0:T(8,128)(2,1)S(1)}, bf16[2,8,2176]{2,1,0:T(8,128)(2,1)S(1)}, u32[]{:S(2)}, u32[]{:S(2)}) collective-permute-start(bf16[2,8,2176]{2,1,0:T(8,128)(2,1)S(1)} %get-tuple-element.9), channel_id=1, source_target_pairs={{0,2},{1,3},{2,34},{3,35},{4,66},{5,67},{6,98},{7,99},{8,130},{9,1... | collective-permute-start | bytes 208904 | tf_op jit(solution)/shard_map/ppermute | solution.py:285

commit v6 on v3

--- a/solution.py
+++ b/solution.py
@@ -24,6 +24,7 @@
 IMG = ("y", "zh", "c")
 REF = ("zl", "xh", "xl")
 SPACE = ("y", "c", "xl")
+NEAR = ("y", "xl")
 BLOCK = ("zl", "xh")
 
 
@@ -84,7 +85,7 @@
     lane = iota((16, LANES), 1)
     pieces = jnp.where(lane == 0, first, jnp.where(lane == 1, second, jnp.where(lane == 2, third, 0.0)))
     pieces = pieces.astype(jnp.bfloat16)
-    for copy in range(16):
+    for copy in range(8):
         out_ref[copy, :, :, :HALF] = low
         out_ref[copy, 0, :, HALF:] = pieces
         out_ref[copy, 1, :, HALF:] = pieces
@@ -99,7 +100,7 @@
     out_ref[1, :, PIXELS:] = label
 
 
-def cross_kernel(img_ref, ref0_ref, ref1_ref, cos_ref, sin_ref, zh_ref, out_ref, shifted):
+def cross_kernel(own_ref, other_ref, ref0_ref, ref1_ref, cos_ref, sin_ref, zh_ref, c_ref, out_ref, shifted):
     straight = zh_ref[0] == 0
     ref0 = ref0_ref[:, :, :PIXELS].astype(jnp.float32)
     ref1 = ref1_ref[:, :, :PIXELS].astype(jnp.float32)
@@ -119,19 +120,20 @@
             shifted[1, rows, :] = jnp.concatenate(rot_im, axis=0).astype(jnp.bfloat16)
         spare = slice(e * LANES + USED, (e + 1) * LANES)
         shifted[:, spare, :] = jnp.zeros((2, LANES - USED, PIXELS), jnp.bfloat16)
-    total = jnp.zeros((128, 2 * LANES), jnp.float32)
-    for h in range(2):
-        for part in range(2):
-            total += lax.dot_general(
-                img_ref[:, h, part, :, :HALF].reshape(128, HALF),
-                shifted[part, :, h * HALF : (h + 1) * HALF],
-                (((1,), (1,)), ((), ())),
-                preferred_element_type=jnp.float32,
-            )
-    pieces = img_ref[:, 0, 0, :, HALF:].reshape(128, LANES).astype(jnp.float32)
-    precision = jnp.sum(pieces, axis=1, keepdims=True)
-    scaled = precision * (total - jnp.concatenate(halves, axis=1))
-    out_ref[...] = scaled.reshape(16, 8, 2 * LANES)
+    half = jnp.concatenate(halves, axis=1)
+    for img_ref, chip in ((own_ref, c_ref[0]), (other_ref, 1 - c_ref[0])):
+        total = jnp.zeros((64, 2 * LANES), jnp.float32)
+        for h in range(2):
+            for part in range(2):
+                total += lax.dot_general(
+                    img_ref[:, h, part, :, :HALF].reshape(64, HALF),
+                    shifted[part, :, h * HALF : (h + 1) * HALF],
+                    (((1,), (1,)), ((), ())),
+                    preferred_element_type=jnp.float32,
+                )
+        pieces = img_ref[:, 0, 0, :, HALF:].reshape(64, LANES).astype(jnp.float32)
+        precision = jnp.sum(pieces, axis=1, keepdims=True)
+        out_ref[pl.ds(chip * 8, 8)] = (precision * (total - half)).reshape(8, 8, 2 * LANES)
 
 
 def label_rows(ref0_ref, ref1_ref, straight):
@@ -182,20 +184,24 @@
         out_ref[:, :, half] = jnp.broadcast_to(message.astype(jnp.bfloat16)[None], (16, 8, LANES))
 
 
-def back_kernel(got_ref, img_ref, cos_ref, sin_ref, zh_ref, out0_ref, out1_ref):
+def back_kernel(got_ref, own_ref, other_ref, cos_ref, sin_ref, zh_ref, c_ref, out0_ref, out1_ref):
     straight = zh_ref[0] == 0
-    got = got_ref[...].astype(jnp.float32)
-    extra = jnp.sum(got, axis=0)
-    post = got.reshape(128, 2 * LANES)
-    post = jnp.where(iota((128, 2 * LANES), 1) % LANES < USED, post, 0.0)
-    weights = jnp.transpose(post).astype(jnp.bfloat16)
+    extra = jnp.sum(got_ref[...].astype(jnp.float32), axis=0)
+    sides = []
+    for img_ref, chip in ((own_ref, c_ref[0]), (other_ref, 1 - c_ref[0])):
+        post = got_ref[pl.ds(chip * 8, 8)].astype(jnp.float32).reshape(64, 2 * LANES)
+        post = jnp.where(iota((64, 2 * LANES), 1) % LANES < USED, post, 0.0)
+        sides.append((img_ref, jnp.transpose(post).astype(jnp.bfloat16)))
     for h in range(2):
         cols = slice(h * HALF, (h + 1) * HALF)
         back = [
-            jnp.dot(
-                weights,
-                img_ref[:, h, part, :, :HALF].reshape(128, HALF),
-                preferred_element_type=jnp.float32,
+            sum(
+                jnp.dot(
+                    weights,
+                    img_ref[:, h, part, :, :HALF].reshape(64, HALF),
+                    preferred_element_type=jnp.float32,
+                )
+                for img_ref, weights in sides
             )
             for part in range(2)
         ]
@@ -254,8 +260,10 @@
 def local(images, references, precision, shifts, labels, log_prior):
     y, zh, c, zl, xh, xl = (lax.axis_index(name) for name in ALL)
     half = zh.astype(jnp.int32)[None]
-    (sent,) = call(image_kernel, [((16, 2, 16, HALF + LANES), jnp.bfloat16)], (images, precision[None]))
-    units = swap(sent, SPACE).reshape(8, 2, 2, 16, HALF + LANES)
+    (sent,) = call(image_kernel, [((8, 2, 16, HALF + LANES), jnp.bfloat16)], (images, precision[None]))
+    own = swap(sent, NEAR).reshape(4, 2, 2, 16, HALF + LANES)
+    other = lax.ppermute(own, "c", [(0, 1), (1, 0)])
+    core = c.astype(jnp.int32)[None]
     (low,) = call(ref_kernel, [((2, 8, PIXELS + LANES), jnp.bfloat16)], (references, labels[None]))
     refs = [lax.ppermute(low, ALL, route) for route in routes(True)]
     tags = [ref[:1, :, PIXELS:] for ref in refs]
@@ -263,9 +271,9 @@
     (cross,) = call(
         cross_kernel,
         [((16, 8, 2 * LANES), jnp.float32)],
-        (units, *refs, cosine, sine, half),
+        (own, other, *refs, cosine, sine, half, core),
         [pltpu.VMEM((2, 2 * LANES, PIXELS), jnp.bfloat16)],
-        scalars=1,
+        scalars=2,
     )
     scores, stats = call(
         score_kernel,
@@ -278,12 +286,12 @@
     partial = call(
         back_kernel,
         [((2, 8, PIXELS + LANES), jnp.bfloat16)] * 2,
-        (posts, units, cosine, sine, half),
-        scalars=1,
+        (posts, own, other, cosine, sine, half, core),
+        scalars=2,
     )
     first, second = [lax.ppermute(part, ALL, route) for part, route in zip(partial, routes(False), strict=True)]
     (new_refs,) = call(final_kernel, [((2, 8, PIXELS), jnp.float32)], (first, second))
-    mine = lax.dynamic_slice_in_dim(posts, (y * 2 + c) * 2, 2, 0).reshape(16, 2 * LANES)
+    mine = lax.dynamic_slice_in_dim(posts, (c * 4 + y) * 2, 2, 0).reshape(16, 2 * LANES)
     shares = mine[:, CLASS : CLASS + 3 * CLASSES].astype(jnp.float32).reshape(16, 3, CLASSES)
     class_post = jnp.sum(shares, axis=1)
     return new_refs, class_post

time: 120 us -> 121 us (level)
  starting transfers between devices: 61.7 us -> 53.3 us
  waiting for transfers between devices: 36.5 us -> 41.8 us
  blocking collectives: 11.6 us -> 13.6 us
    all_to_all x3, starting transfers between devices: 29.4 us -> 18.2 us  [swap(): return lax.all_to_all(operand, axes, 0, 0, tiled=True)]
    ppermute x2, waiting for transfers between devices: 2 us -> 7.51 us  [local(): refs = [lax.ppermute(low, ALL, route) for route in routes(True)]]
    ppermute x0 -> x1, starting transfers between devices: none -> 4.31 us  [local(): other = lax.ppermute(own, 'c', [(0, 1), (1, 0)])]
    all_to_all x1, blocking collectives: 11.6 us -> 13.6 us  [swap(): return lax.all_to_all(operand, axes, 0, 0, tiled=True)]
  transfers between devices with their start and end apart: 7 -> 8, of which waited for: 4 -> 4; matrix products, arithmetic and copies ran while one was open for 1% -> 1% of each run, Pallas kernels for 0% -> 0%
where the time goes in v6:
time: 121 us; the launch traced here: 120 us
  starting transfers between devices  53.3 us (44%)
  waiting for transfers between devices  41.8 us (35%)
  blocking collectives  13.6 us (11%)
  Pallas kernels  6.96 us (6%)
  local copies, waits for them, and re-layouts  2.32 us (2%)
  other arithmetic  1.24 us (1%)
    all_to_all x3, waiting for transfers between devices, swap(): return lax.all_to_all(operand, axes, 0, 0, tiled=True)  22 us
    ppermute x2, starting transfers between devices, local(): refs = [lax.ppermute(low, ALL, route) for route in routes(True)]  18.3 us
    all_to_all x3, starting transfers between devices, swap(): return lax.all_to_all(operand, axes, 0, 0, tiled=True)  18.2 us
    all_to_all x1, blocking collectives, swap(): return lax.all_to_all(operand, axes, 0, 0, tiled=True)  13.6 us
    ppermute x2, starting transfers between devices, local(): lax.ppermute(part, ALL, route)  12.5 us
    ppermute x2, waiting for transfers between devices, local(): lax.ppermute(part, ALL, route)  12.3 us
    ppermute x2, waiting for transfers between devices, local(): refs = [lax.ppermute(low, ALL, route) for route in routes(True)]  7.51 us
    pallas_call x7, Pallas kernels, call(): pl.pallas_call(kernel, out_shape=out, in_specs=in_vmem + in_smem, out_spe...  6.96 us
  transfers between devices with their start and end apart: 8, of which 4 were waited for; matrix products, arithmetic and copies ran while one was open for 1% of the time, Pallas kernels for 0%

profile of v6, /device:TPU:33, one launch (start us, length us, event | category | flops | bytes accessed | tf_op | source)
XLA Modules:
  0.0 120.1 jit_solution(9009328184756613841)
XLA Ops:
  0.6 0.0 copy-start.2
  0.6 0.6 copy-done.2
  1.3 0.0 copy-start
  1.3 0.9 copy-done
  2.2 0.9 shard_map.77
  3.1 0.0 copy-start.1
  3.1 5.2 %all-to-all-start = ((bf16[8,2,16,1152]{3,2,1,0:T(8,128)(2,1)}), bf16[8,2,16,1152]{3,2,1,0:T(8,128)(2,1)S(1)}, u32[]{:S(2)}, u32[]{:S(2)}) async-start(bf16[8,2,16,1152]{3,2,1,0:T(8,128)(2,1)} %shard_map.77), calls=%async_computation | async-start | bytes 1179648 | tf_op jit(solution)/shard_map/all_to_all | solution.py:257
  8.4 0.0 copy-start.3
  8.4 0.0 copy-done.1
  8.4 0.6 copy-done.3
  9.0 0.1 shard_map.78
  9.1 0.0 copy-start.5
  9.1 16.4 %collective-permute-start.2 = (bf16[2,8,2176]{2,1,0:T(8,128)(2,1)S(1)}, bf16[2,8,2176]{2,1,0:T(8,128)(2,1)S(1)}, u32[]{:S(2)}, u32[]{:S(2)}) collective-permute-start(bf16[2,8,2176]{2,1,0:T(8,128)(2,1)S(1)} %shard_map.78), channel_id=1, source_target_pairs={{2,0},{3,1},{34,2},{35,3},{66,4},{67,5},{98,6},{99,7},{130,8},{131... | collective-permute-start | bytes 208904 | tf_op jit(solution)/shard_map/ppermute | solution.py:268
  25.5 1.9 %collective-permute-start.1 = (bf16[2,8,2176]{2,1,0:T(8,128)(2,1)S(1)}, bf16[2,8,2176]{2,1,0:T(8,128)(2,1)S(1)}, u32[]{:S(2)}, u32[]{:S(2)}) collective-permute-start(bf16[2,8,2176]{2,1,0:T(8,128)(2,1)S(1)} %shard_map.78), channel_id=1, source_target_pairs={{0,0},{1,1},{32,2},{33,3},{64,4},{65,5},{96,6},{97,7},{128,8},{129... | collective-permute-start | bytes 208904 | tf_op jit(solution)/shard_map/ppermute | solution.py:268
  27.4 0.0 all-to-all-done
  27.4 4.3 %collective-permute-start = (bf16[4,2,2,16,1152]{4,3,2,1,0:T(8,128)(2,1)S(1)}, bf16[4,2,2,16,1152]{4,3,2,1,0:T(8,128)(2,1)S(1)}, u32[]{:S(2)}, u32[]{:S(2)}) collective-permute-start(bf16[4,2,2,16,1152]{4,3,2,1,0:T(8,128)(2,1)S(1)} %bitcast.13), channel_id=1, source_target_pairs={{0,32},{32,0},{1,33},{33,1},{2,34},{34,2},{3,35},{35,3},{4,36},{36... | collective-permute-start | bytes 1769480 | tf_op jit(solution)/shard_map/ppermute | solution.py:265
  31.7 0.0 copy-done.5
  31.8 0.6 fusion
  32.4 0.0 collective-permute-done.2.ref1_ref
  32.4 7.5 %collective-permute-done.1.ref0_ref = bf16[2,8,2176]{2,1,0:T(8,128)(2,1)S(1)} collective-permute-done((bf16[2,8,2176]{2,1,0:T(8,128)(2,1)S(1)}, bf16[2,8,2176]{2,1,0:T(8,128)(2,1)S(1)}, u32[]{:S(2)}, u32[]{:S(2)}) %collective-permute-start.1) | collective-permute-done | bytes 69664 | tf_op jit(solution)/shard_map/ppermute | solution.py:268
  39.9 0.0 collective-permute-done.other_ref
  39.9 2.1 %shard_map.79 = f32[16,8,256]{2,1,0:T(8,128)} custom-call(bf16[4,2,2,16,1152]{4,3,2,1,0:T(8,128)(2,1)S(1)} %bitcast.14, bf16[4,2,2,16,1152]{4,3,2,1,0:T(8,128)(2,1)S(1)} %collective-permute-done.other_ref, bf16[2,8,2176]{2,1,0:T(8,128)(2,1)S(1)} %collective-permute-done.1.ref0_ref, bf16[2,8,2176]{2,1,0:T(8,128)(2,1)S(1)} %collective-permute-done.2.ref1_ref, ...), custom_call_target="tpu_custom_call" | custom-call | tf_op jit(solution)/shard_map/pallas_call | solution.py:246
  41.9 8.0 %all-to-all-start.1 = ((f32[16,8,256]{2,1,0:T(8,128)}), f32[16,8,256]{2,1,0:T(8,128)S(1)}, u32[]{:S(2)}, u32[]{:S(2)}) async-start(f32[16,8,256]{2,1,0:T(8,128)} %shard_map.79), calls=%async_computation.1 | async-start | bytes 262144 | tf_op jit(solution)/shard_map/all_to_all | solution.py:257
  50.0 0.0 copy-start.4
  50.0 11.1 %all-to-all-done.1.got_ref = f32[16,8,256]{2,1,0:T(8,128)S(1)} async-done(((f32[16,8,256]{2,1,0:T(8,128)}), f32[16,8,256]{2,1,0:T(8,128)S(1)}, u32[]{:S(2)}, u32[]{:S(2)}) %all-to-all-start.1) | async-done | bytes 131104 | tf_op jit(solution)/shard_map/all_to_all | solution.py:257
  61.2 0.0 copy-done.4
  61.2 0.7 shard_map.80
  61.9 13.6 %all_to_all.20.got_ref = f32[16,8,128]{2,1,0:T(8,128)S(1)} all-to-all(f32[16,8,128]{2,1,0:T(8,128)S(1)} %get-tuple-element.6), channel_id=1, replica_groups=mesh['y'=4,'zh'=2,'c'=2,'zl'=8,'xh'=2,'xl'=2] {'y','c','xl'}, dimensions={0} | all-to-all | bytes 131072 | tf_op jit(solution)/shard_map/all_to_all | solution.py:257
  75.5 0.9 shard_map.81
  76.4 4.9 %all-to-all-start.3 = ((bf16[16,8,256]{2,1,0:T(8,128)(2,1)}), bf16[16,8,256]{2,1,0:T(8,128)(2,1)S(1)}, u32[]{:S(2)}, u32[]{:S(2)}) async-start(bf16[16,8,256]{2,1,0:T(8,128)(2,1)} %shard_map.81), calls=%async_computation.3 | async-start | bytes 131072 | tf_op jit(solution)/shard_map/all_to_all | solution.py:257
  81.3 10.9 %all-to-all-done.3.got_ref = bf16[16,8,256]{2,1,0:T(8,128)(2,1)S(1)} async-done(((bf16[16,8,256]{2,1,0:T(8,128)(2,1)}), bf16[16,8,256]{2,1,0:T(8,128)(2,1)S(1)}, u32[]{:S(2)}, u32[]{:S(2)}) %all-to-all-start.3) | async-done | bytes 65568 | tf_op jit(solution)/shard_map/all_to_all | solution.py:257
  92.2 1.5 %shard_map.82 = (bf16[2,8,2176]{2,1,0:T(8,128)(2,1)S(1)}, bf16[2,8,2176]{2,1,0:T(8,128)(2,1)S(1)}) custom-call(bf16[16,8,256]{2,1,0:T(8,128)(2,1)S(1)} %all-to-all-done.3.got_ref, bf16[4,2,2,16,1152]{4,3,2,1,0:T(8,128)(2,1)S(1)} %bitcast.15, bf16[4,2,2,16,1152]{4,3,2,1,0:T(8,128)(2,1)S(1)} %collective-permute-done.other_ref, ...), custom_call_target="tpu_custom_call" | custom-call | tf_op jit(solution)/shard_map/pallas_call | solution.py:246
  93.7 10.3 %collective-permute-start.3 = (bf16[2,8,2176]{2,1,0:T(8,128)(2,1)S(1)}, bf16[2,8,2176]{2,1,0:T(8,128)(2,1)S(1)}, u32[]{:S(2)}, u32[]{:S(2)}) collective-permute-start(bf16[2,8,2176]{2,1,0:T(8,128)(2,1)S(1)} %get-tuple-element.8), channel_id=1, source_target_pairs={{0,0},{1,1},{2,32},{3,33},{4,64},{5,65},{6,96},{7,97},{8,128},{9,1... | collective-permute-start | bytes 208904 | tf_op jit(solution)/shard_map/ppermute | solution.py:292
  104.0 2.2 %collective-permute-start.4 = (bf16[2,8,2176]{2,1,0:T(8,128)(2,1)S(1)}, bf16[2,8,2176]{2,1,0:T(8,128)(2,1)S(1)}, u32[]{:S(2)}, u32[]{:S(2)}) collective-permute-start(bf16[2,8,2176]{2,1,0:T(8,128)(2,1)S(1)} %get-tuple-element.9), channel_id=1, source_target_pairs={{0,2},{1,3},{2,34},{3,35},{4,66},{5,67},{6,98},{7,99},{8,130},{9,1... | collective-permute-start | bytes 208904 | tf_op jit(solution)/shard_map/ppermute | solution.py:292
  106.3 0.1 slice_convert_fusion
  106.3 0.1 copy.8
  106.4 0.6 reduce_sum.9
  107.0 0.0 collective-permute-done.3.first_ref
  107.0 12.3 %collective-permute-done.4.second_ref = bf16[2,8,2176]{2,1,0:T(8,128)(2,1)S(1)} collective-permute-done((bf16[2,8,2176]{2,1,0:T(8,128)(2,1)S(1)}, bf16[2,8,2176]{2,1,0:T(8,128)(2,1)S(1)}, u32[]{:S(2)}, u32[]{:S(2)}) %collective-permute-start.4) | collective-permute-done | bytes 69664 | tf_op jit(solution)/shard_map/ppermute | solution.py:292
  119.3 0.8 shard_map.83
  (6 shorter events, 0.0 us)
Async XLA Ops:
  0.6 0.7 copy-start.2
  1.3 0.9 copy-start
  3.1 5.3 %copy-start.1 = (f32[2,8,2048]{2,1,0:T(8,128)S(1)}, f32[2,8,2048]{2,1,0:T(8,128)}, u32[]{:S(2)}) copy-start(f32[2,8,2048]{2,1,0:T(8,128)} %ref_ref.1) | copy-start | bytes 393220
  3.1 24.3 %all-to-all-start = ((bf16[8,2,16,1152]{3,2,1,0:T(8,128)(2,1)}), bf16[8,2,16,1152]{3,2,1,0:T(8,128)(2,1)S(1)}, u32[]{:S(2)}, u32[]{:S(2)}) async-start(bf16[8,2,16,1152]{3,2,1,0:T(8,128)(2,1)} %shard_map.77), calls=%async_computation | async-start | bytes 1179648 | tf_op jit(solution)/shard_map/all_to_all | solution.py:257
  8.4 0.7 copy-start.3
  9.1 22.6 %copy-start.5 = (s32[12,2]{0,1:T(2,128)S(1)}, s32[12,2]{0,1:T(2,128)}, u32[]{:S(2)}) copy-start(s32[12,2]{0,1:T(2,128)} %param.9) | copy-start | bytes 292
  9.1 23.3 %collective-permute-start.2 = (bf16[2,8,2176]{2,1,0:T(8,128)(2,1)S(1)}, bf16[2,8,2176]{2,1,0:T(8,128)(2,1)S(1)}, u32[]{:S(2)}, u32[]{:S(2)}) collective-permute-start(bf16[2,8,2176]{2,1,0:T(8,128)(2,1)S(1)} %shard_map.78), channel_id=1, source_target_pairs={{2,0},{3,1},{34,2},{35,3},{66,4},{67,5},{98,6},{99,7},{130,8},{131... | collective-permute-start | bytes 208904 | tf_op jit(solution)/shard_map/ppermute | solution.py:268
  25.5 14.4 %collective-permute-start.1 = (bf16[2,8,2176]{2,1,0:T(8,128)(2,1)S(1)}, bf16[2,8,2176]{2,1,0:T(8,128)(2,1)S(1)}, u32[]{:S(2)}, u32[]{:S(2)}) collective-permute-start(bf16[2,8,2176]{2,1,0:T(8,128)(2,1)S(1)} %shard_map.78), channel_id=1, source_target_pairs={{0,0},{1,1},{32,2},{33,3},{64,4},{65,5},{96,6},{97,7},{128,8},{129... | collective-permute-start | bytes 208904 | tf_op jit(solution)/shard_map/ppermute | solution.py:268
  27.4 12.5 %collective-permute-start = (bf16[4,2,2,16,1152]{4,3,2,1,0:T(8,128)(2,1)S(1)}, bf16[4,2,2,16,1152]{4,3,2,1,0:T(8,128)(2,1)S(1)}, u32[]{:S(2)}, u32[]{:S(2)}) collective-permute-start(bf16[4,2,2,16,1152]{4,3,2,1,0:T(8,128)(2,1)S(1)} %bitcast.13), channel_id=1, source_target_pairs={{0,32},{32,0},{1,33},{33,1},{2,34},{34,2},{3,35},{35,3},{4,36},{36... | collective-permute-start | bytes 1769480 | tf_op jit(solution)/shard_map/ppermute | solution.py:265
  41.9 19.2 %all-to-all-start.1 = ((f32[16,8,256]{2,1,0:T(8,128)}), f32[16,8,256]{2,1,0:T(8,128)S(1)}, u32[]{:S(2)}, u32[]{:S(2)}) async-start(f32[16,8,256]{2,1,0:T(8,128)} %shard_map.79), calls=%async_computation.1 | async-start | bytes 262144 | tf_op jit(solution)/shard_map/all_to_all | solution.py:257
  50.0 11.2 %copy-start.4 = (f32[4]{0:T(128)S(1)}, f32[4]{0:T(128)}, u32[]{:S(2)}) copy-start(f32[4]{0:T(128)} %prior_ref.1) | copy-start | bytes 52
  76.4 15.8 %all-to-all-start.3 = ((bf16[16,8,256]{2,1,0:T(8,128)(2,1)}), bf16[16,8,256]{2,1,0:T(8,128)(2,1)S(1)}, u32[]{:S(2)}, u32[]{:S(2)}) async-start(bf16[16,8,256]{2,1,0:T(8,128)(2,1)} %shard_map.81), calls=%async_computation.3 | async-start | bytes 131072 | tf_op jit(solution)/shard_map/all_to_all | solution.py:257
  93.7 13.3 %collective-permute-start.3 = (bf16[2,8,2176]{2,1,0:T(8,128)(2,1)S(1)}, bf16[2,8,2176]{2,1,0:T(8,128)(2,1)S(1)}, u32[]{:S(2)}, u32[]{:S(2)}) collective-permute-start(bf16[2,8,2176]{2,1,0:T(8,128)(2,1)S(1)} %get-tuple-element.8), channel_id=1, source_target_pairs={{0,0},{1,1},{2,32},{3,33},{4,64},{5,65},{6,96},{7,97},{8,128},{9,1... | collective-permute-start | bytes 208904 | tf_op jit(solution)/shard_map/ppermute | solution.py:292
  104.0 15.3 %collective-permute-start.4 = (bf16[2,8,2176]{2,1,0:T(8,128)(2,1)S(1)}, bf16[2,8,2176]{2,1,0:T(8,128)(2,1)S(1)}, u32[]{:S(2)}, u32[]{:S(2)}) collective-permute-start(bf16[2,8,2176]{2,1,0:T(8,128)(2,1)S(1)} %get-tuple-element.9), channel_id=1, source_target_pairs={{0,2},{1,3},{2,34},{3,35},{4,66},{5,67},{6,98},{7,99},{8,130},{9,1... | collective-permute-start | bytes 208904 | tf_op jit(solution)/shard_map/ppermute | solution.py:292

commit v7 on v3

--- a/solution.py
+++ b/solution.py
@@ -19,12 +19,13 @@
 CLASS = USED + 4
 PIXELS = 2048
 HALF = 1024
-SIZES = {"y": 4, "zh": 2, "c": 2, "zl": 8, "xh": 2, "xl": 2}
+SIZES = {"y": 4, "zh": 2, "c": 2, "zu": 2, "zv": 4, "xh": 2, "xl": 2}
 ALL = tuple(SIZES)
 IMG = ("y", "zh", "c")
-REF = ("zl", "xh", "xl")
-SPACE = ("y", "c", "xl")
-BLOCK = ("zl", "xh")
+REF = ("zu", "zv", "xh", "xl")
+SPACE = ("zv", "xh", "xl")
+BLOCK = IMG
+SWAP = [(0, 1), (1, 0)]
 
 
 def place(*coords):
@@ -34,16 +35,15 @@
     return number
 
 
-def routes(inward):
-    made = []
-    for r in range(2):
-        pairs = []
-        for y, zh, c, zl, xh, xl in itertools.product(*(range(size) for size in SIZES.values())):
-            work = place(y, zh, c, zl, xh, xl)
-            home = place(zl // 2, zl % 2, xh, 2 * y + c, r ^ zh, xl)
-            pairs.append((home, work) if inward else (work, home))
-        made.append(pairs)
-    return made
+def image_route():
+    pairs = []
+    for y, zh, c, zu, zv, xh, xl in itertools.product(*(range(size) for size in SIZES.values())):
+        work = place(2 * zu + zv // 2, zv % 2, xh, y // 2, 2 * (y % 2) + zh, c, xl)
+        pairs.append((place(y, zh, c, zu, zv, xh, xl), work))
+    return pairs
+
+
+IMG_ROUTE = image_route()
 
 
 def phases(shifts, block):
@@ -84,10 +84,9 @@
     lane = iota((16, LANES), 1)
     pieces = jnp.where(lane == 0, first, jnp.where(lane == 1, second, jnp.where(lane == 2, third, 0.0)))
     pieces = pieces.astype(jnp.bfloat16)
-    for copy in range(16):
-        out_ref[copy, :, :, :HALF] = low
-        out_ref[copy, 0, :, HALF:] = pieces
-        out_ref[copy, 1, :, HALF:] = pieces
+    out_ref[:, :, :HALF] = low
+    out_ref[0, :, HALF:] = pieces
+    out_ref[1, :, HALF:] = pieces
 
 
 def ref_kernel(ref_ref, label_ref, out_ref):
@@ -99,8 +98,8 @@
     out_ref[1, :, PIXELS:] = label
 
 
-def cross_kernel(img_ref, ref0_ref, ref1_ref, cos_ref, sin_ref, zh_ref, out_ref, shifted):
-    straight = zh_ref[0] == 0
+def cross_kernel(img_ref, ref0_ref, ref1_ref, cos_ref, sin_ref, zu_ref, out_ref, shifted):
+    straight = zu_ref[0] == 0
     ref0 = ref0_ref[:, :, :PIXELS].astype(jnp.float32)
     ref1 = ref1_ref[:, :, :PIXELS].astype(jnp.float32)
     halves = []
@@ -141,8 +140,8 @@
     return jnp.concatenate([as_row(low), as_row(high)], axis=1)
 
 
-def score_kernel(got_ref, ref0_ref, ref1_ref, prior_ref, zh_ref, score_ref, out_ref):
-    labels = label_rows(ref0_ref, ref1_ref, zh_ref[0] == 0)
+def score_kernel(got_ref, ref0_ref, ref1_ref, prior_ref, zu_ref, score_ref, out_ref):
+    labels = label_rows(ref0_ref, ref1_ref, zu_ref[0] == 0)
     prior = jnp.zeros((1, 2 * LANES), jnp.float32)
     for k in range(CLASSES):
         prior = jnp.where(labels == k, prior_ref[k], prior)
@@ -182,8 +181,8 @@
         out_ref[:, :, half] = jnp.broadcast_to(message.astype(jnp.bfloat16)[None], (16, 8, LANES))
 
 
-def back_kernel(got_ref, img_ref, cos_ref, sin_ref, zh_ref, out0_ref, out1_ref):
-    straight = zh_ref[0] == 0
+def back_kernel(got_ref, img_ref, cos_ref, sin_ref, zu_ref, row_ref, out0_ref, out1_ref):
+    straight = zu_ref[0] == 0
     got = got_ref[...].astype(jnp.float32)
     extra = jnp.sum(got, axis=0)
     post = got.reshape(128, 2 * LANES)
@@ -208,9 +207,9 @@
                 sums[2 * e] += back_re * cos - back_im * sin
                 sums[2 * e + 1] += back_im * cos + back_re * sin
         for part in range(2):
-            low, high = sums[part].astype(jnp.bfloat16), sums[2 + part].astype(jnp.bfloat16)
+            low, high = sums[part], sums[2 + part]
             out0_ref[part, :, cols] = jnp.where(straight, low, high)
-            out1_ref[part, :, cols] = jnp.where(straight, high, low)
+            out1_ref[part, :, cols] = jnp.where(straight, high, low).astype(jnp.bfloat16)
     lane = iota((8, LANES), 1)
     masses = []
     for e in range(2):
@@ -218,19 +217,28 @@
         mass = jnp.sum(jnp.where(mine, extra[:, e * LANES : (e + 1) * LANES], 0.0), axis=1, keepdims=True)
         row = jnp.zeros((8, LANES), jnp.float32)
         for number, piece in enumerate(pieces_of(mass)):
-            row = jnp.where(lane == number, piece, row)
-        masses.append(row.astype(jnp.bfloat16))
+            row = jnp.where(lane == MASS + number, piece, row)
+        masses.append(row)
+    shared = (lane >= CLASS) & (lane < CLASS + 3 * CLASSES)
     for part in range(2):
-        out0_ref[part, :, PIXELS:] = jnp.where(straight, masses[0], masses[1])
-        out1_ref[part, :, PIXELS:] = jnp.where(straight, masses[1], masses[0])
-
-
-def final_kernel(first_ref, second_ref, out_ref):
-    extra = first_ref[0, :, PIXELS:].astype(jnp.float32) + second_ref[0, :, PIXELS:].astype(jnp.float32)
-    mass = jnp.sum(extra, axis=1, keepdims=True)
+        classes = got_ref[row_ref[0] + part, :, :LANES].astype(jnp.float32)
+        classes = jnp.where(shared, classes, 0.0)
+        out0_ref[part, :, PIXELS:] = jnp.where(straight, masses[0], masses[1]) + classes
+        out1_ref[part, :, PIXELS:] = (jnp.where(straight, masses[1], masses[0]) + classes).astype(jnp.bfloat16)
+
+
+def final_kernel(first_ref, second_ref, own_ref, out_ref, class_ref):
+    own = own_ref[0] == 1
+    lane = iota((8, LANES), 1)
+    first, second = first_ref[0, :, PIXELS:], second_ref[0, :, PIXELS:].astype(jnp.float32)
+    mine = (lane >= MASS) & (lane < MASS + 3)
+    mass = jnp.sum(jnp.where(mine, first + second, 0.0), axis=1, keepdims=True)
     for part in range(2):
-        both = first_ref[part, :, :PIXELS].astype(jnp.float32) + second_ref[part, :, :PIXELS].astype(jnp.float32)
+        both = first_ref[part, :, :PIXELS] + second_ref[part, :, :PIXELS].astype(jnp.float32)
         out_ref[part] = both / (mass + 1.0)
+        classes = jnp.where(own, first_ref[part, :, PIXELS:], second_ref[part, :, PIXELS:].astype(jnp.float32))
+        parts = [pltpu.roll(classes, LANES - CLASS - CLASSES * number, 1) for number in range(3)]
+        class_ref[8 * part : 8 * part + 8, :] = (parts[0] + parts[1] + parts[2])[:, :CLASSES]
 
 
 def call(kernel, shapes, args, scratch=(), scalars=0):
@@ -252,14 +260,15 @@
 
 
 def local(images, references, precision, shifts, labels, log_prior):
-    y, zh, c, zl, xh, xl = (lax.axis_index(name) for name in ALL)
-    half = zh.astype(jnp.int32)[None]
-    (sent,) = call(image_kernel, [((16, 2, 16, HALF + LANES), jnp.bfloat16)], (images, precision[None]))
-    units = swap(sent, SPACE).reshape(8, 2, 2, 16, HALF + LANES)
+    y, zh, c, zu, zv, xh, xl = (lax.axis_index(name).astype(jnp.int32) for name in ALL)
+    half = zu[None]
+    (sent,) = call(image_kernel, [((2, 16, HALF + LANES), jnp.bfloat16)], (images, precision[None]))
+    sent = lax.ppermute(sent, ALL, IMG_ROUTE)
+    units = swap(jnp.broadcast_to(sent[None], (16,) + sent.shape), SPACE).reshape(8, 2, 2, 16, HALF + LANES)
     (low,) = call(ref_kernel, [((2, 8, PIXELS + LANES), jnp.bfloat16)], (references, labels[None]))
-    refs = [lax.ppermute(low, ALL, route) for route in routes(True)]
+    refs = [low, lax.ppermute(low, "zu", SWAP)]
     tags = [ref[:1, :, PIXELS:] for ref in refs]
-    cosine, sine = phases(shifts, zl * 2 + xh)
+    cosine, sine = phases(shifts, y * 4 + zh * 2 + c)
     (cross,) = call(
         cross_kernel,
         [((16, 8, 2 * LANES), jnp.float32)],
@@ -275,18 +284,20 @@
     )
     (post,) = call(post_kernel, [((16, 8, 2 * LANES), jnp.bfloat16)], (swap(stats, SPACE), scores))
     posts = swap(post, BLOCK)
-    partial = call(
+    first, second = call(
         back_kernel,
-        [((2, 8, PIXELS + LANES), jnp.bfloat16)] * 2,
-        (posts, units, cosine, sine, half),
+        [((2, 8, PIXELS + LANES), jnp.float32), ((2, 8, PIXELS + LANES), jnp.bfloat16)],
+        (posts, units, cosine, sine, half, 2 * (4 * (y % 2) + 2 * zh + c)[None]),
+        scalars=2,
+    )
+    second = lax.ppermute(second, "zu", SWAP)
+    own = (zu == y // 2).astype(jnp.int32)[None]
+    return call(
+        final_kernel,
+        [((2, 8, PIXELS), jnp.float32), ((16, CLASSES), jnp.float32)],
+        (first, second, own),
         scalars=1,
     )
-    first, second = [lax.ppermute(part, ALL, route) for part, route in zip(partial, routes(False), strict=True)]
-    (new_refs,) = call(final_kernel, [((2, 8, PIXELS), jnp.float32)], (first, second))
-    mine = lax.dynamic_slice_in_dim(posts, (y * 2 + c) * 2, 2, 0).reshape(16, 2 * LANES)
-    shares = mine[:, CLASS : CLASS + 3 * CLASSES].astype(jnp.float32).reshape(16, 3, CLASSES)
-    class_post = jnp.sum(shares, axis=1)
-    return new_refs, class_post
 
 
 def solution(mesh):

time: 120 us -> 143 us (1.19)
  the two profiles are of different devices: /device:TPU:33 before, /device:TPU:1 now
where the time goes in v7:
time: 143 us
  waiting for transfers between devices  61.9 us (43%)
  starting transfers between devices  56.4 us (39%)
  blocking collectives  14.8 us (10%)
  Pallas kernels  5.12 us (4%)
  local copies, waits for them, and re-layouts  3.35 us (2%)
    all_to_all x3, starting transfers between devices, swap(): return lax.all_to_all(operand, axes, 0, 0, tiled=True)  40.1 us
    all_to_all x3, waiting for transfers between devices, swap(): return lax.all_to_all(operand, axes, 0, 0, tiled=True)  37.7 us
    all_to_all x1, blocking collectives, swap(): return lax.all_to_all(operand, axes, 0, 0, tiled=True)  14.8 us
    ppermute x1, waiting for transfers between devices, local(): refs = [low, lax.ppermute(low, 'zu', SWAP)]  13.3 us
    ppermute x1, waiting for transfers between devices, local(): second = lax.ppermute(second, 'zu', SWAP)  8.8 us
    ppermute x1, starting transfers between devices, local(): sent = lax.ppermute(sent, ALL, IMG_ROUTE)  6.03 us
    ppermute x1, starting transfers between devices, local(): second = lax.ppermute(second, 'zu', SWAP)  5.23 us
    pallas_call x7, Pallas kernels, call(): pl.pallas_call(kernel, out_shape=out, in_specs=in_vmem + in_smem, out_spe...  5.12 us
  transfers between devices with their start and end apart: 6, of which 6 were waited for; matrix products, arithmetic and copies ran while one was open for 0% of the time, Pallas kernels for 0%

profile of v7, /device:TPU:1, one launch (start us, length us, event | category | flops | bytes accessed | tf_op | source)
XLA Modules:
  0.0 142.9 jit_solution(9763549798902332248)
XLA Ops:
  0.6 0.0 copy-start
  0.6 0.9 copy-done
  1.5 0.0 copy-start.2
  1.5 0.7 copy-done.2
  2.2 0.1 shard_map.77
  2.3 6.0 %collective-permute-start = (bf16[2,16,1152]{2,1,0:T(8,128)(2,1)S(1)}, bf16[2,16,1152]{2,1,0:T(8,128)(2,1)S(1)}, u32[]{:S(2)}, u32[]{:S(2)}) collective-permute-start(bf16[2,16,1152]{2,1,0:T(8,128)(2,1)S(1)} %shard_map.77), channel_id=1, source_target_pairs={{0,0},{1,1},{2,32},{3,33},{4,64},{5,65},{6,96},{7,97},{8,128},{9,1... | collective-permute-start | bytes 221192 | tf_op jit(solution)/shard_map/ppermute | solution.py:266
  8.3 2.0 %collective-permute-done = bf16[2,16,1152]{2,1,0:T(8,128)(2,1)S(1)} collective-permute-done((bf16[2,16,1152]{2,1,0:T(8,128)(2,1)S(1)}, bf16[2,16,1152]{2,1,0:T(8,128)(2,1)S(1)}, u32[]{:S(2)}, u32[]{:S(2)}) %collective-permute-start) | collective-permute-done | bytes 73760 | tf_op jit(solution)/shard_map/ppermute | solution.py:266
  10.3 1.1 broadcast_in_dim.26
  11.5 0.0 copy-start.1
  11.5 0.0 copy-start.3
  11.5 0.0 copy-start.5
  11.5 18.1 %all-to-all-start = ((bf16[16,2,16,1152]{3,2,1,0:T(8,128)(2,1)}), bf16[16,2,16,1152]{3,2,1,0:T(8,128)(2,1)S(1)}, u32[]{:S(2)}, u32[]{:S(2)}) async-start(bf16[16,2,16,1152]{3,2,1,0:T(8,128)(2,1)} %broadcast_in_dim.26), calls=%async_computation | async-start | bytes 2359296 | tf_op jit(solution)/shard_map/all_to_all | solution.py:259
  29.6 0.0 copy-done.1
  29.6 0.0 copy-done.3
  29.6 0.1 shard_map.78.ref0_ref
  29.7 0.0 copy-start.4
  29.7 5.0 %collective-permute-start.1 = (bf16[2,8,2176]{2,1,0:T(8,128)(2,1)S(1)}, bf16[2,8,2176]{2,1,0:T(8,128)(2,1)S(1)}, u32[]{:S(2)}, u32[]{:S(2)}) collective-permute-start(bf16[2,8,2176]{2,1,0:T(8,128)(2,1)S(1)} %shard_map.78.ref0_ref), channel_id=1, source_target_pairs={{0,16},{16,0},{1,17},{17,1},{2,18},{18,2},{3,19},{19,3},{4,20},{20... | collective-permute-start | bytes 208904 | tf_op jit(solution)/shard_map/ppermute | solution.py:269
  34.8 0.0 copy-done.5
  34.8 0.6 fusion
  35.3 13.3 %collective-permute-done.1.ref1_ref = bf16[2,8,2176]{2,1,0:T(8,128)(2,1)S(1)} collective-permute-done((bf16[2,8,2176]{2,1,0:T(8,128)(2,1)S(1)}, bf16[2,8,2176]{2,1,0:T(8,128)(2,1)S(1)}, u32[]{:S(2)}, u32[]{:S(2)}) %collective-permute-start.1) | collective-permute-done | bytes 69664 | tf_op jit(solution)/shard_map/ppermute | solution.py:269
  48.7 8.2 %all-to-all-done = bf16[16,2,16,1152]{3,2,1,0:T(8,128)(2,1)S(1)} async-done(((bf16[16,2,16,1152]{3,2,1,0:T(8,128)(2,1)}), bf16[16,2,16,1152]{3,2,1,0:T(8,128)(2,1)S(1)}, u32[]{:S(2)}, u32[]{:S(2)}) %all-to-all-start) | async-done | bytes 1179680 | tf_op jit(solution)/shard_map/all_to_all | solution.py:259
  56.9 1.5 %shard_map.79 = f32[16,8,256]{2,1,0:T(8,128)} custom-call(bf16[8,2,2,16,1152]{4,3,2,1,0:T(8,128)(2,1)S(1)} %bitcast.10, bf16[2,8,2176]{2,1,0:T(8,128)(2,1)S(1)} %shard_map.78.ref0_ref, bf16[2,8,2176]{2,1,0:T(8,128)(2,1)S(1)} %collective-permute-done.1.ref1_ref, f32[12,2048]{1,0:T(8,128)S(1)} %get-tuple-element.13.cos_ref, ...), custom_call_target="tpu_custom_call" | custom-call | tf_op jit(solution)/shard_map/pallas_call | solution.py:248
  58.4 16.7 %all-to-all-start.1 = ((f32[16,8,256]{2,1,0:T(8,128)}), f32[16,8,256]{2,1,0:T(8,128)S(1)}, u32[]{:S(2)}, u32[]{:S(2)}) async-start(f32[16,8,256]{2,1,0:T(8,128)} %shard_map.79), calls=%async_computation.1 | async-start | bytes 262144 | tf_op jit(solution)/shard_map/all_to_all | solution.py:259
  75.1 14.9 %all-to-all-done.1.got_ref = f32[16,8,256]{2,1,0:T(8,128)S(1)} async-done(((f32[16,8,256]{2,1,0:T(8,128)}), f32[16,8,256]{2,1,0:T(8,128)S(1)}, u32[]{:S(2)}, u32[]{:S(2)}) %all-to-all-start.1) | async-done | bytes 131104 | tf_op jit(solution)/shard_map/all_to_all | solution.py:259
  90.0 0.0 copy-done.4
  90.0 0.7 shard_map.80
  90.8 14.8 %all_to_all.20.got_ref = f32[16,8,128]{2,1,0:T(8,128)S(1)} all-to-all(f32[16,8,128]{2,1,0:T(8,128)S(1)} %get-tuple-element.6), channel_id=1, replica_groups=mesh['y'=4,'zh'=2,'c'=2,'zu'=2,'zv'=4,'xh'=2,'xl'=2] {'zv','xh','xl'}, dimensions={0} | all-to-all | bytes 131072 | tf_op jit(solution)/shard_map/all_to_all | solution.py:259
  105.5 0.9 shard_map.81
  106.5 5.4 %all-to-all-start.3 = ((bf16[16,8,256]{2,1,0:T(8,128)(2,1)}), bf16[16,8,256]{2,1,0:T(8,128)(2,1)S(1)}, u32[]{:S(2)}, u32[]{:S(2)}) async-start(bf16[16,8,256]{2,1,0:T(8,128)(2,1)} %shard_map.81), calls=%async_computation.3 | async-start | bytes 131072 | tf_op jit(solution)/shard_map/all_to_all | solution.py:259
  111.8 14.6 %all-to-all-done.3.got_ref = bf16[16,8,256]{2,1,0:T(8,128)(2,1)S(1)} async-done(((bf16[16,8,256]{2,1,0:T(8,128)(2,1)}), bf16[16,8,256]{2,1,0:T(8,128)(2,1)S(1)}, u32[]{:S(2)}, u32[]{:S(2)}) %all-to-all-start.3) | async-done | bytes 65568 | tf_op jit(solution)/shard_map/all_to_all | solution.py:259
  126.4 1.0 shard_map.82
  127.5 5.2 %collective-permute-start.2 = (bf16[2,8,2176]{2,1,0:T(8,128)(2,1)S(1)}, bf16[2,8,2176]{2,1,0:T(8,128)(2,1)S(1)}, u32[]{:S(2)}, u32[]{:S(2)}) collective-permute-start(bf16[2,8,2176]{2,1,0:T(8,128)(2,1)S(1)} %get-tuple-element.9), channel_id=1, source_target_pairs={{0,16},{16,0},{1,17},{17,1},{2,18},{18,2},{3,19},{19,3},{4,20},{20... | collective-permute-start | bytes 208904 | tf_op jit(solution)/shard_map/ppermute | solution.py:293
  132.7 8.8 %collective-permute-done.2.second_ref = bf16[2,8,2176]{2,1,0:T(8,128)(2,1)S(1)} collective-permute-done((bf16[2,8,2176]{2,1,0:T(8,128)(2,1)S(1)}, bf16[2,8,2176]{2,1,0:T(8,128)(2,1)S(1)}, u32[]{:S(2)}, u32[]{:S(2)}) %collective-permute-start.2) | collective-permute-done | bytes 69664 | tf_op jit(solution)/shard_map/ppermute | solution.py:293
  141.5 0.8 shard_map.83
  142.3 0.7 copy.8
  (4 shorter events, 0.0 us)
Async XLA Ops:
  0.6 0.9 copy-start
  1.5 0.7 copy-start.2
  2.3 8.1 %collective-permute-start = (bf16[2,16,1152]{2,1,0:T(8,128)(2,1)S(1)}, bf16[2,16,1152]{2,1,0:T(8,128)(2,1)S(1)}, u32[]{:S(2)}, u32[]{:S(2)}) collective-permute-start(bf16[2,16,1152]{2,1,0:T(8,128)(2,1)S(1)} %shard_map.77), channel_id=1, source_target_pairs={{0,0},{1,1},{2,32},{3,33},{4,64},{5,65},{6,96},{7,97},{8,128},{9,1... | collective-permute-start | bytes 221192 | tf_op jit(solution)/shard_map/ppermute | solution.py:266
  11.5 18.1 %copy-start.1 = (f32[2,8,2048]{2,1,0:T(8,128)S(1)}, f32[2,8,2048]{2,1,0:T(8,128)}, u32[]{:S(2)}) copy-start(f32[2,8,2048]{2,1,0:T(8,128)} %ref_ref.1) | copy-start | bytes 393220
  11.5 18.1 %copy-start.3 = (s32[8]{0:T(128)S(1)}, s32[8]{0:T(128)}, u32[]{:S(2)}) copy-start(s32[8]{0:T(128)} %param.10) | copy-start | bytes 100
  11.5 23.3 %copy-start.5 = (s32[12,2]{0,1:T(2,128)S(1)}, s32[12,2]{0,1:T(2,128)}, u32[]{:S(2)}) copy-start(s32[12,2]{0,1:T(2,128)} %param.9) | copy-start | bytes 292
  11.5 45.4 %all-to-all-start = ((bf16[16,2,16,1152]{3,2,1,0:T(8,128)(2,1)}), bf16[16,2,16,1152]{3,2,1,0:T(8,128)(2,1)S(1)}, u32[]{:S(2)}, u32[]{:S(2)}) async-start(bf16[16,2,16,1152]{3,2,1,0:T(8,128)(2,1)} %broadcast_in_dim.26), calls=%async_computation | async-start | bytes 2359296 | tf_op jit(solution)/shard_map/all_to_all | solution.py:259
  29.7 60.3 %copy-start.4 = (f32[4]{0:T(128)S(1)}, f32[4]{0:T(128)}, u32[]{:S(2)}) copy-start(f32[4]{0:T(128)} %prior_ref.1) | copy-start | bytes 52
  29.7 19.0 %collective-permute-start.1 = (bf16[2,8,2176]{2,1,0:T(8,128)(2,1)S(1)}, bf16[2,8,2176]{2,1,0:T(8,128)(2,1)S(1)}, u32[]{:S(2)}, u32[]{:S(2)}) collective-permute-start(bf16[2,8,2176]{2,1,0:T(8,128)(2,1)S(1)} %shard_map.78.ref0_ref), channel_id=1, source_target_pairs={{0,16},{16,0},{1,17},{17,1},{2,18},{18,2},{3,19},{19,3},{4,20},{20... | collective-permute-start | bytes 208904 | tf_op jit(solution)/shard_map/ppermute | solution.py:269
  58.4 31.6 %all-to-all-start.1 = ((f32[16,8,256]{2,1,0:T(8,128)}), f32[16,8,256]{2,1,0:T(8,128)S(1)}, u32[]{:S(2)}, u32[]{:S(2)}) async-start(f32[16,8,256]{2,1,0:T(8,128)} %shard_map.79), calls=%async_computation.1 | async-start | bytes 262144 | tf_op jit(solution)/shard_map/all_to_all | solution.py:259
  106.5 20.0 %all-to-all-start.3 = ((bf16[16,8,256]{2,1,0:T(8,128)(2,1)}), bf16[16,8,256]{2,1,0:T(8,128)(2,1)S(1)}, u32[]{:S(2)}, u32[]{:S(2)}) async-start(bf16[16,8,256]{2,1,0:T(8,128)(2,1)} %shard_map.81), calls=%async_computation.3 | async-start | bytes 131072 | tf_op jit(solution)/shard_map/all_to_all | solution.py:259
  127.5 14.1 %collective-permute-start.2 = (bf16[2,8,2176]{2,1,0:T(8,128)(2,1)S(1)}, bf16[2,8,2176]{2,1,0:T(8,128)(2,1)S(1)}, u32[]{:S(2)}, u32[]{:S(2)}) collective-permute-start(bf16[2,8,2176]{2,1,0:T(8,128)(2,1)S(1)} %get-tuple-element.9), channel_id=1, source_target_pairs={{0,16},{16,0},{1,17},{17,1},{2,18},{18,2},{3,19},{19,3},{4,20},{20... | collective-permute-start | bytes 208904 | tf_op jit(solution)/shard_map/ppermute | solution.py:293

commit v8 on v6

--- a/solution.py
+++ b/solution.py
@@ -98,6 +98,10 @@
     label = jnp.broadcast_to(label, (8, LANES)).astype(jnp.bfloat16)
     out_ref[0, :, PIXELS:] = label
     out_ref[1, :, PIXELS:] = label
+
+
+def joined(own_ref, other_ref, h, part):
+    return jnp.concatenate([ref[:, h, part, :, :HALF].reshape(64, HALF) for ref in (own_ref, other_ref)], axis=0)
 
 
 def cross_kernel(own_ref, other_ref, ref0_ref, ref1_ref, cos_ref, sin_ref, zh_ref, c_ref, out_ref, shifted):
@@ -121,19 +125,20 @@
         spare = slice(e * LANES + USED, (e + 1) * LANES)
         shifted[:, spare, :] = jnp.zeros((2, LANES - USED, PIXELS), jnp.bfloat16)
     half = jnp.concatenate(halves, axis=1)
-    for img_ref, chip in ((own_ref, c_ref[0]), (other_ref, 1 - c_ref[0])):
-        total = jnp.zeros((64, 2 * LANES), jnp.float32)
-        for h in range(2):
-            for part in range(2):
-                total += lax.dot_general(
-                    img_ref[:, h, part, :, :HALF].reshape(64, HALF),
-                    shifted[part, :, h * HALF : (h + 1) * HALF],
-                    (((1,), (1,)), ((), ())),
-                    preferred_element_type=jnp.float32,
-                )
-        pieces = img_ref[:, 0, 0, :, HALF:].reshape(64, LANES).astype(jnp.float32)
-        precision = jnp.sum(pieces, axis=1, keepdims=True)
-        out_ref[pl.ds(chip * 8, 8)] = (precision * (total - half)).reshape(8, 8, 2 * LANES)
+    total = jnp.zeros((128, 2 * LANES), jnp.float32)
+    for h in range(2):
+        for part in range(2):
+            total += lax.dot_general(
+                joined(own_ref, other_ref, h, part),
+                shifted[part, :, h * HALF : (h + 1) * HALF],
+                (((1,), (1,)), ((), ())),
+                preferred_element_type=jnp.float32,
+            )
+    pieces = [ref[:, 0, 0, :, HALF:].reshape(64, LANES).astype(jnp.float32) for ref in (own_ref, other_ref)]
+    precision = jnp.sum(jnp.concatenate(pieces, axis=0), axis=1, keepdims=True)
+    scaled = (precision * (total - half)).reshape(16, 8, 2 * LANES)
+    out_ref[pl.ds(c_ref[0] * 8, 8)] = scaled[:8]
+    out_ref[pl.ds((1 - c_ref[0]) * 8, 8)] = scaled[8:]
 
 
 def label_rows(ref0_ref, ref1_ref, straight):
@@ -187,22 +192,14 @@
 def back_kernel(got_ref, own_ref, other_ref, cos_ref, sin_ref, zh_ref, c_ref, out0_ref, out1_ref):
     straight = zh_ref[0] == 0
     extra = jnp.sum(got_ref[...].astype(jnp.float32), axis=0)
-    sides = []
-    for img_ref, chip in ((own_ref, c_ref[0]), (other_ref, 1 - c_ref[0])):
-        post = got_ref[pl.ds(chip * 8, 8)].astype(jnp.float32).reshape(64, 2 * LANES)
-        post = jnp.where(iota((64, 2 * LANES), 1) % LANES < USED, post, 0.0)
-        sides.append((img_ref, jnp.transpose(post).astype(jnp.bfloat16)))
+    halves = [got_ref[pl.ds(chip * 8, 8)].astype(jnp.float32) for chip in (c_ref[0], 1 - c_ref[0])]
+    post = jnp.concatenate(halves, axis=0).reshape(128, 2 * LANES)
+    post = jnp.where(iota((128, 2 * LANES), 1) % LANES < USED, post, 0.0)
+    weights = jnp.transpose(post).astype(jnp.bfloat16)
     for h in range(2):
         cols = slice(h * HALF, (h + 1) * HALF)
         back = [
-            sum(
-                jnp.dot(
-                    weights,
-                    img_ref[:, h, part, :, :HALF].reshape(64, HALF),
-                    preferred_element_type=jnp.float32,
-                )
-                for img_ref, weights in sides
-            )
+            jnp.dot(weights, joined(own_ref, other_ref, h, part), preferred_element_type=jnp.float32)
             for part in range(2)
         ]
         sums = [jnp.zeros((8, HALF), jnp.float32) for both in range(4)]
@@ -239,7 +236,7 @@
         out_ref[part] = both / (mass + 1.0)
 
 
-def call(kernel, shapes, args, scratch=(), scalars=0):
+def call(kernel, shapes, args, scratch=(), scalars=0, room=32):
     in_vmem = [pl.BlockSpec(memory_space=pltpu.VMEM)] * (len(args) - scalars)
     in_smem = [pl.BlockSpec(memory_space=pltpu.SMEM)] * scalars
     out = [jax.ShapeDtypeStruct(shape, dtype) for shape, dtype in shapes]
@@ -249,7 +246,7 @@
         in_specs=in_vmem + in_smem,
         out_specs=[pl.BlockSpec(memory_space=pltpu.VMEM)] * len(out),
         scratch_shapes=list(scratch),
-        compiler_params=pltpu.CompilerParams(vmem_limit_bytes=32 << 20),
+        compiler_params=pltpu.CompilerParams(vmem_limit_bytes=room << 20),
     )(*args)
 
 
@@ -260,7 +257,7 @@
 def local(images, references, precision, shifts, labels, log_prior):
     y, zh, c, zl, xh, xl = (lax.axis_index(name) for name in ALL)
     half = zh.astype(jnp.int32)[None]
-    (sent,) = call(image_kernel, [((8, 2, 16, HALF + LANES), jnp.bfloat16)], (images, precision[None]))
+    (sent,) = call(image_kernel, [((8, 2, 16, HALF + LANES), jnp.bfloat16)], (images, precision[None]), room=60)
     own = swap(sent, NEAR).reshape(4, 2, 2, 16, HALF + LANES)
     other = lax.ppermute(own, "c", [(0, 1), (1, 0)])
     core = c.astype(jnp.int32)[None]

time: 121 us -> 119 us (0.983)
  local copies, waits for them, and re-layouts: 2.32 us -> 0.77 us
    unnamed x12 -> x8, local copies, waits for them, and re-layouts: 2.21 us -> 0.66 us
where the time goes in v8:
time: 119 us; the launch traced here: 118 us
  starting transfers between devices  53.3 us (45%)
  waiting for transfers between devices  41.8 us (35%)
  blocking collectives  13.6 us (11%)
  Pallas kernels  6.86 us (6%)
  other arithmetic  1.24 us (1%)
    all_to_all x3, waiting for transfers between devices, swap(): return lax.all_to_all(operand, axes, 0, 0, tiled=True)  22 us
    ppermute x2, starting transfers between devices, local(): refs = [lax.ppermute(low, ALL, route) for route in routes(True)]  18.3 us
    all_to_all x3, starting transfers between devices, swap(): return lax.all_to_all(operand, axes, 0, 0, tiled=True)  18.2 us
    all_to_all x1, blocking collectives, swap(): return lax.all_to_all(operand, axes, 0, 0, tiled=True)  13.6 us
    ppermute x2, starting transfers between devices, local(): lax.ppermute(part, ALL, route)  12.5 us
    ppermute x2, waiting for transfers between devices, local(): lax.ppermute(part, ALL, route)  12.3 us
    ppermute x2, waiting for transfers between devices, local(): refs = [lax.ppermute(low, ALL, route) for route in routes(True)]  7.51 us
    pallas_call x7, Pallas kernels, call(): pl.pallas_call(kernel, out_shape=out, in_specs=in_vmem + in_smem, out_spe...  6.86 us
  transfers between devices with their start and end apart: 8, of which 4 were waited for; matrix products, arithmetic and copies ran while one was open for 1% of the time, Pallas kernels for 0%

profile of v8, /device:TPU:33, one launch (start us, length us, event | category | flops | bytes accessed | tf_op | source)
XLA Modules:
  0.0 118.4 jit_solution(16963284751403955292)
XLA Ops:
  0.6 1.8 %shard_map.77 = bf16[8,2,16,1152]{3,2,1,0:T(8,128)(2,1)} custom-call(f32[2,16,1024]{2,1,0:T(8,128)} %img_ref.1, f32[1,16]{1,0:T(1,128)} %bitcast.17), custom_call_target="tpu_custom_call" | custom-call | tf_op jit(solution)/shard_map/pallas_call | solution.py:243
  2.5 0.0 copy-start
  2.5 5.2 %all-to-all-start = ((bf16[8,2,16,1152]{3,2,1,0:T(8,128)(2,1)}), bf16[8,2,16,1152]{3,2,1,0:T(8,128)(2,1)S(1)}, u32[]{:S(2)}, u32[]{:S(2)}) async-start(bf16[8,2,16,1152]{3,2,1,0:T(8,128)(2,1)} %shard_map.77), calls=%async_computation | async-start | bytes 1179648 | tf_op jit(solution)/shard_map/all_to_all | solution.py:254
  7.7 0.0 copy-start.1
  7.7 0.0 copy-done
  7.7 0.6 copy-done.1
  8.4 0.1 shard_map.78
  8.4 0.0 copy-start.3
  8.5 16.4 %collective-permute-start.2 = (bf16[2,8,2176]{2,1,0:T(8,128)(2,1)S(1)}, bf16[2,8,2176]{2,1,0:T(8,128)(2,1)S(1)}, u32[]{:S(2)}, u32[]{:S(2)}) collective-permute-start(bf16[2,8,2176]{2,1,0:T(8,128)(2,1)S(1)} %shard_map.78), channel_id=1, source_target_pairs={{2,0},{3,1},{34,2},{35,3},{66,4},{67,5},{98,6},{99,7},{130,8},{131... | collective-permute-start | bytes 208904 | tf_op jit(solution)/shard_map/ppermute | solution.py:265
  24.8 1.9 %collective-permute-start.1 = (bf16[2,8,2176]{2,1,0:T(8,128)(2,1)S(1)}, bf16[2,8,2176]{2,1,0:T(8,128)(2,1)S(1)}, u32[]{:S(2)}, u32[]{:S(2)}) collective-permute-start(bf16[2,8,2176]{2,1,0:T(8,128)(2,1)S(1)} %shard_map.78), channel_id=1, source_target_pairs={{0,0},{1,1},{32,2},{33,3},{64,4},{65,5},{96,6},{97,7},{128,8},{129... | collective-permute-start | bytes 208904 | tf_op jit(solution)/shard_map/ppermute | solution.py:265
  26.8 0.0 all-to-all-done
  26.8 4.3 %collective-permute-start = (bf16[4,2,2,16,1152]{4,3,2,1,0:T(8,128)(2,1)S(1)}, bf16[4,2,2,16,1152]{4,3,2,1,0:T(8,128)(2,1)S(1)}, u32[]{:S(2)}, u32[]{:S(2)}) collective-permute-start(bf16[4,2,2,16,1152]{4,3,2,1,0:T(8,128)(2,1)S(1)} %bitcast.13), channel_id=1, source_target_pairs={{0,32},{32,0},{1,33},{33,1},{2,34},{34,2},{3,35},{35,3},{4,36},{36... | collective-permute-start | bytes 1769480 | tf_op jit(solution)/shard_map/ppermute | solution.py:262
  31.1 0.0 copy-done.3
  31.1 0.6 fusion
  31.7 0.0 collective-permute-done.2.ref1_ref
  31.7 7.5 %collective-permute-done.1.ref0_ref = bf16[2,8,2176]{2,1,0:T(8,128)(2,1)S(1)} collective-permute-done((bf16[2,8,2176]{2,1,0:T(8,128)(2,1)S(1)}, bf16[2,8,2176]{2,1,0:T(8,128)(2,1)S(1)}, u32[]{:S(2)}, u32[]{:S(2)}) %collective-permute-start.1) | collective-permute-done | bytes 69664 | tf_op jit(solution)/shard_map/ppermute | solution.py:265
  39.2 0.0 collective-permute-done.other_ref
  39.2 1.5 %shard_map.79 = f32[16,8,256]{2,1,0:T(8,128)} custom-call(bf16[4,2,2,16,1152]{4,3,2,1,0:T(8,128)(2,1)S(1)} %bitcast.14, bf16[4,2,2,16,1152]{4,3,2,1,0:T(8,128)(2,1)S(1)} %collective-permute-done.other_ref, bf16[2,8,2176]{2,1,0:T(8,128)(2,1)S(1)} %collective-permute-done.1.ref0_ref, bf16[2,8,2176]{2,1,0:T(8,128)(2,1)S(1)} %collective-permute-done.2.ref1_ref, ...), custom_call_target="tpu_custom_call" | custom-call | tf_op jit(solution)/shard_map/pallas_call | solution.py:243
  40.8 8.0 %all-to-all-start.1 = ((f32[16,8,256]{2,1,0:T(8,128)}), f32[16,8,256]{2,1,0:T(8,128)S(1)}, u32[]{:S(2)}, u32[]{:S(2)}) async-start(f32[16,8,256]{2,1,0:T(8,128)} %shard_map.79), calls=%async_computation.1 | async-start | bytes 262144 | tf_op jit(solution)/shard_map/all_to_all | solution.py:254
  48.8 0.0 copy-start.2
  48.9 11.1 %all-to-all-done.1.got_ref = f32[16,8,256]{2,1,0:T(8,128)S(1)} async-done(((f32[16,8,256]{2,1,0:T(8,128)}), f32[16,8,256]{2,1,0:T(8,128)S(1)}, u32[]{:S(2)}, u32[]{:S(2)}) %all-to-all-start.1) | async-done | bytes 131104 | tf_op jit(solution)/shard_map/all_to_all | solution.py:254
  60.0 0.0 copy-done.2
  60.0 0.7 shard_map.80
  60.7 13.6 %all_to_all.20.got_ref = f32[16,8,128]{2,1,0:T(8,128)S(1)} all-to-all(f32[16,8,128]{2,1,0:T(8,128)S(1)} %get-tuple-element.6), channel_id=1, replica_groups=mesh['y'=4,'zh'=2,'c'=2,'zl'=8,'xh'=2,'xl'=2] {'y','c','xl'}, dimensions={0} | all-to-all | bytes 131072 | tf_op jit(solution)/shard_map/all_to_all | solution.py:254
  74.3 0.9 shard_map.81
  75.2 4.9 %all-to-all-start.3 = ((bf16[16,8,256]{2,1,0:T(8,128)(2,1)}), bf16[16,8,256]{2,1,0:T(8,128)(2,1)S(1)}, u32[]{:S(2)}, u32[]{:S(2)}) async-start(bf16[16,8,256]{2,1,0:T(8,128)(2,1)} %shard_map.81), calls=%async_computation.3 | async-start | bytes 131072 | tf_op jit(solution)/shard_map/all_to_all | solution.py:254
  80.1 10.9 %all-to-all-done.3.got_ref = bf16[16,8,256]{2,1,0:T(8,128)(2,1)S(1)} async-done(((bf16[16,8,256]{2,1,0:T(8,128)(2,1)}), bf16[16,8,256]{2,1,0:T(8,128)(2,1)S(1)}, u32[]{:S(2)}, u32[]{:S(2)}) %all-to-all-start.3) | async-done | bytes 65568 | tf_op jit(solution)/shard_map/all_to_all | solution.py:254
  91.0 1.0 shard_map.82
  92.0 10.3 %collective-permute-start.3 = (bf16[2,8,2176]{2,1,0:T(8,128)(2,1)S(1)}, bf16[2,8,2176]{2,1,0:T(8,128)(2,1)S(1)}, u32[]{:S(2)}, u32[]{:S(2)}) collective-permute-start(bf16[2,8,2176]{2,1,0:T(8,128)(2,1)S(1)} %get-tuple-element.8), channel_id=1, source_target_pairs={{0,0},{1,1},{2,32},{3,33},{4,64},{5,65},{6,96},{7,97},{8,128},{9,1... | collective-permute-start | bytes 208904 | tf_op jit(solution)/shard_map/ppermute | solution.py:289
  102.4 2.2 %collective-permute-start.4 = (bf16[2,8,2176]{2,1,0:T(8,128)(2,1)S(1)}, bf16[2,8,2176]{2,1,0:T(8,128)(2,1)S(1)}, u32[]{:S(2)}, u32[]{:S(2)}) collective-permute-start(bf16[2,8,2176]{2,1,0:T(8,128)(2,1)S(1)} %get-tuple-element.9), channel_id=1, source_target_pairs={{0,2},{1,3},{2,34},{3,35},{4,66},{5,67},{6,98},{7,99},{8,130},{9,1... | collective-permute-start | bytes 208904 | tf_op jit(solution)/shard_map/ppermute | solution.py:289
  104.6 0.1 slice_convert_fusion
  104.7 0.1 copy.8
  104.8 0.6 reduce_sum.9
  105.4 0.0 collective-permute-done.3.first_ref
  105.4 12.3 %collective-permute-done.4.second_ref = bf16[2,8,2176]{2,1,0:T(8,128)(2,1)S(1)} collective-permute-done((bf16[2,8,2176]{2,1,0:T(8,128)(2,1)S(1)}, bf16[2,8,2176]{2,1,0:T(8,128)(2,1)S(1)}, u32[]{:S(2)}, u32[]{:S(2)}) %collective-permute-start.4) | collective-permute-done | bytes 69664 | tf_op jit(solution)/shard_map/ppermute | solution.py:289
  117.6 0.8 shard_map.83
  (6 shorter events, 0.0 us)
Async XLA Ops:
  2.5 5.3 %copy-start = (f32[2,8,2048]{2,1,0:T(8,128)S(1)}, f32[2,8,2048]{2,1,0:T(8,128)}, u32[]{:S(2)}) copy-start(f32[2,8,2048]{2,1,0:T(8,128)} %ref_ref.1) | copy-start | bytes 393220
  2.5 24.3 %all-to-all-start = ((bf16[8,2,16,1152]{3,2,1,0:T(8,128)(2,1)}), bf16[8,2,16,1152]{3,2,1,0:T(8,128)(2,1)S(1)}, u32[]{:S(2)}, u32[]{:S(2)}) async-start(bf16[8,2,16,1152]{3,2,1,0:T(8,128)(2,1)} %shard_map.77), calls=%async_computation | async-start | bytes 1179648 | tf_op jit(solution)/shard_map/all_to_all | solution.py:254
  7.7 0.7 copy-start.1
  8.4 22.6 %copy-start.3 = (s32[12,2]{0,1:T(2,128)S(1)}, s32[12,2]{0,1:T(2,128)}, u32[]{:S(2)}) copy-start(s32[12,2]{0,1:T(2,128)} %param.9) | copy-start | bytes 292
  8.5 23.3 %collective-permute-start.2 = (bf16[2,8,2176]{2,1,0:T(8,128)(2,1)S(1)}, bf16[2,8,2176]{2,1,0:T(8,128)(2,1)S(1)}, u32[]{:S(2)}, u32[]{:S(2)}) collective-permute-start(bf16[2,8,2176]{2,1,0:T(8,128)(2,1)S(1)} %shard_map.78), channel_id=1, source_target_pairs={{2,0},{3,1},{34,2},{35,3},{66,4},{67,5},{98,6},{99,7},{130,8},{131... | collective-permute-start | bytes 208904 | tf_op jit(solution)/shard_map/ppermute | solution.py:265
  24.8 14.4 %collective-permute-start.1 = (bf16[2,8,2176]{2,1,0:T(8,128)(2,1)S(1)}, bf16[2,8,2176]{2,1,0:T(8,128)(2,1)S(1)}, u32[]{:S(2)}, u32[]{:S(2)}) collective-permute-start(bf16[2,8,2176]{2,1,0:T(8,128)(2,1)S(1)} %shard_map.78), channel_id=1, source_target_pairs={{0,0},{1,1},{32,2},{33,3},{64,4},{65,5},{96,6},{97,7},{128,8},{129... | collective-permute-start | bytes 208904 | tf_op jit(solution)/shard_map/ppermute | solution.py:265
  26.8 12.5 %collective-permute-start = (bf16[4,2,2,16,1152]{4,3,2,1,0:T(8,128)(2,1)S(1)}, bf16[4,2,2,16,1152]{4,3,2,1,0:T(8,128)(2,1)S(1)}, u32[]{:S(2)}, u32[]{:S(2)}) collective-permute-start(bf16[4,2,2,16,1152]{4,3,2,1,0:T(8,128)(2,1)S(1)} %bitcast.13), channel_id=1, source_target_pairs={{0,32},{32,0},{1,33},{33,1},{2,34},{34,2},{3,35},{35,3},{4,36},{36... | collective-permute-start | bytes 1769480 | tf_op jit(solution)/shard_map/ppermute | solution.py:262
  40.8 19.2 %all-to-all-start.1 = ((f32[16,8,256]{2,1,0:T(8,128)}), f32[16,8,256]{2,1,0:T(8,128)S(1)}, u32[]{:S(2)}, u32[]{:S(2)}) async-start(f32[16,8,256]{2,1,0:T(8,128)} %shard_map.79), calls=%async_computation.1 | async-start | bytes 262144 | tf_op jit(solution)/shard_map/all_to_all | solution.py:254
  48.8 11.2 %copy-start.2 = (f32[4]{0:T(128)S(1)}, f32[4]{0:T(128)}, u32[]{:S(2)}) copy-start(f32[4]{0:T(128)} %prior_ref.1) | copy-start | bytes 52
  75.2 15.8 %all-to-all-start.3 = ((bf16[16,8,256]{2,1,0:T(8,128)(2,1)}), bf16[16,8,256]{2,1,0:T(8,128)(2,1)S(1)}, u32[]{:S(2)}, u32[]{:S(2)}) async-start(bf16[16,8,256]{2,1,0:T(8,128)(2,1)} %shard_map.81), calls=%async_computation.3 | async-start | bytes 131072 | tf_op jit(solution)/shard_map/all_to_all | solution.py:254
  92.0 13.3 %collective-permute-start.3 = (bf16[2,8,2176]{2,1,0:T(8,128)(2,1)S(1)}, bf16[2,8,2176]{2,1,0:T(8,128)(2,1)S(1)}, u32[]{:S(2)}, u32[]{:S(2)}) collective-permute-start(bf16[2,8,2176]{2,1,0:T(8,128)(2,1)S(1)} %get-tuple-element.8), channel_id=1, source_target_pairs={{0,0},{1,1},{2,32},{3,33},{4,64},{5,65},{6,96},{7,97},{8,128},{9,1... | collective-permute-start | bytes 208904 | tf_op jit(solution)/shard_map/ppermute | solution.py:289
  102.4 15.3 %collective-permute-start.4 = (bf16[2,8,2176]{2,1,0:T(8,128)(2,1)S(1)}, bf16[2,8,2176]{2,1,0:T(8,128)(2,1)S(1)}, u32[]{:S(2)}, u32[]{:S(2)}) collective-permute-start(bf16[2,8,2176]{2,1,0:T(8,128)(2,1)S(1)} %get-tuple-element.9), channel_id=1, source_target_pairs={{0,2},{1,3},{2,34},{3,35},{4,66},{5,67},{6,98},{7,99},{8,130},{9,1... | collective-permute-start | bytes 208904 | tf_op jit(solution)/shard_map/ppermute | solution.py:289

commit v9 on v8

--- a/solution.py
+++ b/solution.py
@@ -23,9 +23,9 @@
 ALL = tuple(SIZES)
 IMG = ("y", "zh", "c")
 REF = ("zl", "xh", "xl")
-SPACE = ("y", "c", "xl")
-NEAR = ("y", "xl")
-BLOCK = ("zl", "xh")
+SPACE = ("y", "xh", "xl")
+SWAP = [(0, 1), (1, 0)]
+BLOCK = ("zl", "c")
 
 
 def place(*coords):
@@ -41,7 +41,7 @@
         pairs = []
         for y, zh, c, zl, xh, xl in itertools.product(*(range(size) for size in SIZES.values())):
             work = place(y, zh, c, zl, xh, xl)
-            home = place(zl // 2, zl % 2, xh, 2 * y + c, r ^ zh, xl)
+            home = place(zl // 2, zl % 2, c, 2 * y + (r ^ zh), xh, xl)
             pairs.append((home, work) if inward else (work, home))
         made.append(pairs)
     return made
@@ -85,7 +85,7 @@
     lane = iota((16, LANES), 1)
     pieces = jnp.where(lane == 0, first, jnp.where(lane == 1, second, jnp.where(lane == 2, third, 0.0)))
     pieces = pieces.astype(jnp.bfloat16)
-    for copy in range(8):
+    for copy in range(16):
         out_ref[copy, :, :, :HALF] = low
         out_ref[copy, 0, :, HALF:] = pieces
         out_ref[copy, 1, :, HALF:] = pieces
@@ -257,14 +257,16 @@
 def local(images, references, precision, shifts, labels, log_prior):
     y, zh, c, zl, xh, xl = (lax.axis_index(name) for name in ALL)
     half = zh.astype(jnp.int32)[None]
-    (sent,) = call(image_kernel, [((8, 2, 16, HALF + LANES), jnp.bfloat16)], (images, precision[None]), room=60)
-    own = swap(sent, NEAR).reshape(4, 2, 2, 16, HALF + LANES)
-    other = lax.ppermute(own, "c", [(0, 1), (1, 0)])
+    (sent,) = call(image_kernel, [((16, 2, 16, HALF + LANES), jnp.bfloat16)], (images, precision[None]), room=60)
+    units = swap(sent, SPACE).reshape(4, 2, 2, 2, 16, HALF + LANES)
+    own = lax.dynamic_index_in_dim(units, c, 1, keepdims=False)
+    other = lax.dynamic_index_in_dim(units, 1 - c, 1, keepdims=False)
+    other = lax.ppermute(other, "c", SWAP)
     core = c.astype(jnp.int32)[None]
     (low,) = call(ref_kernel, [((2, 8, PIXELS + LANES), jnp.bfloat16)], (references, labels[None]))
     refs = [lax.ppermute(low, ALL, route) for route in routes(True)]
     tags = [ref[:1, :, PIXELS:] for ref in refs]
-    cosine, sine = phases(shifts, zl * 2 + xh)
+    cosine, sine = phases(shifts, zl * 2 + c)
     (cross,) = call(
         cross_kernel,
         [((16, 8, 2 * LANES), jnp.float32)],

time: 119 us -> 115 us (0.966)
  the two profiles are of different devices: /device:TPU:33 before, /device:TPU:25 now
where the time goes in v9:
time: 115 us; the launch traced here: 114 us
  starting transfers between devices  56.8 us (49%)
  waiting for transfers between devices  37.5 us (33%)
  blocking collectives  10.6 us (9%)
  Pallas kernels  7.1 us (6%)
  other arithmetic  1.24 us (1%)
    all_to_all x3, starting transfers between devices, swap(): return lax.all_to_all(operand, axes, 0, 0, tiled=True)  28.2 us
    all_to_all x3, waiting for transfers between devices, swap(): return lax.all_to_all(operand, axes, 0, 0, tiled=True)  23.2 us
    ppermute x2, starting transfers between devices, local(): refs = [lax.ppermute(low, ALL, route) for route in routes(True)]  13.3 us
    all_to_all x1, blocking collectives, swap(): return lax.all_to_all(operand, axes, 0, 0, tiled=True)  10.6 us
    ppermute x2, starting transfers between devices, local(): lax.ppermute(part, ALL, route)  10.3 us
    ppermute x2, waiting for transfers between devices, local(): lax.ppermute(part, ALL, route)  9.37 us
    pallas_call x7, Pallas kernels, call(): pl.pallas_call(kernel, out_shape=out, in_specs=in_vmem + in_smem, out_spe...  7.1 us
    ppermute x1, starting transfers between devices, local(): other = lax.ppermute(other, 'c', SWAP)  5.01 us
  transfers between devices with their start and end apart: 8, of which 6 were waited for; matrix products, arithmetic and copies ran while one was open for 1% of the time, Pallas kernels for 0%

profile of v9, /device:TPU:25, one launch (start us, length us, event | category | flops | bytes accessed | tf_op | source)
XLA Modules:
  0.0 114.2 jit_solution(15657323022296827948)
XLA Ops:
  0.6 2.1 %shard_map.77 = bf16[16,2,16,1152]{3,2,1,0:T(8,128)(2,1)} custom-call(f32[2,16,1024]{2,1,0:T(8,128)} %img_ref.1, f32[1,16]{1,0:T(1,128)} %bitcast.23), custom_call_target="tpu_custom_call" | custom-call | tf_op jit(solution)/shard_map/pallas_call | solution.py:243
  2.7 0.0 copy-start
  2.7 0.0 copy-start.1
  2.7 6.7 %all-to-all-start = ((bf16[16,2,16,1152]{3,2,1,0:T(8,128)(2,1)}), bf16[16,2,16,1152]{3,2,1,0:T(8,128)(2,1)S(1)}, u32[]{:S(2)}, u32[]{:S(2)}) async-start(bf16[16,2,16,1152]{3,2,1,0:T(8,128)(2,1)} %shard_map.77), calls=%async_computation | async-start | bytes 2359296 | tf_op jit(solution)/shard_map/all_to_all | solution.py:254
  9.4 0.0 copy-done
  9.5 0.0 copy-done.1
  9.5 0.1 shard_map.78
  9.5 11.3 %collective-permute-start.1 = (bf16[2,8,2176]{2,1,0:T(8,128)(2,1)S(1)}, bf16[2,8,2176]{2,1,0:T(8,128)(2,1)S(1)}, u32[]{:S(2)}, u32[]{:S(2)}) collective-permute-start(bf16[2,8,2176]{2,1,0:T(8,128)(2,1)S(1)} %shard_map.78), channel_id=1, source_target_pairs={{0,0},{1,1},{2,2},{3,3},{64,4},{65,5},{66,6},{67,7},{128,8},{129,9... | collective-permute-start | bytes 208904 | tf_op jit(solution)/shard_map/ppermute | solution.py:267
  20.9 2.0 %collective-permute-start.2 = (bf16[2,8,2176]{2,1,0:T(8,128)(2,1)S(1)}, bf16[2,8,2176]{2,1,0:T(8,128)(2,1)S(1)}, u32[]{:S(2)}, u32[]{:S(2)}) collective-permute-start(bf16[2,8,2176]{2,1,0:T(8,128)(2,1)S(1)} %shard_map.78), channel_id=1, source_target_pairs={{4,0},{5,1},{6,2},{7,3},{68,4},{69,5},{70,6},{71,7},{132,8},{133,9... | collective-permute-start | bytes 208904 | tf_op jit(solution)/shard_map/ppermute | solution.py:267
  22.9 1.2 %all-to-all-done = bf16[16,2,16,1152]{3,2,1,0:T(8,128)(2,1)S(1)} async-done(((bf16[16,2,16,1152]{3,2,1,0:T(8,128)(2,1)}), bf16[16,2,16,1152]{3,2,1,0:T(8,128)(2,1)S(1)}, u32[]{:S(2)}, u32[]{:S(2)}) %all-to-all-start) | async-done | bytes 1179680 | tf_op jit(solution)/shard_map/all_to_all | solution.py:254
  24.0 0.0 copy-start.3
  24.0 0.1 dynamic-slice_bitcast_fusion
  24.1 0.0 copy-start.2
  24.1 5.0 %collective-permute-start = (bf16[4,2,2,16,1152]{4,3,2,1,0:T(8,128)(2,1)S(1)}, bf16[4,2,2,16,1152]{4,3,2,1,0:T(8,128)(2,1)S(1)}, u32[]{:S(2)}, u32[]{:S(2)}) collective-permute-start(bf16[4,2,2,16,1152]{4,3,2,1,0:T(8,128)(2,1)S(1)} %get-tuple-element.10), channel_id=1, source_target_pairs={{0,32},{32,0},{1,33},{33,1},{2,34},{34,2},{3,35},{35,3},{4,36},{36... | collective-permute-start | bytes 1769480 | tf_op jit(solution)/shard_map/ppermute | solution.py:264
  29.1 0.0 copy-done.3
  29.2 0.6 fusion
  29.8 0.0 collective-permute-done.1.ref0_ref
  29.8 4.9 %collective-permute-done.2.ref1_ref = bf16[2,8,2176]{2,1,0:T(8,128)(2,1)S(1)} collective-permute-done((bf16[2,8,2176]{2,1,0:T(8,128)(2,1)S(1)}, bf16[2,8,2176]{2,1,0:T(8,128)(2,1)S(1)}, u32[]{:S(2)}, u32[]{:S(2)}) %collective-permute-start.2) | collective-permute-done | bytes 69664 | tf_op jit(solution)/shard_map/ppermute | solution.py:267
  34.6 0.0 collective-permute-done.other_ref
  34.7 1.5 %shard_map.79 = f32[16,8,256]{2,1,0:T(8,128)} custom-call(bf16[4,2,2,16,1152]{4,3,2,1,0:T(8,128)(2,1)S(1)} %get-tuple-element.11.own_ref, bf16[4,2,2,16,1152]{4,3,2,1,0:T(8,128)(2,1)S(1)} %collective-permute-done.other_ref, bf16[2,8,2176]{2,1,0:T(8,128)(2,1)S(1)} %collective-permute-done.1.ref0_ref, bf16[2,8,2176]{2,1,0:T(8,128)(2,1)S(1)} %collective-permute-done.2.ref1_ref, ...), custom_call_target="tpu_custom_call" | custom-call | tf_op jit(solution)/shard_map/pallas_call | solution.py:243
  36.2 15.1 %all-to-all-start.1 = ((f32[16,8,256]{2,1,0:T(8,128)}), f32[16,8,256]{2,1,0:T(8,128)S(1)}, u32[]{:S(2)}, u32[]{:S(2)}) async-start(f32[16,8,256]{2,1,0:T(8,128)} %shard_map.79), calls=%async_computation.1 | async-start | bytes 262144 | tf_op jit(solution)/shard_map/all_to_all | solution.py:254
  51.3 12.0 %all-to-all-done.1.got_ref = f32[16,8,256]{2,1,0:T(8,128)S(1)} async-done(((f32[16,8,256]{2,1,0:T(8,128)}), f32[16,8,256]{2,1,0:T(8,128)S(1)}, u32[]{:S(2)}, u32[]{:S(2)}) %all-to-all-start.1) | async-done | bytes 131104 | tf_op jit(solution)/shard_map/all_to_all | solution.py:254
  63.3 0.0 copy-done.2
  63.3 0.7 shard_map.80
  64.1 10.6 %all_to_all.20.got_ref = f32[16,8,128]{2,1,0:T(8,128)S(1)} all-to-all(f32[16,8,128]{2,1,0:T(8,128)S(1)} %get-tuple-element.6), channel_id=1, replica_groups=mesh['y'=4,'zh'=2,'c'=2,'zl'=8,'xh'=2,'xl'=2] {'y','xh','xl'}, dimensions={0} | all-to-all | bytes 131072 | tf_op jit(solution)/shard_map/all_to_all | solution.py:254
  74.7 0.9 shard_map.81
  75.6 6.4 %all-to-all-start.3 = ((bf16[16,8,256]{2,1,0:T(8,128)(2,1)}), bf16[16,8,256]{2,1,0:T(8,128)(2,1)S(1)}, u32[]{:S(2)}, u32[]{:S(2)}) async-start(bf16[16,8,256]{2,1,0:T(8,128)(2,1)} %shard_map.81), calls=%async_computation.3 | async-start | bytes 131072 | tf_op jit(solution)/shard_map/all_to_all | solution.py:254
  82.0 10.1 %all-to-all-done.3.got_ref = bf16[16,8,256]{2,1,0:T(8,128)(2,1)S(1)} async-done(((bf16[16,8,256]{2,1,0:T(8,128)(2,1)}), bf16[16,8,256]{2,1,0:T(8,128)(2,1)S(1)}, u32[]{:S(2)}, u32[]{:S(2)}) %all-to-all-start.3) | async-done | bytes 65568 | tf_op jit(solution)/shard_map/all_to_all | solution.py:254
  92.0 1.0 shard_map.82
  93.0 4.5 %collective-permute-start.3 = (bf16[2,8,2176]{2,1,0:T(8,128)(2,1)S(1)}, bf16[2,8,2176]{2,1,0:T(8,128)(2,1)S(1)}, u32[]{:S(2)}, u32[]{:S(2)}) collective-permute-start(bf16[2,8,2176]{2,1,0:T(8,128)(2,1)S(1)} %get-tuple-element.8), channel_id=1, source_target_pairs={{0,0},{1,1},{2,2},{3,3},{4,64},{5,65},{6,66},{7,67},{8,128},{9,129... | collective-permute-start | bytes 208904 | tf_op jit(solution)/shard_map/ppermute | solution.py:291
  97.6 5.7 %collective-permute-start.4 = (bf16[2,8,2176]{2,1,0:T(8,128)(2,1)S(1)}, bf16[2,8,2176]{2,1,0:T(8,128)(2,1)S(1)}, u32[]{:S(2)}, u32[]{:S(2)}) collective-permute-start(bf16[2,8,2176]{2,1,0:T(8,128)(2,1)S(1)} %get-tuple-element.9), channel_id=1, source_target_pairs={{0,4},{1,5},{2,6},{3,7},{4,68},{5,69},{6,70},{7,71},{8,132},{9,133... | collective-permute-start | bytes 208904 | tf_op jit(solution)/shard_map/ppermute | solution.py:291
  103.3 0.1 slice_convert_fusion
  103.4 0.1 copy.14
  103.5 0.6 reduce_sum.9
  104.1 2.0 %collective-permute-done.3.first_ref = bf16[2,8,2176]{2,1,0:T(8,128)(2,1)S(1)} collective-permute-done((bf16[2,8,2176]{2,1,0:T(8,128)(2,1)S(1)}, bf16[2,8,2176]{2,1,0:T(8,128)(2,1)S(1)}, u32[]{:S(2)}, u32[]{:S(2)}) %collective-permute-start.3) | collective-permute-done | bytes 69664 | tf_op jit(solution)/shard_map/ppermute | solution.py:291
  106.1 7.4 %collective-permute-done.4.second_ref = bf16[2,8,2176]{2,1,0:T(8,128)(2,1)S(1)} collective-permute-done((bf16[2,8,2176]{2,1,0:T(8,128)(2,1)S(1)}, bf16[2,8,2176]{2,1,0:T(8,128)(2,1)S(1)}, u32[]{:S(2)}, u32[]{:S(2)}) %collective-permute-start.4) | collective-permute-done | bytes 69664 | tf_op jit(solution)/shard_map/ppermute | solution.py:291
  113.5 0.8 shard_map.83
  (6 shorter events, 0.0 us)
Async XLA Ops:
  2.7 6.7 %copy-start = (f32[2,8,2048]{2,1,0:T(8,128)S(1)}, f32[2,8,2048]{2,1,0:T(8,128)}, u32[]{:S(2)}) copy-start(f32[2,8,2048]{2,1,0:T(8,128)} %ref_ref.1) | copy-start | bytes 393220
  2.7 6.8 %copy-start.1 = (s32[8]{0:T(128)S(1)}, s32[8]{0:T(128)}, u32[]{:S(2)}) copy-start(s32[8]{0:T(128)} %param.10) | copy-start | bytes 100
  2.7 21.3 %all-to-all-start = ((bf16[16,2,16,1152]{3,2,1,0:T(8,128)(2,1)}), bf16[16,2,16,1152]{3,2,1,0:T(8,128)(2,1)S(1)}, u32[]{:S(2)}, u32[]{:S(2)}) async-start(bf16[16,2,16,1152]{3,2,1,0:T(8,128)(2,1)} %shard_map.77), calls=%async_computation | async-start | bytes 2359296 | tf_op jit(solution)/shard_map/all_to_all | solution.py:254
  9.5 20.2 %collective-permute-start.1 = (bf16[2,8,2176]{2,1,0:T(8,128)(2,1)S(1)}, bf16[2,8,2176]{2,1,0:T(8,128)(2,1)S(1)}, u32[]{:S(2)}, u32[]{:S(2)}) collective-permute-start(bf16[2,8,2176]{2,1,0:T(8,128)(2,1)S(1)} %shard_map.78), channel_id=1, source_target_pairs={{0,0},{1,1},{2,2},{3,3},{64,4},{65,5},{66,6},{67,7},{128,8},{129,9... | collective-permute-start | bytes 208904 | tf_op jit(solution)/shard_map/ppermute | solution.py:267
  20.9 13.8 %collective-permute-start.2 = (bf16[2,8,2176]{2,1,0:T(8,128)(2,1)S(1)}, bf16[2,8,2176]{2,1,0:T(8,128)(2,1)S(1)}, u32[]{:S(2)}, u32[]{:S(2)}) collective-permute-start(bf16[2,8,2176]{2,1,0:T(8,128)(2,1)S(1)} %shard_map.78), channel_id=1, source_target_pairs={{4,0},{5,1},{6,2},{7,3},{68,4},{69,5},{70,6},{71,7},{132,8},{133,9... | collective-permute-start | bytes 208904 | tf_op jit(solution)/shard_map/ppermute | solution.py:267
  24.0 5.1 %copy-start.3 = (s32[12,2]{0,1:T(2,128)S(1)}, s32[12,2]{0,1:T(2,128)}, u32[]{:S(2)}) copy-start(s32[12,2]{0,1:T(2,128)} %param.9) | copy-start | bytes 292
  24.1 39.2 %copy-start.2 = (f32[4]{0:T(128)S(1)}, f32[4]{0:T(128)}, u32[]{:S(2)}) copy-start(f32[4]{0:T(128)} %prior_ref.1) | copy-start | bytes 52
  24.1 10.5 %collective-permute-start = (bf16[4,2,2,16,1152]{4,3,2,1,0:T(8,128)(2,1)S(1)}, bf16[4,2,2,16,1152]{4,3,2,1,0:T(8,128)(2,1)S(1)}, u32[]{:S(2)}, u32[]{:S(2)}) collective-permute-start(bf16[4,2,2,16,1152]{4,3,2,1,0:T(8,128)(2,1)S(1)} %get-tuple-element.10), channel_id=1, source_target_pairs={{0,32},{32,0},{1,33},{33,1},{2,34},{34,2},{3,35},{35,3},{4,36},{36... | collective-permute-start | bytes 1769480 | tf_op jit(solution)/shard_map/ppermute | solution.py:264
  36.2 27.1 %all-to-all-start.1 = ((f32[16,8,256]{2,1,0:T(8,128)}), f32[16,8,256]{2,1,0:T(8,128)S(1)}, u32[]{:S(2)}, u32[]{:S(2)}) async-start(f32[16,8,256]{2,1,0:T(8,128)} %shard_map.79), calls=%async_computation.1 | async-start | bytes 262144 | tf_op jit(solution)/shard_map/all_to_all | solution.py:254
  75.6 16.4 %all-to-all-start.3 = ((bf16[16,8,256]{2,1,0:T(8,128)(2,1)}), bf16[16,8,256]{2,1,0:T(8,128)(2,1)S(1)}, u32[]{:S(2)}, u32[]{:S(2)}) async-start(bf16[16,8,256]{2,1,0:T(8,128)(2,1)} %shard_map.81), calls=%async_computation.3 | async-start | bytes 131072 | tf_op jit(solution)/shard_map/all_to_all | solution.py:254
  93.0 13.1 %collective-permute-start.3 = (bf16[2,8,2176]{2,1,0:T(8,128)(2,1)S(1)}, bf16[2,8,2176]{2,1,0:T(8,128)(2,1)S(1)}, u32[]{:S(2)}, u32[]{:S(2)}) collective-permute-start(bf16[2,8,2176]{2,1,0:T(8,128)(2,1)S(1)} %get-tuple-element.8), channel_id=1, source_target_pairs={{0,0},{1,1},{2,2},{3,3},{4,64},{5,65},{6,66},{7,67},{8,128},{9,129... | collective-permute-start | bytes 208904 | tf_op jit(solution)/shard_map/ppermute | solution.py:291
  97.6 15.9 %collective-permute-start.4 = (bf16[2,8,2176]{2,1,0:T(8,128)(2,1)S(1)}, bf16[2,8,2176]{2,1,0:T(8,128)(2,1)S(1)}, u32[]{:S(2)}, u32[]{:S(2)}) collective-permute-start(bf16[2,8,2176]{2,1,0:T(8,128)(2,1)S(1)} %get-tuple-element.9), channel_id=1, source_target_pairs={{0,4},{1,5},{2,6},{3,7},{4,68},{5,69},{6,70},{7,71},{8,132},{9,133... | collective-permute-start | bytes 208904 | tf_op jit(solution)/shard_map/ppermute | solution.py:291

commit v10 on v9

--- a/solution.py
+++ b/solution.py
@@ -104,52 +104,52 @@
     return jnp.concatenate([ref[:, h, part, :, :HALF].reshape(64, HALF) for ref in (own_ref, other_ref)], axis=0)
 
 
-def cross_kernel(own_ref, other_ref, ref0_ref, ref1_ref, cos_ref, sin_ref, zh_ref, c_ref, out_ref, shifted):
-    straight = zh_ref[0] == 0
-    ref0 = ref0_ref[:, :, :PIXELS].astype(jnp.float32)
-    ref1 = ref1_ref[:, :, :PIXELS].astype(jnp.float32)
-    halves = []
-    for e in range(2):
-        ref = jnp.where(straight, ref0, ref1) if e == 0 else jnp.where(straight, ref1, ref0)
-        re, im = ref[0], ref[1]
-        halves.append(as_row(0.5 * jnp.sum(re * re + im * im, axis=1, keepdims=True)))
-        for pair in range(SHIFTS // 2):
-            rot_re, rot_im = [], []
-            for t in (2 * pair, 2 * pair + 1):
-                cos, sin = cos_ref[t : t + 1, :], sin_ref[t : t + 1, :]
-                rot_re.append(re * cos + im * sin)
-                rot_im.append(im * cos - re * sin)
-            rows = slice(e * LANES + 16 * pair, e * LANES + 16 * pair + 16)
-            shifted[0, rows, :] = jnp.concatenate(rot_re, axis=0).astype(jnp.bfloat16)
-            shifted[1, rows, :] = jnp.concatenate(rot_im, axis=0).astype(jnp.bfloat16)
-        spare = slice(e * LANES + USED, (e + 1) * LANES)
-        shifted[:, spare, :] = jnp.zeros((2, LANES - USED, PIXELS), jnp.bfloat16)
-    half = jnp.concatenate(halves, axis=1)
+def rotate_kernel(ref_ref, cos_ref, sin_ref, shifted, row_ref):
+    re = ref_ref[0, :, :PIXELS].astype(jnp.float32)
+    im = ref_ref[1, :, :PIXELS].astype(jnp.float32)
+    row_ref[0:1, :] = as_row(0.5 * jnp.sum(re * re + im * im, axis=1, keepdims=True))
+    row_ref[1:2, :] = as_row(ref_ref[0, :, PIXELS:].astype(jnp.float32))
+    for pair in range(SHIFTS // 2):
+        rot_re, rot_im = [], []
+        for t in (2 * pair, 2 * pair + 1):
+            cos, sin = cos_ref[t : t + 1, :], sin_ref[t : t + 1, :]
+            rot_re.append(re * cos + im * sin)
+            rot_im.append(im * cos - re * sin)
+        rows = slice(16 * pair, 16 * pair + 16)
+        shifted[0, rows, :] = jnp.concatenate(rot_re, axis=0).astype(jnp.bfloat16)
+        shifted[1, rows, :] = jnp.concatenate(rot_im, axis=0).astype(jnp.bfloat16)
+    shifted[:, USED:, :] = jnp.zeros((2, LANES - USED, PIXELS), jnp.bfloat16)
+
+
+def cross_kernel(own_ref, other_ref, first_ref, second_ref, row0_ref, row1_ref, zh_ref, c_ref, out_ref):
     total = jnp.zeros((128, 2 * LANES), jnp.float32)
     for h in range(2):
+        cols = slice(h * HALF, (h + 1) * HALF)
         for part in range(2):
             total += lax.dot_general(
                 joined(own_ref, other_ref, h, part),
-                shifted[part, :, h * HALF : (h + 1) * HALF],
+                jnp.concatenate([first_ref[part, :, cols], second_ref[part, :, cols]], axis=0),
                 (((1,), (1,)), ((), ())),
                 preferred_element_type=jnp.float32,
             )
+    total -= jnp.concatenate([row0_ref[0:1, :], row1_ref[0:1, :]], axis=1)
     pieces = [ref[:, 0, 0, :, HALF:].reshape(64, LANES).astype(jnp.float32) for ref in (own_ref, other_ref)]
     precision = jnp.sum(jnp.concatenate(pieces, axis=0), axis=1, keepdims=True)
-    scaled = (precision * (total - half)).reshape(16, 8, 2 * LANES)
-    out_ref[pl.ds(c_ref[0] * 8, 8)] = scaled[:8]
-    out_ref[pl.ds((1 - c_ref[0]) * 8, 8)] = scaled[8:]
-
-
-def label_rows(ref0_ref, ref1_ref, straight):
-    first = ref0_ref[0].astype(jnp.float32)
-    second = ref1_ref[0].astype(jnp.float32)
-    low, high = jnp.where(straight, first, second), jnp.where(straight, second, first)
-    return jnp.concatenate([as_row(low), as_row(high)], axis=1)
-
-
-def score_kernel(got_ref, ref0_ref, ref1_ref, prior_ref, zh_ref, score_ref, out_ref):
-    labels = label_rows(ref0_ref, ref1_ref, zh_ref[0] == 0)
+    scaled = precision * total
+    straight = zh_ref[0] == 0
+    left, right = scaled[:, :LANES], scaled[:, LANES:]
+    sides = [jnp.where(straight, left, right), jnp.where(straight, right, left)]
+    for e in range(2):
+        side = sides[e].reshape(16, 8, LANES)
+        lanes = slice(e * LANES, (e + 1) * LANES)
+        out_ref[pl.ds(c_ref[0] * 8, 8), :, lanes] = side[:8]
+        out_ref[pl.ds((1 - c_ref[0]) * 8, 8), :, lanes] = side[8:]
+
+
+def score_kernel(got_ref, row0_ref, row1_ref, prior_ref, zh_ref, score_ref, out_ref):
+    straight = zh_ref[0] == 0
+    first, second = row0_ref[1:2, :], row1_ref[1:2, :]
+    labels = jnp.concatenate([jnp.where(straight, first, second), jnp.where(straight, second, first)], axis=1)
     prior = jnp.zeros((1, 2 * LANES), jnp.float32)
     for k in range(CLASSES):
         prior = jnp.where(labels == k, prior_ref[k], prior)
@@ -236,7 +236,7 @@
         out_ref[part] = both / (mass + 1.0)
 
 
-def call(kernel, shapes, args, scratch=(), scalars=0, room=32):
+def call(kernel, shapes, args, scratch=(), scalars=0, room=12):
     in_vmem = [pl.BlockSpec(memory_space=pltpu.VMEM)] * (len(args) - scalars)
     in_smem = [pl.BlockSpec(memory_space=pltpu.SMEM)] * scalars
     out = [jax.ShapeDtypeStruct(shape, dtype) for shape, dtype in shapes]
@@ -265,19 +265,28 @@
     core = c.astype(jnp.int32)[None]
     (low,) = call(ref_kernel, [((2, 8, PIXELS + LANES), jnp.bfloat16)], (references, labels[None]))
     refs = [lax.ppermute(low, ALL, route) for route in routes(True)]
-    tags = [ref[:1, :, PIXELS:] for ref in refs]
     cosine, sine = phases(shifts, zl * 2 + c)
+    rotated = [
+        call(
+            rotate_kernel,
+            [((2, LANES, PIXELS), jnp.bfloat16), ((2, LANES), jnp.float32)],
+            (ref, cosine, sine),
+            room=8,
+        )
+        for ref in refs
+    ]
+    (first, row0), (second, row1) = rotated
     (cross,) = call(
         cross_kernel,
         [((16, 8, 2 * LANES), jnp.float32)],
-        (own, other, *refs, cosine, sine, half, core),
-        [pltpu.VMEM((2, 2 * LANES, PIXELS), jnp.bfloat16)],
+        (own, other, first, second, row0, row1, half, core),
         scalars=2,
+        room=16,
     )
     scores, stats = call(
         score_kernel,
         [((8, 2 * LANES), jnp.float32), ((16, 8, LANES), jnp.float32)],
-        (swap(cross, BLOCK), *tags, log_prior, half),
+        (swap(cross, BLOCK), row0, row1, log_prior, half),
         scalars=2,
     )
     (post,) = call(post_kernel, [((16, 8, 2 * LANES), jnp.bfloat16)], (swap(stats, SPACE), scores))

time: 115 us -> 114 us (level)
  blocking collectives: 10.6 us -> 37.5 us
  starting transfers between devices: 56.8 us -> 41.3 us
  waiting for transfers between devices: 37.5 us -> 25.5 us
    all_to_all x1 -> x2, blocking collectives: 10.6 us -> 37.5 us  [swap(): return lax.all_to_all(operand, axes, 0, 0, tiled=True)]
    all_to_all x3 -> x2, starting transfers between devices: 28.2 us -> 13.1 us  [swap(): return lax.all_to_all(operand, axes, 0, 0, tiled=True)]
    all_to_all x3 -> x2, waiting for transfers between devices: 23.2 us -> 11.2 us  [swap(): return lax.all_to_all(operand, axes, 0, 0, tiled=True)]
    pallas_call x7 -> x9, Pallas kernels: 7.1 us -> 7.14 us  [call(): pl.pallas_call(kernel, out_shape=out, in_specs=in_vmem + in_smem, out_spe...]
  transfers between devices with their start and end apart: 8 -> 7, of which waited for: 6 -> 5; matrix products, arithmetic and copies ran while one was open for 1% -> 1% of each run, Pallas kernels for 0% -> 1%
where the time goes in v10:
time: 114 us
  starting transfers between devices  41.3 us (36%)
  blocking collectives  37.5 us (33%)
  waiting for transfers between devices  25.5 us (22%)
  Pallas kernels  7.14 us (6%)
  other arithmetic  1.24 us (1%)
    all_to_all x2, blocking collectives, swap(): return lax.all_to_all(operand, axes, 0, 0, tiled=True)  37.5 us
    ppermute x2, starting transfers between devices, local(): refs = [lax.ppermute(low, ALL, route) for route in routes(True)]  13.3 us
    all_to_all x2, starting transfers between devices, swap(): return lax.all_to_all(operand, axes, 0, 0, tiled=True)  13.1 us
    all_to_all x2, waiting for transfers between devices, swap(): return lax.all_to_all(operand, axes, 0, 0, tiled=True)  11.2 us
    ppermute x2, starting transfers between devices, local(): lax.ppermute(part, ALL, route)  9.86 us
    ppermute x2, waiting for transfers between devices, local(): lax.ppermute(part, ALL, route)  9.77 us
    pallas_call x9, Pallas kernels, call(): pl.pallas_call(kernel, out_shape=out, in_specs=in_vmem + in_smem, out_spe...  7.14 us
    ppermute x1, starting transfers between devices, local(): other = lax.ppermute(other, 'c', SWAP)  5.01 us
  transfers between devices with their start and end apart: 7, of which 5 were waited for; matrix products, arithmetic and copies ran while one was open for 1% of the time, Pallas kernels for 1%

profile of v10, /device:TPU:25, one launch (start us, length us, event | category | flops | bytes accessed | tf_op | source)
XLA Modules:
  0.0 113.7 jit_solution(9980226126462118574)
XLA Ops:
  0.6 2.1 %shard_map.77 = bf16[16,2,16,1152]{3,2,1,0:T(8,128)(2,1)} custom-call(f32[2,16,1024]{2,1,0:T(8,128)} %img_ref.1, f32[1,16]{1,0:T(1,128)} %bitcast.23), custom_call_target="tpu_custom_call" | custom-call | tf_op jit(solution)/shard_map/pallas_call | solution.py:243
  2.7 0.0 copy-start
  2.7 0.0 copy-start.1
  2.7 6.7 %all-to-all-start = ((bf16[16,2,16,1152]{3,2,1,0:T(8,128)(2,1)}), bf16[16,2,16,1152]{3,2,1,0:T(8,128)(2,1)S(1)}, u32[]{:S(2)}, u32[]{:S(2)}) async-start(bf16[16,2,16,1152]{3,2,1,0:T(8,128)(2,1)} %shard_map.77), calls=%async_computation | async-start | bytes 2359296 | tf_op jit(solution)/shard_map/all_to_all | solution.py:254
  9.4 0.0 copy-done
  9.5 0.0 copy-done.1
  9.5 0.1 shard_map.78
  9.5 11.3 %collective-permute-start.1 = (bf16[2,8,2176]{2,1,0:T(8,128)(2,1)S(1)}, bf16[2,8,2176]{2,1,0:T(8,128)(2,1)S(1)}, u32[]{:S(2)}, u32[]{:S(2)}) collective-permute-start(bf16[2,8,2176]{2,1,0:T(8,128)(2,1)S(1)} %shard_map.78), channel_id=1, source_target_pairs={{0,0},{1,1},{2,2},{3,3},{64,4},{65,5},{66,6},{67,7},{128,8},{129,9... | collective-permute-start | bytes 208904 | tf_op jit(solution)/shard_map/ppermute | solution.py:267
  20.9 2.0 %collective-permute-start.2 = (bf16[2,8,2176]{2,1,0:T(8,128)(2,1)S(1)}, bf16[2,8,2176]{2,1,0:T(8,128)(2,1)S(1)}, u32[]{:S(2)}, u32[]{:S(2)}) collective-permute-start(bf16[2,8,2176]{2,1,0:T(8,128)(2,1)S(1)} %shard_map.78), channel_id=1, source_target_pairs={{4,0},{5,1},{6,2},{7,3},{68,4},{69,5},{70,6},{71,7},{132,8},{133,9... | collective-permute-start | bytes 208904 | tf_op jit(solution)/shard_map/ppermute | solution.py:267
  22.9 1.2 %all-to-all-done = bf16[16,2,16,1152]{3,2,1,0:T(8,128)(2,1)S(1)} async-done(((bf16[16,2,16,1152]{3,2,1,0:T(8,128)(2,1)}), bf16[16,2,16,1152]{3,2,1,0:T(8,128)(2,1)S(1)}, u32[]{:S(2)}, u32[]{:S(2)}) %all-to-all-start) | async-done | bytes 1179680 | tf_op jit(solution)/shard_map/all_to_all | solution.py:254
  24.0 0.0 copy-start.3
  24.0 0.1 dynamic-slice_bitcast_fusion
  24.1 5.0 %collective-permute-start = (bf16[4,2,2,16,1152]{4,3,2,1,0:T(8,128)(2,1)S(1)}, bf16[4,2,2,16,1152]{4,3,2,1,0:T(8,128)(2,1)S(1)}, u32[]{:S(2)}, u32[]{:S(2)}) collective-permute-start(bf16[4,2,2,16,1152]{4,3,2,1,0:T(8,128)(2,1)S(1)} %get-tuple-element.18), channel_id=1, source_target_pairs={{0,32},{32,0},{1,33},{33,1},{2,34},{34,2},{3,35},{35,3},{4,36},{36... | collective-permute-start | bytes 1769480 | tf_op jit(solution)/shard_map/ppermute | solution.py:264
  29.1 0.0 copy-done.3
  29.2 0.6 fusion
  29.7 0.0 collective-permute-done.1.ref_ref
  29.8 0.4 shard_map.79
  30.1 4.5 %collective-permute-done.2.ref_ref = bf16[2,8,2176]{2,1,0:T(8,128)(2,1)S(1)} collective-permute-done((bf16[2,8,2176]{2,1,0:T(8,128)(2,1)S(1)}, bf16[2,8,2176]{2,1,0:T(8,128)(2,1)S(1)}, u32[]{:S(2)}, u32[]{:S(2)}) %collective-permute-start.2) | collective-permute-done | bytes 69664 | tf_op jit(solution)/shard_map/ppermute | solution.py:267
  34.6 0.4 shard_map.80
  35.0 0.0 collective-permute-done.other_ref
  35.0 0.0 copy-start.2
  35.0 0.9 shard_map.81
  35.9 26.9 %all_to_all.20.got_ref = f32[16,8,256]{2,1,0:T(8,128)S(1)} all-to-all(f32[16,8,256]{2,1,0:T(8,128)S(1)} %shard_map.81), channel_id=1, replica_groups=mesh['y'=4,'zh'=2,'c'=2,'zl'=8,'xh'=2,'xl'=2] {'zl','c'}, dimensions={0} | all-to-all | bytes 262144 | tf_op jit(solution)/shard_map/all_to_all | solution.py:254
  62.8 0.0 copy-done.2
  62.8 0.7 shard_map.82
  63.6 10.6 %all_to_all.21.got_ref = f32[16,8,128]{2,1,0:T(8,128)S(1)} all-to-all(f32[16,8,128]{2,1,0:T(8,128)S(1)} %get-tuple-element.14), channel_id=1, replica_groups=mesh['y'=4,'zh'=2,'c'=2,'zl'=8,'xh'=2,'xl'=2] {'y','xh','xl'}, dimensions={0} | all-to-all | bytes 131072 | tf_op jit(solution)/shard_map/all_to_all | solution.py:254
  74.2 0.9 shard_map.83
  75.1 6.4 %all-to-all-start.3 = ((bf16[16,8,256]{2,1,0:T(8,128)(2,1)}), bf16[16,8,256]{2,1,0:T(8,128)(2,1)S(1)}, u32[]{:S(2)}, u32[]{:S(2)}) async-start(bf16[16,8,256]{2,1,0:T(8,128)(2,1)} %shard_map.83), calls=%async_computation.3 | async-start | bytes 131072 | tf_op jit(solution)/shard_map/all_to_all | solution.py:254
  81.5 10.1 %all-to-all-done.3.got_ref = bf16[16,8,256]{2,1,0:T(8,128)(2,1)S(1)} async-done(((bf16[16,8,256]{2,1,0:T(8,128)(2,1)}), bf16[16,8,256]{2,1,0:T(8,128)(2,1)S(1)}, u32[]{:S(2)}, u32[]{:S(2)}) %all-to-all-start.3) | async-done | bytes 65568 | tf_op jit(solution)/shard_map/all_to_all | solution.py:254
  91.5 1.0 shard_map.84
  92.5 4.5 %collective-permute-start.3 = (bf16[2,8,2176]{2,1,0:T(8,128)(2,1)S(1)}, bf16[2,8,2176]{2,1,0:T(8,128)(2,1)S(1)}, u32[]{:S(2)}, u32[]{:S(2)}) collective-permute-start(bf16[2,8,2176]{2,1,0:T(8,128)(2,1)S(1)} %get-tuple-element.16), channel_id=1, source_target_pairs={{0,0},{1,1},{2,2},{3,3},{4,64},{5,65},{6,66},{7,67},{8,128},{9,129... | collective-permute-start | bytes 208904 | tf_op jit(solution)/shard_map/ppermute | solution.py:300
  97.1 5.3 %collective-permute-start.4 = (bf16[2,8,2176]{2,1,0:T(8,128)(2,1)S(1)}, bf16[2,8,2176]{2,1,0:T(8,128)(2,1)S(1)}, u32[]{:S(2)}, u32[]{:S(2)}) collective-permute-start(bf16[2,8,2176]{2,1,0:T(8,128)(2,1)S(1)} %get-tuple-element.17), channel_id=1, source_target_pairs={{0,4},{1,5},{2,6},{3,7},{4,68},{5,69},{6,70},{7,71},{8,132},{9,133... | collective-permute-start | bytes 208904 | tf_op jit(solution)/shard_map/ppermute | solution.py:300
  102.4 0.1 slice_convert_fusion
  102.5 0.1 copy.14
  102.6 0.6 reduce_sum.9
  103.2 2.4 %collective-permute-done.3.first_ref = bf16[2,8,2176]{2,1,0:T(8,128)(2,1)S(1)} collective-permute-done((bf16[2,8,2176]{2,1,0:T(8,128)(2,1)S(1)}, bf16[2,8,2176]{2,1,0:T(8,128)(2,1)S(1)}, u32[]{:S(2)}, u32[]{:S(2)}) %collective-permute-start.3) | collective-permute-done | bytes 69664 | tf_op jit(solution)/shard_map/ppermute | solution.py:300
  105.6 7.4 %collective-permute-done.4.second_ref = bf16[2,8,2176]{2,1,0:T(8,128)(2,1)S(1)} collective-permute-done((bf16[2,8,2176]{2,1,0:T(8,128)(2,1)S(1)}, bf16[2,8,2176]{2,1,0:T(8,128)(2,1)S(1)}, u32[]{:S(2)}, u32[]{:S(2)}) %collective-permute-start.4) | collective-permute-done | bytes 69664 | tf_op jit(solution)/shard_map/ppermute | solution.py:300
  113.0 0.8 shard_map.85
  (4 shorter events, 0.0 us)
Async XLA Ops:
  2.7 6.7 %copy-start = (f32[2,8,2048]{2,1,0:T(8,128)S(1)}, f32[2,8,2048]{2,1,0:T(8,128)}, u32[]{:S(2)}) copy-start(f32[2,8,2048]{2,1,0:T(8,128)} %ref_ref.1) | copy-start | bytes 393220
  2.7 6.8 %copy-start.1 = (s32[8]{0:T(128)S(1)}, s32[8]{0:T(128)}, u32[]{:S(2)}) copy-start(s32[8]{0:T(128)} %param.10) | copy-start | bytes 100
  2.7 21.3 %all-to-all-start = ((bf16[16,2,16,1152]{3,2,1,0:T(8,128)(2,1)}), bf16[16,2,16,1152]{3,2,1,0:T(8,128)(2,1)S(1)}, u32[]{:S(2)}, u32[]{:S(2)}) async-start(bf16[16,2,16,1152]{3,2,1,0:T(8,128)(2,1)} %shard_map.77), calls=%async_computation | async-start | bytes 2359296 | tf_op jit(solution)/shard_map/all_to_all | solution.py:254
  9.5 20.2 %collective-permute-start.1 = (bf16[2,8,2176]{2,1,0:T(8,128)(2,1)S(1)}, bf16[2,8,2176]{2,1,0:T(8,128)(2,1)S(1)}, u32[]{:S(2)}, u32[]{:S(2)}) collective-permute-start(bf16[2,8,2176]{2,1,0:T(8,128)(2,1)S(1)} %shard_map.78), channel_id=1, source_target_pairs={{0,0},{1,1},{2,2},{3,3},{64,4},{65,5},{66,6},{67,7},{128,8},{129,9... | collective-permute-start | bytes 208904 | tf_op jit(solution)/shard_map/ppermute | solution.py:267
  20.9 13.8 %collective-permute-start.2 = (bf16[2,8,2176]{2,1,0:T(8,128)(2,1)S(1)}, bf16[2,8,2176]{2,1,0:T(8,128)(2,1)S(1)}, u32[]{:S(2)}, u32[]{:S(2)}) collective-permute-start(bf16[2,8,2176]{2,1,0:T(8,128)(2,1)S(1)} %shard_map.78), channel_id=1, source_target_pairs={{4,0},{5,1},{6,2},{7,3},{68,4},{69,5},{70,6},{71,7},{132,8},{133,9... | collective-permute-start | bytes 208904 | tf_op jit(solution)/shard_map/ppermute | solution.py:267
  24.0 5.1 %copy-start.3 = (s32[12,2]{0,1:T(2,128)S(1)}, s32[12,2]{0,1:T(2,128)}, u32[]{:S(2)}) copy-start(s32[12,2]{0,1:T(2,128)} %param.9) | copy-start | bytes 292
  24.1 10.9 %collective-permute-start = (bf16[4,2,2,16,1152]{4,3,2,1,0:T(8,128)(2,1)S(1)}, bf16[4,2,2,16,1152]{4,3,2,1,0:T(8,128)(2,1)S(1)}, u32[]{:S(2)}, u32[]{:S(2)}) collective-permute-start(bf16[4,2,2,16,1152]{4,3,2,1,0:T(8,128)(2,1)S(1)} %get-tuple-element.18), channel_id=1, source_target_pairs={{0,32},{32,0},{1,33},{33,1},{2,34},{34,2},{3,35},{35,3},{4,36},{36... | collective-permute-start | bytes 1769480 | tf_op jit(solution)/shard_map/ppermute | solution.py:264
  35.0 27.8 %copy-start.2 = (f32[4]{0:T(128)S(1)}, f32[4]{0:T(128)}, u32[]{:S(2)}) copy-start(f32[4]{0:T(128)} %prior_ref.1) | copy-start | bytes 52
  75.1 16.4 %all-to-all-start.3 = ((bf16[16,8,256]{2,1,0:T(8,128)(2,1)}), bf16[16,8,256]{2,1,0:T(8,128)(2,1)S(1)}, u32[]{:S(2)}, u32[]{:S(2)}) async-start(bf16[16,8,256]{2,1,0:T(8,128)(2,1)} %shard_map.83), calls=%async_computation.3 | async-start | bytes 131072 | tf_op jit(solution)/shard_map/all_to_all | solution.py:254
  92.5 13.1 %collective-permute-start.3 = (bf16[2,8,2176]{2,1,0:T(8,128)(2,1)S(1)}, bf16[2,8,2176]{2,1,0:T(8,128)(2,1)S(1)}, u32[]{:S(2)}, u32[]{:S(2)}) collective-permute-start(bf16[2,8,2176]{2,1,0:T(8,128)(2,1)S(1)} %get-tuple-element.16), channel_id=1, source_target_pairs={{0,0},{1,1},{2,2},{3,3},{4,64},{5,65},{6,66},{7,67},{8,128},{9,129... | collective-permute-start | bytes 208904 | tf_op jit(solution)/shard_map/ppermute | solution.py:300
  97.1 15.9 %collective-permute-start.4 = (bf16[2,8,2176]{2,1,0:T(8,128)(2,1)S(1)}, bf16[2,8,2176]{2,1,0:T(8,128)(2,1)S(1)}, u32[]{:S(2)}, u32[]{:S(2)}) collective-permute-start(bf16[2,8,2176]{2,1,0:T(8,128)(2,1)S(1)} %get-tuple-element.17), channel_id=1, source_target_pairs={{0,4},{1,5},{2,6},{3,7},{4,68},{5,69},{6,70},{7,71},{8,132},{9,133... | collective-permute-start | bytes 208904 | tf_op jit(solution)/shard_map/ppermute | solution.py:300

commit v11 on v10

--- a/solution.py
+++ b/solution.py
@@ -76,7 +76,7 @@
     return first, second, value - first - second
 
 
-def image_kernel(img_ref, precision_ref, out_ref):
+def image_kernel(img_ref, precision_ref, out_hbm, block, sems):
     low = img_ref[...].astype(jnp.bfloat16)
     precision = jnp.sum(
         jnp.where(iota((16, 16), 0) == iota((16, 16), 1), precision_ref[...], 0.0), axis=1, keepdims=True
@@ -85,10 +85,14 @@
     lane = iota((16, LANES), 1)
     pieces = jnp.where(lane == 0, first, jnp.where(lane == 1, second, jnp.where(lane == 2, third, 0.0)))
     pieces = pieces.astype(jnp.bfloat16)
-    for copy in range(16):
-        out_ref[copy, :, :, :HALF] = low
-        out_ref[copy, 0, :, HALF:] = pieces
-        out_ref[copy, 1, :, HALF:] = pieces
+    block[:, :, :HALF] = low
+    block[0, :, HALF:] = pieces
+    block[1, :, HALF:] = pieces
+    copies = [pltpu.make_async_copy(block, out_hbm.at[slot], sems.at[slot]) for slot in range(16)]
+    for copy in copies:
+        copy.start()
+    for copy in copies:
+        copy.wait()
 
 
 def ref_kernel(ref_ref, label_ref, out_ref):
@@ -236,7 +240,7 @@
         out_ref[part] = both / (mass + 1.0)
 
 
-def call(kernel, shapes, args, scratch=(), scalars=0, room=12):
+def call(kernel, shapes, args, scratch=(), scalars=0, room=12, out_space=pltpu.VMEM):
     in_vmem = [pl.BlockSpec(memory_space=pltpu.VMEM)] * (len(args) - scalars)
     in_smem = [pl.BlockSpec(memory_space=pltpu.SMEM)] * scalars
     out = [jax.ShapeDtypeStruct(shape, dtype) for shape, dtype in shapes]
@@ -244,7 +248,7 @@
         kernel,
         out_shape=out,
         in_specs=in_vmem + in_smem,
-        out_specs=[pl.BlockSpec(memory_space=pltpu.VMEM)] * len(out),
+        out_specs=[pl.BlockSpec(memory_space=out_space)] * len(out),
         scratch_shapes=list(scratch),
         compiler_params=pltpu.CompilerParams(vmem_limit_bytes=room << 20),
     )(*args)
@@ -257,7 +261,14 @@
 def local(images, references, precision, shifts, labels, log_prior):
     y, zh, c, zl, xh, xl = (lax.axis_index(name) for name in ALL)
     half = zh.astype(jnp.int32)[None]
-    (sent,) = call(image_kernel, [((16, 2, 16, HALF + LANES), jnp.bfloat16)], (images, precision[None]), room=60)
+    (sent,) = call(
+        image_kernel,
+        [((16, 2, 16, HALF + LANES), jnp.bfloat16)],
+        (images, precision[None]),
+        [pltpu.VMEM((2, 16, HALF + LANES), jnp.bfloat16), pltpu.SemaphoreType.DMA((16,))],
+        room=60,
+        out_space=pl.ANY,
+    )
     units = swap(sent, SPACE).reshape(4, 2, 2, 2, 16, HALF + LANES)
     own = lax.dynamic_index_in_dim(units, c, 1, keepdims=False)
     other = lax.dynamic_index_in_dim(units, 1 - c, 1, keepdims=False)
@@ -289,7 +300,7 @@
         (swap(cross, BLOCK), row0, row1, log_prior, half),
         scalars=2,
     )
-    (post,) = call(post_kernel, [((16, 8, 2 * LANES), jnp.bfloat16)], (swap(stats, SPACE), scores))
+    (post,) = call(post_kernel, [((16, 8, 2 * LANES), jnp.bfloat16)], (swap(stats, SPACE), scores), room=8)
     posts = swap(post, BLOCK)
     partial = call(
         back_kernel,

time: 114 us -> 114 us (level)
  no operation moved by 1% of the time
where the time goes in v11:
time: 114 us
  starting transfers between devices  41.3 us (36%)
  blocking collectives  37.5 us (33%)
  waiting for transfers between devices  25.5 us (22%)
  Pallas kernels  7.27 us (6%)
  other arithmetic  1.24 us (1%)
    all_to_all x2, blocking collectives, swap(): return lax.all_to_all(operand, axes, 0, 0, tiled=True)  37.5 us
    ppermute x2, starting transfers between devices, local(): refs = [lax.ppermute(low, ALL, route) for route in routes(True)]  13.3 us
    all_to_all x2, starting transfers between devices, swap(): return lax.all_to_all(operand, axes, 0, 0, tiled=True)  13.1 us
    all_to_all x2, waiting for transfers between devices, swap(): return lax.all_to_all(operand, axes, 0, 0, tiled=True)  11.2 us
    ppermute x2, starting transfers between devices, local(): lax.ppermute(part, ALL, route)  9.86 us
    ppermute x2, waiting for transfers between devices, local(): lax.ppermute(part, ALL, route)  9.78 us
    pallas_call x9, Pallas kernels, call(): pl.pallas_call(kernel, out_shape=out, in_specs=in_vmem + in_smem, out_spe...  7.27 us
    ppermute x1, starting transfers between devices, local(): other = lax.ppermute(other, 'c', SWAP)  5.01 us
  transfers between devices with their start and end apart: 7, of which 5 were waited for; matrix products, arithmetic and copies ran while one was open for 1% of the time, Pallas kernels for 1%

profile of v11, /device:TPU:25, one launch (start us, length us, event | category | flops | bytes accessed | tf_op | source)
XLA Modules:
  0.0 113.9 jit_solution(16122423580132452586)
XLA Ops:
  0.6 2.2 %shard_map.77 = bf16[16,2,16,1152]{3,2,1,0:T(8,128)(2,1)} custom-call(f32[2,16,1024]{2,1,0:T(8,128)} %img_ref.1, f32[1,16]{1,0:T(1,128)} %bitcast.23), custom_call_target="tpu_custom_call" | custom-call | tf_op jit(solution)/shard_map/pallas_call | solution.py:247
  2.8 0.0 copy-start
  2.8 0.0 copy-start.1
  2.9 6.8 %all-to-all-start = ((bf16[16,2,16,1152]{3,2,1,0:T(8,128)(2,1)}), bf16[16,2,16,1152]{3,2,1,0:T(8,128)(2,1)S(1)}, u32[]{:S(2)}, u32[]{:S(2)}) async-start(bf16[16,2,16,1152]{3,2,1,0:T(8,128)(2,1)} %shard_map.77), calls=%async_computation | async-start | bytes 2359296 | tf_op jit(solution)/shard_map/all_to_all | solution.py:258
  9.6 0.0 copy-done
  9.6 0.0 copy-done.1
  9.6 0.1 shard_map.78
  9.7 11.3 %collective-permute-start.1 = (bf16[2,8,2176]{2,1,0:T(8,128)(2,1)S(1)}, bf16[2,8,2176]{2,1,0:T(8,128)(2,1)S(1)}, u32[]{:S(2)}, u32[]{:S(2)}) collective-permute-start(bf16[2,8,2176]{2,1,0:T(8,128)(2,1)S(1)} %shard_map.78), channel_id=1, source_target_pairs={{0,0},{1,1},{2,2},{3,3},{64,4},{65,5},{66,6},{67,7},{128,8},{129,9... | collective-permute-start | bytes 208904 | tf_op jit(solution)/shard_map/ppermute | solution.py:278
  21.0 2.0 %collective-permute-start.2 = (bf16[2,8,2176]{2,1,0:T(8,128)(2,1)S(1)}, bf16[2,8,2176]{2,1,0:T(8,128)(2,1)S(1)}, u32[]{:S(2)}, u32[]{:S(2)}) collective-permute-start(bf16[2,8,2176]{2,1,0:T(8,128)(2,1)S(1)} %shard_map.78), channel_id=1, source_target_pairs={{4,0},{5,1},{6,2},{7,3},{68,4},{69,5},{70,6},{71,7},{132,8},{133,9... | collective-permute-start | bytes 208904 | tf_op jit(solution)/shard_map/ppermute | solution.py:278
  23.0 1.2 %all-to-all-done = bf16[16,2,16,1152]{3,2,1,0:T(8,128)(2,1)S(1)} async-done(((bf16[16,2,16,1152]{3,2,1,0:T(8,128)(2,1)}), bf16[16,2,16,1152]{3,2,1,0:T(8,128)(2,1)S(1)}, u32[]{:S(2)}, u32[]{:S(2)}) %all-to-all-start) | async-done | bytes 1179680 | tf_op jit(solution)/shard_map/all_to_all | solution.py:258
  24.2 0.0 copy-start.3
  24.2 0.1 dynamic-slice_bitcast_fusion
  24.3 5.0 %collective-permute-start = (bf16[4,2,2,16,1152]{4,3,2,1,0:T(8,128)(2,1)S(1)}, bf16[4,2,2,16,1152]{4,3,2,1,0:T(8,128)(2,1)S(1)}, u32[]{:S(2)}, u32[]{:S(2)}) collective-permute-start(bf16[4,2,2,16,1152]{4,3,2,1,0:T(8,128)(2,1)S(1)} %get-tuple-element.18), channel_id=1, source_target_pairs={{0,32},{32,0},{1,33},{33,1},{2,34},{34,2},{3,35},{35,3},{4,36},{36... | collective-permute-start | bytes 1769480 | tf_op jit(solution)/shard_map/ppermute | solution.py:275
  29.3 0.0 copy-done.3
  29.4 0.6 fusion
  29.9 0.0 collective-permute-done.1.ref_ref
  29.9 0.4 shard_map.79
  30.3 4.5 %collective-permute-done.2.ref_ref = bf16[2,8,2176]{2,1,0:T(8,128)(2,1)S(1)} collective-permute-done((bf16[2,8,2176]{2,1,0:T(8,128)(2,1)S(1)}, bf16[2,8,2176]{2,1,0:T(8,128)(2,1)S(1)}, u32[]{:S(2)}, u32[]{:S(2)}) %collective-permute-start.2) | collective-permute-done | bytes 69664 | tf_op jit(solution)/shard_map/ppermute | solution.py:278
  34.8 0.4 shard_map.80
  35.2 0.0 collective-permute-done.other_ref
  35.2 0.0 copy-start.2
  35.2 0.9 shard_map.81
  36.1 26.9 %all_to_all.20.got_ref = f32[16,8,256]{2,1,0:T(8,128)S(1)} all-to-all(f32[16,8,256]{2,1,0:T(8,128)S(1)} %shard_map.81), channel_id=1, replica_groups=mesh['y'=4,'zh'=2,'c'=2,'zl'=8,'xh'=2,'xl'=2] {'zl','c'}, dimensions={0} | all-to-all | bytes 262144 | tf_op jit(solution)/shard_map/all_to_all | solution.py:258
  63.0 0.0 copy-done.2
  63.0 0.7 shard_map.82
  63.7 10.6 %all_to_all.21.got_ref = f32[16,8,128]{2,1,0:T(8,128)S(1)} all-to-all(f32[16,8,128]{2,1,0:T(8,128)S(1)} %get-tuple-element.14), channel_id=1, replica_groups=mesh['y'=4,'zh'=2,'c'=2,'zl'=8,'xh'=2,'xl'=2] {'y','xh','xl'}, dimensions={0} | all-to-all | bytes 131072 | tf_op jit(solution)/shard_map/all_to_all | solution.py:258
  74.3 0.9 shard_map.83
  75.3 6.4 %all-to-all-start.3 = ((bf16[16,8,256]{2,1,0:T(8,128)(2,1)}), bf16[16,8,256]{2,1,0:T(8,128)(2,1)S(1)}, u32[]{:S(2)}, u32[]{:S(2)}) async-start(bf16[16,8,256]{2,1,0:T(8,128)(2,1)} %shard_map.83), calls=%async_computation.3 | async-start | bytes 131072 | tf_op jit(solution)/shard_map/all_to_all | solution.py:258
  81.6 10.1 %all-to-all-done.3.got_ref = bf16[16,8,256]{2,1,0:T(8,128)(2,1)S(1)} async-done(((bf16[16,8,256]{2,1,0:T(8,128)(2,1)}), bf16[16,8,256]{2,1,0:T(8,128)(2,1)S(1)}, u32[]{:S(2)}, u32[]{:S(2)}) %all-to-all-start.3) | async-done | bytes 65568 | tf_op jit(solution)/shard_map/all_to_all | solution.py:258
  91.7 1.0 shard_map.84
  92.7 4.5 %collective-permute-start.3 = (bf16[2,8,2176]{2,1,0:T(8,128)(2,1)S(1)}, bf16[2,8,2176]{2,1,0:T(8,128)(2,1)S(1)}, u32[]{:S(2)}, u32[]{:S(2)}) collective-permute-start(bf16[2,8,2176]{2,1,0:T(8,128)(2,1)S(1)} %get-tuple-element.16), channel_id=1, source_target_pairs={{0,0},{1,1},{2,2},{3,3},{4,64},{5,65},{6,66},{7,67},{8,128},{9,129... | collective-permute-start | bytes 208904 | tf_op jit(solution)/shard_map/ppermute | solution.py:311
  97.2 5.3 %collective-permute-start.4 = (bf16[2,8,2176]{2,1,0:T(8,128)(2,1)S(1)}, bf16[2,8,2176]{2,1,0:T(8,128)(2,1)S(1)}, u32[]{:S(2)}, u32[]{:S(2)}) collective-permute-start(bf16[2,8,2176]{2,1,0:T(8,128)(2,1)S(1)} %get-tuple-element.17), channel_id=1, source_target_pairs={{0,4},{1,5},{2,6},{3,7},{4,68},{5,69},{6,70},{7,71},{8,132},{9,133... | collective-permute-start | bytes 208904 | tf_op jit(solution)/shard_map/ppermute | solution.py:311
  102.6 0.1 slice_convert_fusion
  102.7 0.1 copy.14
  102.8 0.6 reduce_sum.9
  103.4 2.4 %collective-permute-done.3.first_ref = bf16[2,8,2176]{2,1,0:T(8,128)(2,1)S(1)} collective-permute-done((bf16[2,8,2176]{2,1,0:T(8,128)(2,1)S(1)}, bf16[2,8,2176]{2,1,0:T(8,128)(2,1)S(1)}, u32[]{:S(2)}, u32[]{:S(2)}) %collective-permute-start.3) | collective-permute-done | bytes 69664 | tf_op jit(solution)/shard_map/ppermute | solution.py:311
  105.8 7.4 %collective-permute-done.4.second_ref = bf16[2,8,2176]{2,1,0:T(8,128)(2,1)S(1)} collective-permute-done((bf16[2,8,2176]{2,1,0:T(8,128)(2,1)S(1)}, bf16[2,8,2176]{2,1,0:T(8,128)(2,1)S(1)}, u32[]{:S(2)}, u32[]{:S(2)}) %collective-permute-start.4) | collective-permute-done | bytes 69664 | tf_op jit(solution)/shard_map/ppermute | solution.py:311
  113.1 0.8 shard_map.85
  (4 shorter events, 0.0 us)
Async XLA Ops:
  2.8 6.8 %copy-start = (f32[2,8,2048]{2,1,0:T(8,128)S(1)}, f32[2,8,2048]{2,1,0:T(8,128)}, u32[]{:S(2)}) copy-start(f32[2,8,2048]{2,1,0:T(8,128)} %ref_ref.1) | copy-start | bytes 393220
  2.8 6.8 %copy-start.1 = (s32[8]{0:T(128)S(1)}, s32[8]{0:T(128)}, u32[]{:S(2)}) copy-start(s32[8]{0:T(128)} %param.10) | copy-start | bytes 100
  2.9 21.3 %all-to-all-start = ((bf16[16,2,16,1152]{3,2,1,0:T(8,128)(2,1)}), bf16[16,2,16,1152]{3,2,1,0:T(8,128)(2,1)S(1)}, u32[]{:S(2)}, u32[]{:S(2)}) async-start(bf16[16,2,16,1152]{3,2,1,0:T(8,128)(2,1)} %shard_map.77), calls=%async_computation | async-start | bytes 2359296 | tf_op jit(solution)/shard_map/all_to_all | solution.py:258
  9.7 20.2 %collective-permute-start.1 = (bf16[2,8,2176]{2,1,0:T(8,128)(2,1)S(1)}, bf16[2,8,2176]{2,1,0:T(8,128)(2,1)S(1)}, u32[]{:S(2)}, u32[]{:S(2)}) collective-permute-start(bf16[2,8,2176]{2,1,0:T(8,128)(2,1)S(1)} %shard_map.78), channel_id=1, source_target_pairs={{0,0},{1,1},{2,2},{3,3},{64,4},{65,5},{66,6},{67,7},{128,8},{129,9... | collective-permute-start | bytes 208904 | tf_op jit(solution)/shard_map/ppermute | solution.py:278
  21.0 13.8 %collective-permute-start.2 = (bf16[2,8,2176]{2,1,0:T(8,128)(2,1)S(1)}, bf16[2,8,2176]{2,1,0:T(8,128)(2,1)S(1)}, u32[]{:S(2)}, u32[]{:S(2)}) collective-permute-start(bf16[2,8,2176]{2,1,0:T(8,128)(2,1)S(1)} %shard_map.78), channel_id=1, source_target_pairs={{4,0},{5,1},{6,2},{7,3},{68,4},{69,5},{70,6},{71,7},{132,8},{133,9... | collective-permute-start | bytes 208904 | tf_op jit(solution)/shard_map/ppermute | solution.py:278
  24.2 5.1 %copy-start.3 = (s32[12,2]{0,1:T(2,128)S(1)}, s32[12,2]{0,1:T(2,128)}, u32[]{:S(2)}) copy-start(s32[12,2]{0,1:T(2,128)} %param.9) | copy-start | bytes 292
  24.3 10.9 %collective-permute-start = (bf16[4,2,2,16,1152]{4,3,2,1,0:T(8,128)(2,1)S(1)}, bf16[4,2,2,16,1152]{4,3,2,1,0:T(8,128)(2,1)S(1)}, u32[]{:S(2)}, u32[]{:S(2)}) collective-permute-start(bf16[4,2,2,16,1152]{4,3,2,1,0:T(8,128)(2,1)S(1)} %get-tuple-element.18), channel_id=1, source_target_pairs={{0,32},{32,0},{1,33},{33,1},{2,34},{34,2},{3,35},{35,3},{4,36},{36... | collective-permute-start | bytes 1769480 | tf_op jit(solution)/shard_map/ppermute | solution.py:275
  35.2 27.8 %copy-start.2 = (f32[4]{0:T(128)S(1)}, f32[4]{0:T(128)}, u32[]{:S(2)}) copy-start(f32[4]{0:T(128)} %prior_ref.1) | copy-start | bytes 52
  75.3 16.4 %all-to-all-start.3 = ((bf16[16,8,256]{2,1,0:T(8,128)(2,1)}), bf16[16,8,256]{2,1,0:T(8,128)(2,1)S(1)}, u32[]{:S(2)}, u32[]{:S(2)}) async-start(bf16[16,8,256]{2,1,0:T(8,128)(2,1)} %shard_map.83), calls=%async_computation.3 | async-start | bytes 131072 | tf_op jit(solution)/shard_map/all_to_all | solution.py:258
  92.7 13.1 %collective-permute-start.3 = (bf16[2,8,2176]{2,1,0:T(8,128)(2,1)S(1)}, bf16[2,8,2176]{2,1,0:T(8,128)(2,1)S(1)}, u32[]{:S(2)}, u32[]{:S(2)}) collective-permute-start(bf16[2,8,2176]{2,1,0:T(8,128)(2,1)S(1)} %get-tuple-element.16), channel_id=1, source_target_pairs={{0,0},{1,1},{2,2},{3,3},{4,64},{5,65},{6,66},{7,67},{8,128},{9,129... | collective-permute-start | bytes 208904 | tf_op jit(solution)/shard_map/ppermute | solution.py:311
  97.2 15.9 %collective-permute-start.4 = (bf16[2,8,2176]{2,1,0:T(8,128)(2,1)S(1)}, bf16[2,8,2176]{2,1,0:T(8,128)(2,1)S(1)}, u32[]{:S(2)}, u32[]{:S(2)}) collective-permute-start(bf16[2,8,2176]{2,1,0:T(8,128)(2,1)S(1)} %get-tuple-element.17), channel_id=1, source_target_pairs={{0,4},{1,5},{2,6},{3,7},{4,68},{5,69},{6,70},{7,71},{8,132},{9,133... | collective-permute-start | bytes 208904 | tf_op jit(solution)/shard_map/ppermute | solution.py:311
